TPU v7x, 32 devices: a whole 2x2x4 slice. The times are simulated.
32 devices in a mesh: wide: 16 (over z, x, core), tensor: 2 (over y).
Axes of the slice: x: 2, y: 2, z: 4, core: 2. Of those that a mesh axis runs over, the one named last changes fastest.
Arguments:
- tokens: bfloat16 [50432, 384], P(('wide', 'tensor')), may hold values from -6 to 6
- ln1_gain: float32 [384], P('wide'), may hold values from 0.1 to 1.9
- qkv_weight: bfloat16 [384, 3, 384], P('wide', None, 'tensor'), may hold values from -0.3125 to 0.3125
- out_weight: bfloat16 [384, 384], P('tensor', 'wide'), may hold values from -0.875 to 0.875
- ln2_gain: float32 [384], P('wide'), may hold values from 0.1 to 1.9
- fc1_weight: bfloat16 [384, 1536], P('wide', 'tensor'), may hold values from -0.3125 to 0.3125
- fc2_weight: bfloat16 [1536, 384], P('tensor', 'wide'), may hold values from -0.15625 to 0.15625
- out_grad: bfloat16 [50432, 384], P(('wide', 'tensor')), may hold values from -6 to 6
Outputs:
- layer_out: bfloat16 [50432, 384], P(('wide', 'tensor'))
- input_token_gradient: float32 [50432, 384], P(('wide', 'tensor'))
- ln1_gain_grad: float32 [384], P('wide')
- qkv_weight_grad: float32 [384, 3, 384], P('wide', None, 'tensor')
- out_weight_grad: float32 [384, 384], P('tensor', 'wide')
- ln2_gain_grad: float32 [384], P('wide')
- fc1_weight_grad: float32 [384, 1536], P('wide', 'tensor')
- fc2_weight_grad: float32 [1536, 384], P('tensor', 'wide')
All inputs are finite; a program needn't handle non-finite values.
Results may differ from a plain program's by a relative error of at most 0.035.
Values may be sent and summed in bfloat16 or wider, within the bound.
No kernel may reach another device: no remote copies, remote signals or barrier semaphores. Data moves between devices by JAX's collectives and lax.ppermute only.
A program may use at most 128 MiB of HBM per device.

v0:
```python
import jax
import jax.numpy as jnp
from jax import lax
from jax.sharding import PartitionSpec as P

HD = 64
SEQ = 197


def apply_layer_norm(values):
    center = values - jnp.mean(values, axis=-1, keepdims=True)
    spread = jnp.mean(center * center, axis=-1, keepdims=True)
    inverse_deviation = lax.rsqrt(spread + 1e-06)
    return (center * inverse_deviation, inverse_deviation)


def norm_backward_pass(incoming_gradient, centered_normalized, inverse_deviation, complete_gain):
    gain_scaled = incoming_gradient * complete_gain
    return inverse_deviation * (
        gain_scaled
        - jnp.mean(gain_scaled, axis=-1, keepdims=True)
        - centered_normalized * jnp.mean(gain_scaled * centered_normalized, axis=-1, keepdims=True)
    )


def local(tokens, ln1_gain, qkv_weight, out_weight, ln2_gain, fc1_weight, fc2_weight, out_grad):
    dev_rows = tokens.shape[0]
    score_scale = HD ** (-0.5)
    first_norm_gain, qkv_full, out_full, second_norm_gain, fc1_full, fc2_full = (
        lax.all_gather(ln1_gain.astype(jnp.bfloat16), "wide", axis=0, tiled=True).astype(
            ln1_gain.dtype
        ),
        lax.all_gather(qkv_weight, "wide", axis=0, tiled=True),
        lax.all_gather(out_weight, "wide", axis=1, tiled=True),
        lax.all_gather(ln2_gain.astype(jnp.bfloat16), "wide", axis=0, tiled=True).astype(
            ln2_gain.dtype
        ),
        lax.all_gather(fc1_weight, "wide", axis=0, tiled=True),
        lax.all_gather(fc2_weight, "wide", axis=1, tiled=True),
    )
    qkv_full, out_full, fc1_full, fc2_full = (
        lax.all_gather(qkv_full, "tensor", axis=2, tiled=True),
        lax.all_gather(out_full, "tensor", axis=0, tiled=True),
        lax.all_gather(fc1_full, "tensor", axis=1, tiled=True),
        lax.all_gather(fc2_full, "tensor", axis=0, tiled=True),
    )
    images = dev_rows // SEQ
    local_width = qkv_full.shape[2]
    local_heads = local_width // HD
    input_tokens = tokens.astype(jnp.float32)
    first_centered_normalized, first_inverse_deviation = apply_layer_norm(input_tokens)
    first_normed_tokens = (first_centered_normalized * first_norm_gain).astype(jnp.bfloat16)
    projected = jnp.einsum(
        "rd,dcf->rcf", first_normed_tokens, qkv_full, preferred_element_type=jnp.float32
    ).astype(jnp.bfloat16)
    queries = projected[:, 0, :].reshape(images, SEQ, local_heads, HD)
    key_rows = projected[:, 1, :].reshape(images, SEQ, local_heads, HD)
    value_rows = projected[:, 2, :].reshape(images, SEQ, local_heads, HD)
    scores = (
        jnp.einsum("ishd,ithd->ihst", queries, key_rows, preferred_element_type=jnp.float32)
        * score_scale
    )
    row_top = jnp.max(scores, axis=-1, keepdims=True)
    expon = jnp.exp(scores - row_top)
    totals = jnp.sum(expon, axis=-1, keepdims=True)
    log_total = row_top + jnp.log(totals)
    probs_low = (expon / totals).astype(jnp.bfloat16)
    heads_out = (
        jnp.einsum("ihst,ithd->ishd", probs_low, value_rows, preferred_element_type=jnp.float32)
        .astype(jnp.bfloat16)
        .reshape(dev_rows, local_width)
    )
    block = heads_out
    attn_part = jnp.dot(block, out_full, preferred_element_type=jnp.float32)
    attention_residual = input_tokens + attn_part
    second_centered_normalized, second_inverse_deviation = apply_layer_norm(attention_residual)
    second_normed_tokens = (second_centered_normalized * second_norm_gain).astype(jnp.bfloat16)
    hidden_pre = jnp.dot(second_normed_tokens, fc1_full, preferred_element_type=jnp.float32)
    hidden = jax.nn.gelu(hidden_pre, approximate=True).astype(jnp.bfloat16)
    block = hidden
    mlp_part = jnp.dot(block, fc2_full, preferred_element_type=jnp.float32)
    layer_out = (attention_residual + mlp_part).astype(jnp.bfloat16)
    fc2_grad = jnp.dot(hidden.T, out_grad, preferred_element_type=jnp.float32)
    hidden_grad = jnp.dot(out_grad, fc2_full.T, preferred_element_type=jnp.float32)
    _, gelu_pull = jax.vjp(lambda pre: jax.nn.gelu(pre, approximate=True), hidden_pre)
    pre_grad = gelu_pull(hidden_grad)[0].astype(jnp.bfloat16)
    fc1_grad = jnp.dot(second_normed_tokens.T, pre_grad, preferred_element_type=jnp.float32)
    block = pre_grad
    second_normed_gradient = jnp.dot(block, fc1_full.T, preferred_element_type=jnp.float32)
    second_gain_piece = jnp.sum(second_normed_gradient * second_centered_normalized, axis=0)
    attention_residual_gradient = out_grad.astype(jnp.float32) + norm_backward_pass(
        second_normed_gradient,
        second_centered_normalized,
        second_inverse_deviation,
        second_norm_gain,
    )
    middle_low = attention_residual_gradient.astype(jnp.bfloat16)
    out_grad_weight = jnp.dot(heads_out.T, middle_low, preferred_element_type=jnp.float32)
    heads_grad = jnp.dot(middle_low, out_full.T, preferred_element_type=jnp.float32).astype(
        jnp.bfloat16
    )
    heads_grad = heads_grad.reshape(images, SEQ, local_heads, HD)
    probs_again = jnp.exp(
        jnp.einsum("ishd,ithd->ihst", queries, key_rows, preferred_element_type=jnp.float32)
        * score_scale
        - log_total
    )
    probs_again_low = probs_again.astype(jnp.bfloat16)
    probs_grad = jnp.einsum(
        "ishd,ithd->ihst", heads_grad, value_rows, preferred_element_type=jnp.float32
    )
    values_grad = jnp.einsum(
        "ihst,ishd->ithd", probs_again_low, heads_grad, preferred_element_type=jnp.float32
    )
    scores_grad = (
        probs_again * (probs_grad - jnp.sum(probs_again * probs_grad, axis=-1, keepdims=True))
    ).astype(jnp.bfloat16)
    queries_grad = (
        jnp.einsum("ihst,ithd->ishd", scores_grad, key_rows, preferred_element_type=jnp.float32)
        * score_scale
    )
    keys_grad = (
        jnp.einsum("ihst,ishd->ithd", scores_grad, queries, preferred_element_type=jnp.float32)
        * score_scale
    )
    qkv_grad = jnp.stack(
        [
            queries_grad.reshape(dev_rows, local_width),
            keys_grad.reshape(dev_rows, local_width),
            values_grad.reshape(dev_rows, local_width),
        ],
        axis=1,
    ).astype(jnp.bfloat16)
    qkv_grad_weight = jnp.einsum(
        "rd,rcf->dcf", first_normed_tokens, qkv_grad, preferred_element_type=jnp.float32
    )
    block = qkv_grad
    first_normed_gradient = jnp.einsum(
        "rcf,dcf->rd", block, qkv_full, preferred_element_type=jnp.float32
    )
    first_gain_piece = jnp.sum(first_normed_gradient * first_centered_normalized, axis=0)
    input_token_gradient = attention_residual_gradient + norm_backward_pass(
        first_normed_gradient, first_centered_normalized, first_inverse_deviation, first_norm_gain
    )
    gain_one_sum, gain_two_sum = lax.psum((first_gain_piece, second_gain_piece), "tensor")
    qkv_grad_weight, out_grad_weight, fc1_grad, fc2_grad = (
        lax.psum_scatter(
            qkv_grad_weight.astype(jnp.bfloat16), "tensor", scatter_dimension=2, tiled=True
        ).astype(jnp.float32),
        lax.psum_scatter(
            out_grad_weight.astype(jnp.bfloat16), "tensor", scatter_dimension=0, tiled=True
        ).astype(jnp.float32),
        lax.psum_scatter(
            fc1_grad.astype(jnp.bfloat16), "tensor", scatter_dimension=1, tiled=True
        ).astype(jnp.float32),
        lax.psum_scatter(
            fc2_grad.astype(jnp.bfloat16), "tensor", scatter_dimension=0, tiled=True
        ).astype(jnp.float32),
    )
    gain_one_shard, qkv_shard, out_shard, gain_two_shard, fc1_shard, fc2_shard = (
        lax.psum_scatter(gain_one_sum, "wide", scatter_dimension=0, tiled=True),
        lax.psum_scatter(qkv_grad_weight, "wide", scatter_dimension=0, tiled=True),
        lax.psum_scatter(out_grad_weight, "wide", scatter_dimension=1, tiled=True),
        lax.psum_scatter(gain_two_sum, "wide", scatter_dimension=0, tiled=True),
        lax.psum_scatter(fc1_grad, "wide", scatter_dimension=0, tiled=True),
        lax.psum_scatter(fc2_grad, "wide", scatter_dimension=1, tiled=True),
    )
    return (
        layer_out,
        input_token_gradient,
        gain_one_shard,
        qkv_shard,
        out_shard,
        gain_two_shard,
        fc1_shard,
        fc2_shard,
    )


def solution(mesh):
    placed = (
        P(("wide", "tensor"), None),
        P("wide"),
        P("wide", None, "tensor"),
        P("tensor", "wide"),
        P("wide"),
        P("wide", "tensor"),
        P("tensor", "wide"),
        P(("wide", "tensor"), None),
    )
    return jax.shard_map(
        local,
        mesh=mesh,
        in_specs=placed,
        out_specs=(
            P(("wide", "tensor"), None),
            P(("wide", "tensor"), None),
            P("wide"),
            P("wide", None, "tensor"),
            P("tensor", "wide"),
            P("wide"),
            P("wide", "tensor"),
            P("tensor", "wide"),
        ),
        check_vma=False,
    )
```

profile of v0, /device:TPU:0, one launch (start us, length us, event | category | flops | bytes accessed | tf_op | source)
XLA Modules:
  0.0 668.8 jit_solution(17851825771241101775)
XLA Ops:
  7.3 26.6 %all_gather.36 = bf16[384,768]{1,0:T(8,128)(2,1)} all-gather(bf16[24,768]{1,0:T(8,128)(2,1)} %param.13), channel_id=1, replica_groups=mesh['wide'=16,'tensor'=2] {'wide'}, dimensions={0}, use_global_device_ids=true | all-gather | bytes 626688 | tf_op jit(solution)/shard_map/all_gather | solution.py:38
  33.9 20.7 %all_gather.38 = bf16[768,384]{0,1:T(8,128)(2,1)} all-gather(bf16[768,24]{0,1:T(8,128)(2,1)} %param.14), channel_id=1, replica_groups=mesh['wide'=16,'tensor'=2] {'wide'}, dimensions={1}, use_global_device_ids=true | all-gather | bytes 626688 | tf_op jit(solution)/shard_map/all_gather | solution.py:39
  56.5 31.3 %all-reduce.7 = (bf16[384]{0:T(512)(128)(2,1)S(1)}, bf16[384]{0:T(512)(128)(2,1)S(1)}) all-reduce(bf16[384]{0:T(512)(128)(2,1)S(1)} %dynamic-update-slice, bf16[384]{0:T(512)(128)(2,1)S(1)} %dynamic-update-slice.1), channel_id=1, replica_groups=mesh['wide'=16,'tensor'=2] {'wide'}, use_global_device_ids=true, to_apply=%add | all-reduce | flops 768 | bytes 3072
  88.8 17.7 %all_gather.33 = bf16[192,384]{0,1:T(8,128)(2,1)S(1)} all-gather(bf16[192,24]{0,1:T(8,128)(2,1)S(1)} %copy-done.18), channel_id=1, replica_groups=mesh['wide'=16,'tensor'=2] {'wide'}, dimensions={1}, use_global_device_ids=true | all-gather | bytes 156672 | tf_op jit(solution)/shard_map/all_gather | solution.py:34
  106.6 6.8 %all_gather.34 = bf16[384,384]{1,0:T(8,128)(2,1)S(1)} all-gather(bf16[192,384]{1,0:T(8,128)(2,1)S(1)} %copy.97), channel_id=1, replica_groups=mesh['wide'=16,'tensor'=2] {'tensor'}, dimensions={0}, use_global_device_ids=true | all-gather | bytes 442368 | tf_op jit(solution)/shard_map/all_gather | solution.py:43
  113.4 20.7 %all_gather.31 = bf16[384,3,192]{2,0,1:T(8,128)(2,1)S(1)} all-gather(bf16[24,3,192]{2,0,1:T(8,128)(2,1)S(1)} %copy-done.17), channel_id=1, replica_groups=mesh['wide'=16,'tensor'=2] {'wide'}, dimensions={0}, use_global_device_ids=true | all-gather | bytes 470016 | tf_op jit(solution)/shard_map/all_gather | solution.py:33
  134.3 13.1 %all_gather.32 = bf16[384,3,384]{0,2,1:T(8,128)(2,1)S(1)} all-gather(bf16[384,3,192]{0,2,1:T(8,128)(2,1)S(1)} %copy.88), channel_id=1, replica_groups=mesh['wide'=16,'tensor'=2] {'tensor'}, dimensions={2}, use_global_device_ids=true | all-gather | bytes 1327104 | tf_op jit(solution)/shard_map/all_gather | solution.py:42
  158.9 5.0 reshape.100
  168.4 4.8 reshape.99
  194.0 6.8 %fusion.45 = f32[1576,1536]{1,0:T(8,128)} fusion(bf16[384,1536]{1,0:T(8,128)(2,1)} %all-gather.3.cloned.1.call-done, f32[1576,384]{1,0:T(8,128)S(1)} %get-tuple-element.60, f32[384]{0:T(512)S(1)} %convert_element_type.91, f32[1576]{0:T(1024)S(1)} %add_rsqrt_fusion, f32[1576]{0:T(1024)S(1)} %broadcast_multiply_fusion.4), kind=kOutput, calls=%fused_computation.81 | convolution fusion | flops 1861545984 | bytes 13297472 | tf_op jit(solution)/shard_map/dot_general | solution.py:78
  200.8 10.6 %fusion.6 = bf16[1576,1536]{1,0:T(8,128)(2,1)S(1)} fusion(f32[1576,1536]{1,0:T(8,128)} %fusion.45, bf16[1576,384]{1,0:T(8,128)(2,1)} %param.15, bf16[1536,384]{0,1:T(8,128)(2,1)} %all-gather.5.cloned.1.call-done), kind=kOutput, calls=%fused_computation.13 | convolution fusion | flops 1907539968 | bytes 16914432 | tf_op jit(solution)/shard_map/dot_general | solution.py:84
  219.8 4.8 reshape.102
  229.1 7.5 %fusion.32 = bf16[8,197,6,64]{1,3,2,0:T(8,128)(2,1)} fusion(bf16[8,197,6,64]{1,3,2,0:T(8,128)(2,1)} %copy.99, f32[8,6,197,197]{2,3,1,0:T(8,128)} %copy-done, f32[8,6,197]{2,1,0:T(8,128)S(1)} %log_add_fusion), kind=kOutput, calls=%fused_computation.57 | convolution fusion | flops 244636176 | bytes 9909888 | tf_op jit(solution)/shard_map/ihst,ishd->ithd/dot_general | solution.py:112
  236.6 7.7 %multiply_reduce_fusion = (f32[8,6,197]{2,1,0:T(8,128)S(1)}, f32[8,6,197,197]{2,3,1,0:T(8,128)}) fusion(f32[8,6,197,197]{2,3,1,0:T(8,128)} %copy-done, f32[8,6,197]{2,1,0:T(8,128)S(1)} %log_add_fusion, bf16[8,197,6,64]{1,3,2,0:T(8,128)(2,1)S(1)} %copy-done.7, bf16[8,197,6,64]{1,3,2,0:T(8,128)(2,1)S(1)} %copy-done.9), kind=kOutput, calls=%fused_computation.3 | convolution fusion | flops 245884368 | bytes 17399040 | tf_op jit(solution)/shard_map/ishd,ithd->ihst/dot_general | solution.py:109
  244.3 12.1 %multiply_convert_fusion = bf16[8,6,197,197]{2,3,1,0:T(8,128)(2,1)} fusion(f32[8,6,197,197]{2,3,1,0:T(8,128)} %get-tuple-element.63, f32[8,6,197,197]{2,3,1,0:T(8,128)} %copy-done, f32[8,6,197]{2,1,0:T(8,128)S(1)} %get-tuple-element.62, f32[8,6,197]{2,1,0:T(8,128)S(1)} %log_add_fusion), kind=kLoop, calls=%fused_computation.2 | loop fusion | flops 9314160 | bytes 18703968 | tf_op jit(solution)/shard_map/convert_element_type | solution.py:117
  256.4 5.8 fusion.37
  264.5 4.8 copy.123
  269.2 5.2 reshape.91
  279.2 5.2 reshape.89
  289.1 5.2 reshape.90
  305.9 8.9 %convolution_convert_fusion.1 = bf16[1536,384]{1,0:T(8,128)(2,1)} fusion(bf16[1576,384]{1,0:T(8,128)(2,1)} %param.15, f32[1576,1536]{1,0:T(8,128)} %fusion.45), kind=kOutput, calls=%fused_computation.37 | convolution fusion | flops 1881501696 | bytes 12072960 | tf_op jit(solution)/shard_map/dot_general | solution.py:83
  314.9 5.9 convolution_convert_fusion.2
  323.3 8.9 %reduce-scatter.14.cloned.1.call-done = bf16[192,384]{1,0:T(8,128)(2,1)} async-done(((bf16[384,384]{1,0:T(8,128)(2,1)}), bf16[192,384]{1,0:T(8,128)(2,1)}) %reduce-scatter.14.cloned.1.call-update) | async-done | bytes 147472 | tf_op jit(solution)/shard_map/reduce_scatter | solution.py:150
  334.1 22.1 %reduce-scatter.20.cloned.1.call-done = bf16[768,384]{1,0:T(8,128)(2,1)} async-done(((bf16[1536,384]{1,0:T(8,128)(2,1)}), bf16[768,384]{1,0:T(8,128)(2,1)}) %reduce-scatter.20.cloned.1.call-update) | async-done | bytes 589840 | tf_op jit(solution)/shard_map/reduce_scatter | solution.py:156
  359.2 6.4 fusion.26
  365.6 33.0 %all-reduce.5 = (f32[384]{0:T(512)S(1)}, f32[384]{0:T(512)S(1)}) all-reduce(f32[384]{0:T(512)S(1)} %get-tuple-element.42, f32[384]{0:T(512)S(1)} %get-tuple-element.40), channel_id=2, replica_groups=mesh['wide'=16,'tensor'=2] {'wide'}, use_global_device_ids=true, to_apply=%region_13.0.clone | all-reduce | flops 768 | bytes 6144
  398.7 5.4 all-reduce.6
  411.0 6.8 %fusion.20 = bf16[1576,384]{1,0:T(8,128)(2,1)} fusion(f32[1576,384]{1,0:T(8,128)S(1)} %get-tuple-element.60, bf16[1536,384]{0,1:T(8,128)(2,1)S(1)} %copy-done.20, f32[1576,1536]{1,0:T(8,128)} %fusion.45), kind=kOutput, calls=%fused_computation.36 | convolution fusion | flops 1882122240 | bytes 14493696 | tf_op jit(solution)/shard_map/dot_general | solution.py:81
  417.8 62.2 %all-reduce.10.cloned.1.call-done = f32[384,3,192]{2,1,0:T(4,128)} async-done(((f32[384,3,192]{2,1,0:T(4,128)}), f32[384,3,192]{2,1,0:T(4,128)}) %all-reduce.10.cloned.1.call-update) | async-done | bytes 884752
  481.5 57.4 %reduce-scatter.22.cloned.1.call-done = f32[24,192]{1,0:T(8,128)} async-done(((f32[384,192]{1,0:T(8,128)}), f32[24,192]{1,0:T(8,128)}) %reduce-scatter.22.cloned.1.call-update) | async-done | bytes 18448
  538.9 61.4 %reduce-scatter.24.cloned.1.call-done = f32[24,768]{1,0:T(8,128)} async-done(((f32[384,768]{1,0:T(8,128)}), f32[24,768]{1,0:T(8,128)}) %reduce-scatter.24.cloned.1.call-update) | async-done | bytes 73744
  600.3 61.3 %reduce-scatter.18.cloned.1.call-done = f32[24,768]{1,0:T(8,128)} async-done(((f32[384,768]{1,0:T(8,128)}), f32[24,768]{1,0:T(8,128)}) %reduce-scatter.18.cloned.1.call-update) | async-done | bytes 73744 | tf_op jit(solution)/shard_map/reduce_scatter | solution.py:165
  (127 shorter events, 90.8 us)
Async XLA Ops:
  7.2 47.6 %copy-start.19 = (u32[32]{0:T(128)S(1)}, u32[32]{0:T(128)}, u32[]{:S(2)}) copy-start(u32[32]{0:T(128)} %constant.41) | copy-start | bytes 388
  7.2 47.5 %copy-start.21 = (f32[24]{0:T(128)S(1)}, f32[24]{0:T(128)}, u32[]{:S(2)}) copy-start(f32[24]{0:T(128)} %param.9) | copy-start | bytes 292
  7.2 47.5 %copy-start.22 = (f32[24]{0:T(128)S(1)}, f32[24]{0:T(128)}, u32[]{:S(2)}) copy-start(f32[24]{0:T(128)} %param.12) | copy-start | bytes 292
  7.2 80.6 %copy-start.5 = (bf16[1576,384]{1,0:T(8,128)(2,1)S(1)}, bf16[1576,384]{1,0:T(8,128)(2,1)}, u32[]{:S(2)}) copy-start(bf16[1576,384]{1,0:T(8,128)(2,1)} %param.8) | copy-start | bytes 3631108
  7.2 81.6 %copy-start.18 = (bf16[192,24]{0,1:T(8,128)(2,1)S(1)}, bf16[192,24]{0,1:T(8,128)(2,1)}, u32[]{:S(2)}) copy-start(bf16[192,24]{0,1:T(8,128)(2,1)} %param.11) | copy-start | bytes 27652
  7.2 186.8 %all-gather.3.cloned.1.call-start = ((), (), s32[]{:S(2)}) async-start(), calls=%async_computation.7 | async-start | bytes 1769472 | tf_op jit(solution)/shard_map/all_gather | solution.py:44
  33.8 79.5 %copy-start.17 = (bf16[24,3,192]{2,0,1:T(8,128)(2,1)S(1)}, bf16[24,3,192]{2,0,1:T(8,128)(2,1)}, u32[]{:S(2)}) copy-start(bf16[24,3,192]{2,0,1:T(8,128)(2,1)} %param.10) | copy-start | bytes 82948
  33.9 166.9 %all-gather.5.cloned.1.call-start = ((), (), s32[]{:S(2)}) async-start(), calls=%async_computation.8 | async-start | bytes 1769472 | tf_op jit(solution)/shard_map/all_gather | solution.py:45
  54.6 266.3 %reduce-scatter.12.cloned.1.call-start = ((), (), s32[]{:S(2)}) async-start(), calls=%async_computation.9 | async-start | bytes 1327104 | tf_op jit(solution)/shard_map/reduce_scatter | solution.py:147
  147.4 2.4 copy-start.14
  158.9 18.9 %copy-start.3 = (bf16[8,197,6,64]{1,3,2,0:T(8,128)(2,1)}, bf16[8,197,6,64]{1,3,2,0:T(8,128)(2,1)S(1)}, u32[]{:S(2)}) copy-start(bf16[8,197,6,64]{1,3,2,0:T(8,128)(2,1)S(1)} %copy.93) | copy-start | bytes 3631108
  180.7 3.8 copy-start
  180.7 3.8 copy-start.8
  200.8 10.6 %copy-start.13 = (bf16[384,1536]{1,0:T(8,128)(2,1)S(1)}, bf16[384,1536]{1,0:T(8,128)(2,1)}, u32[]{:S(2)}) copy-start(bf16[384,1536]{1,0:T(8,128)(2,1)} %all-gather.3.cloned.1.call-done) | copy-start | bytes 3538948
  211.4 3.4 copy-start.23
  211.4 3.4 copy-start.12
  229.1 7.5 %copy-start.7 = (bf16[8,197,6,64]{1,3,2,0:T(8,128)(2,1)S(1)}, bf16[8,197,6,64]{1,3,2,0:T(8,128)(2,1)}, u32[]{:S(2)}) copy-start(bf16[8,197,6,64]{1,3,2,0:T(8,128)(2,1)} %copy.99) | copy-start | bytes 3631108
  229.1 7.5 %copy-start.9 = (bf16[8,197,6,64]{1,3,2,0:T(8,128)(2,1)S(1)}, bf16[8,197,6,64]{1,3,2,0:T(8,128)(2,1)}, u32[]{:S(2)}) copy-start(bf16[8,197,6,64]{1,3,2,0:T(8,128)(2,1)} %copy.94) | copy-start | bytes 3631108
  256.4 5.9 copy-start.1
  256.4 5.9 copy-start.4
  294.3 2.0 copy-start.10
  295.9 2.4 copy-start.6
  296.5 1.8 copy-start.16
  301.9 30.3 %reduce-scatter.14.cloned.1.call-start = ((), (), s32[]{:S(2)}) async-start(), calls=%async_computation.10 | async-start | bytes 442368 | tf_op jit(solution)/shard_map/reduce_scatter | solution.py:150
  305.6 50.5 %reduce-scatter.20.cloned.1.call-start = ((), (), s32[]{:S(2)}) async-start(), calls=%async_computation.13 | async-start | bytes 1769472 | tf_op jit(solution)/shard_map/reduce_scatter | solution.py:156
  314.8 89.3 %reduce-scatter.16.cloned.1.call-start = ((), (), s32[]{:S(2)}) async-start(), calls=%async_computation.11 | async-start | bytes 1769472 | tf_op jit(solution)/shard_map/reduce_scatter | solution.py:153
  320.8 159.1 %all-reduce.10.cloned.1.call-start = ((), (), s32[]{:S(2)}) async-start(), calls=%async_computation.16 | async-start | bytes 3145728
  323.2 36.0 %copy-start.15 = (bf16[384,3,384]{0,2,1:T(8,128)(2,1)S(1)}, bf16[384,3,384]{0,2,1:T(8,128)(2,1)}, u32[]{:S(2)}) copy-start(bf16[384,3,384]{0,2,1:T(8,128)(2,1)} %copy-done.14) | copy-start | bytes 2654212
  323.2 215.7 %reduce-scatter.22.cloned.1.call-start = ((), (), s32[]{:S(2)}) async-start(), calls=%async_computation.14 | async-start | bytes 417792
  334.0 266.3 %reduce-scatter.24.cloned.1.call-start = ((), (), s32[]{:S(2)}) async-start(), calls=%async_computation.15 | async-start | bytes 1253376
  358.5 303.0 %reduce-scatter.18.cloned.1.call-start = ((), (), s32[]{:S(2)}) async-start(), calls=%async_computation.12 | async-start | bytes 1253376 | tf_op jit(solution)/shard_map/reduce_scatter | solution.py:165
  406.4 4.5 copy-start.20
  (2 other events, 3.1 us)
Sparse Core Ops, SparseCore 0:
  34.0 20.0 all-gather.2
  55.6 22.7 all-gather.4
  302.0 15.8 reduce-scatter.11
  320.0 12.1 reduce-scatter.13
  334.3 21.8 reduce-scatter.19
  358.8 21.8 reduce-scatter.15
  384.2 95.7 all-reduce.9
  484.0 54.8 reduce-scatter.21
  543.1 57.1 reduce-scatter.23
  604.3 57.1 reduce-scatter.17
where the time goes:
time: 676 us; the launch traced here: 669 us
  waiting for transfers between devices  273 us (40%)
  blocking collectives  175 us (26%)
  matrix products  91.8 us (14%)
  local copies, waits for them, and re-layouts  87.6 us (13%)
  other arithmetic  23.9 us (4%)
  between operations  16.3 us (2%)
    unnamed x13, waiting for transfers between devices  181 us
    unnamed x2, blocking collectives  64.2 us
    reduce_scatter x1, waiting for transfers between devices, local(): lax.psum_scatter(fc1_grad, 'wide', scatter_dimension=0, tiled=True)  61.3 us
    another operation x7, local copies, waits for them, and re-layouts, local(): jnp.stack([queries_grad.reshape(dev_rows, local_width), keys_grad.reshape...  30.1 us
    all_gather x1, blocking collectives, local(): lax.all_gather(fc1_weight, 'wide', axis=0, tiled=True)  26.6 us
    reduce_scatter x1, waiting for transfers between devices, local(): lax.psum_scatter(fc2_grad.astype(jnp.bfloat16), 'tensor', scatter_dimensi...  22.1 us
    all_gather x1, blocking collectives, local(): lax.all_gather(qkv_weight, 'wide', axis=0, tiled=True)  20.7 us
    all_gather x1, blocking collectives, local(): lax.all_gather(fc2_weight, 'wide', axis=1, tiled=True)  20.7 us
  transfers between devices with their start and end apart: 10, of which 6 were waited for; matrix products, arithmetic and copies ran while one was open for 15% of the time, Pallas kernels for 0%

commit v1 on v0

v1 whole, which is shorter than its diff:
```python
import functools

import jax
import jax.numpy as jnp
from jax import lax
from jax.experimental import pallas as pl
from jax.experimental.pallas import tpu as pltpu
from jax.sharding import PartitionSpec as P

HD = 64
SEQ = 197
PAD = 208
D = 384
QC = 640
F32 = jnp.float32
BF16 = jnp.bfloat16
NT = (((1,), (1,)), ((), ()))
TN = (((0,), (0,)), ((), ()))
GELU_C = 0.7978845608028654
VMEM_LIMIT = 60 * 1024 * 1024


def dot(a, b, dims=(((1,), (0,)), ((), ()))):
    return lax.dot_general(a, b, dims, preferred_element_type=F32)


def stage_bits(wide):
    bits = [("wide", 1 << k) for k in range(1, wide.bit_length() - 1)]
    bits = bits[1:] + bits[:1]
    return bits + [("tensor", 1), ("wide", 1)]


def relative(stages):
    places = [(0, 0)]
    for axis, bit in stages:
        places = places + [(w ^ bit, t) if axis == "wide" else (w, t ^ bit) for w, t in places]
    return places


def swap(value, stage, sizes):
    axis, bit = stage
    return lax.ppermute(value, axis, [(i, i ^ bit) for i in range(sizes[axis])])


def gather(block, stages, sizes):
    held = block[None]
    for stage in stages:
        held = jnp.concatenate([held, swap(held, stage, sizes)], axis=0)
    return held


def scatter_sum(blocks, stages, sizes):
    held = blocks
    for stage in reversed(stages):
        half = held.shape[0] // 2
        got = swap(held[half:], stage, sizes)
        total = held[:half].astype(F32) + got.astype(F32)
        held = total if half == 1 else total.astype(BF16)
    return held[0]


def in_order(places, held):
    me_w, me_t = lax.axis_index("wide"), lax.axis_index("tensor")
    at = {place: p for p, place in enumerate(places)}
    wide = len(places) // 2
    table = jnp.array([[at[w, t] for w in range(wide)] for t in range(2)], jnp.int32)
    order = table[me_t ^ jnp.arange(2)[:, None], me_w ^ jnp.arange(wide)[None, :]]
    return held[order.reshape(-1)].reshape(16, 48, held.shape[2])


def out_of_order(places, blocks, rows):
    me_w, me_t = lax.axis_index("wide"), lax.axis_index("tensor")
    wide = len(places) // 2
    order = jnp.array([w for w, _ in places], jnp.int32) ^ me_w
    order += wide * (jnp.array([t for _, t in places], jnp.int32) ^ me_t)
    return blocks.reshape(len(places), rows, blocks.shape[2])[order]


def rows_of(places, rows):
    if rows == 48:
        me_w, me_t = 0, 0
        places = [(w, t) for t in range(2) for w in range(8)]
    else:
        me_w, me_t = lax.axis_index("wide"), lax.axis_index("tensor")
    for p, (w, t) in enumerate(places):
        start = (me_w ^ w) * rows
        if rows % 8 == 0:
            start = pl.multiple_of(start, 8)
        yield p, me_t ^ t, pl.ds(start, rows)


def normalize(v):
    center = v - jnp.mean(v, axis=-1, keepdims=True)
    rstd = lax.rsqrt(jnp.mean(center * center, axis=-1, keepdims=True) + 1e-06)
    return center * rstd, rstd


def norm_back(grad, xhat, rstd, gain):
    g = grad * gain
    return rstd * (
        g
        - jnp.mean(g, axis=-1, keepdims=True)
        - xhat * jnp.mean(g * xhat, axis=-1, keepdims=True)
    )


def head_masks(shape):
    lane = lax.broadcasted_iota(jnp.int32, shape, len(shape) - 1)
    return lane < HD


def pick(value, low, side):
    zero = jnp.zeros_like(value)
    return jnp.where(low, value, zero) if side == 0 else jnp.where(low, zero, value)


def attend_kernel(places, rows, buf, x_ref, qkv_ref, probs_ref, heads_ref, n1_ref, w_ref, gain_ref, scr):
    @pl.when(pl.program_id(0) == 0)
    def _():
        for p, t, where in rows_of(places, rows):
            scr[t, where, :] = buf[p].astype(F32)
        for c in range(3):
            at = c * D
            w_ref[:, at : at + 128] = scr[0, :, c * 128 : c * 128 + 128].astype(BF16)
            w_ref[:, at + 128 : at + 256] = scr[1, :, c * 128 : c * 128 + 128].astype(BF16)
            one = 384 + c * HD
            last = jnp.concatenate([scr[0, :, one : one + HD], scr[1, :, one : one + HD]], axis=1)
            w_ref[:, at + 256 : at + 384] = last.astype(BF16)
        turned = scr[0, :, 512:640].T
        gain_ref[...] = turned[HD : HD + 8, :]

    xhat, _ = normalize(x_ref[0].astype(F32))
    n1 = (xhat * gain_ref[0:1, :]).astype(BF16)
    n1_ref[0] = n1
    proj = dot(n1, w_ref[...])
    low = head_masks((PAD, 128))
    key_ok = lax.broadcasted_iota(jnp.int32, (PAD, PAD), 0) < SEQ
    for c in range(3):
        at = slice(c * 128, c * 128 + 128)
        q = (proj[:, at] * (HD**-0.5)).astype(BF16)
        k = proj[:, D + c * 128 : D + c * 128 + 128].astype(BF16)
        v = proj[:, 2 * D + c * 128 : 2 * D + c * 128 + 128].astype(BF16)
        qkv_ref[0, :, at] = q
        qkv_ref[0, :, D + c * 128 : D + c * 128 + 128] = k
        qkv_ref[0, :, 2 * D + c * 128 : 2 * D + c * 128 + 128] = v
        v_turned = v.T
        parts = []
        for side in range(2):
            scores = dot(pick(k, low, side), q, NT)
            scores = jnp.where(key_ok, scores, -1e30)
            expon = jnp.exp(scores - jnp.max(scores, axis=0, keepdims=True))
            probs = expon * (1.0 / jnp.sum(expon, axis=0, keepdims=True))
            probs = probs.astype(BF16)
            probs_ref[0, 2 * c + side] = probs
            parts.append(dot(v_turned[side * HD : side * HD + HD, :], probs))
        heads_ref[0, :, at] = jnp.concatenate(parts, axis=0).T.astype(BF16)


def mlp_kernel(
    places, rows, images, fs, buf, x_ref, og_ref, h_ref, gain_ref,
    mid_ref, hid_ref, mg_ref, hg_ref, fc2_ref, out_ref,
    scr, w_out, w_fc1, n2_all, pg_all, hid_all, og_all, ml_all, h_all,
):
    step = pl.program_id(0)
    half = fs

    @pl.when(step == 0)
    def _():
        for p, t, where in rows_of(places, rows):
            scr[t, where, :] = buf[p].astype(F32)
        w_out[:, 0:128] = scr[0, :, 0:128].astype(BF16)
        w_out[:, 128:256] = scr[1, :, 0:128].astype(BF16)
        w_out[:, 256:384] = jnp.concatenate([scr[0, :, 128:192], scr[1, :, 128:192]], axis=1).astype(BF16)
        for t in range(2):
            w_fc1[:, t * half : t * half + half] = scr[t, :, 256 : 256 + half].astype(BF16)
            fc2_ref[:, t * half : t * half + half] = scr[t, :, 256 + half :].astype(BF16)

    @pl.when(step < images)
    def _():
        at = pl.ds(pl.multiple_of(step * PAD, PAD), PAD)
        gain = gain_ref[1:2, :]
        h = h_ref[0]
        og = og_ref[0]
        h_all[at, :] = h
        og_all[at, :] = og
        middle = x_ref[0].astype(F32) + dot(h, w_out[...], NT)
        mid_ref[0] = middle
        xhat, rstd = normalize(middle)
        n2 = (xhat * gain).astype(BF16)
        n2_all[at, :] = n2
        width = w_fc1.shape[1] // 2
        back = None
        for c in range(2):
            cols = slice(c * width, c * width + width)
            u = dot(n2, w_fc1[:, cols])
            square = u * u
            bent = jnp.tanh(GELU_C * u * (1.0 + 0.044715 * square))
            hid = (0.5 * u * (1.0 + bent)).astype(BF16)
            hid_ref[0, :, cols] = hid
            hid_all[at, cols] = hid
            slope = 0.5 * (1.0 + bent) + 0.5 * u * (1.0 - bent * bent) * (GELU_C * (1.0 + 0.134145 * square))
            pg = (dot(og, fc2_ref[:, cols]) * slope).astype(BF16)
            pg_all[at, cols] = pg
            part = dot(pg, w_fc1[:, cols], NT)
            back = part if back is None else back + part
        mg = og.astype(F32) + norm_back(back, xhat, rstd, gain)
        mg_ref[0] = mg
        ml = mg.astype(BF16)
        ml_all[at, :] = ml
        hg_ref[0] = dot(ml, w_out[...]).astype(BF16)

    @pl.when(step == images)
    def _():
        turned = n2_all[...].T
        row_sum = jnp.zeros((D, 1), F32)
        chunk = half // 3
        for t in range(2):
            for c in range(3):
                cols = slice(t * half + c * chunk, t * half + c * chunk + chunk)
                grad = dot(turned, pg_all[:, cols])
                scr[t, :, 256 + c * chunk : 256 + c * chunk + chunk] = grad
                row_sum += jnp.sum(grad * w_fc1[:, cols].astype(F32), axis=1, keepdims=True)
        turned = og_all[...].T
        for t in range(2):
            for c in range(3):
                cols = slice(t * half + c * chunk, t * half + c * chunk + chunk)
                scr[t, :, 256 + half + c * chunk : 256 + half + c * chunk + chunk] = dot(turned, hid_all[:, cols])
        grad = dot(ml_all[...].T, h_all[...])
        scr[0, :, 0:128] = grad[:, 0:128]
        scr[1, :, 0:128] = grad[:, 128:256]
        gain = jnp.broadcast_to(row_sum, (D, HD))
        scr[0, :, 128:256] = jnp.concatenate([grad[:, 256 : 256 + HD], gain], axis=1)
        scr[1, :, 128:256] = jnp.concatenate([grad[:, 256 + HD : 384], gain], axis=1)
        for p, t, where in rows_of(places, rows):
            out_ref[p] = scr[t, where, :].astype(BF16)


def attend_back_kernel(
    places, rows, images, qkv_ref, probs_ref, hg_ref, n1_ref, w_ref, grad_ref, out_ref, scr, n1_all, grad_all
):
    step = pl.program_id(0)

    @pl.when(step < images)
    def _():
        at = pl.ds(pl.multiple_of(step * PAD, PAD), PAD)
        n1_all[at, :] = n1_ref[0]
        low = head_masks((PAD, 128))
        for c in range(3):
            cols = slice(c * 128, c * 128 + 128)
            kcols = slice(D + c * 128, D + c * 128 + 128)
            vcols = slice(2 * D + c * 128, 2 * D + c * 128 + 128)
            q, k, v = qkv_ref[0, :, cols], qkv_ref[0, :, kcols], qkv_ref[0, :, vcols]
            do = hg_ref[0, :, cols]
            k_turned = k.T
            dq, dk, dv = [], [], []
            for side in range(2):
                probs_low = probs_ref[0, 2 * c + side]
                probs = probs_low.astype(F32)
                dp = dot(pick(v, low, side), do, NT)
                ds = probs * (dp - jnp.sum(probs * dp, axis=0, keepdims=True))
                ds = ds.astype(BF16)
                dv.append(dot(probs_low, do))
                dk.append(dot(ds, q))
                dq.append(dot(k_turned[side * HD : side * HD + HD, :], ds))
            for span, value in (
                (cols, jnp.concatenate(dq, axis=0).T * (HD**-0.5)),
                (kcols, jnp.where(low, dk[0], dk[1])),
                (vcols, jnp.where(low, dv[0], dv[1])),
            ):
                value = value.astype(BF16)
                grad_ref[0, :, span] = value
                grad_all[at, span] = value

    @pl.when(step == images)
    def _():
        turned = n1_all[...].T
        row_sum = jnp.zeros((D, 1), F32)
        singles = []
        for c in range(3):
            span = slice(c * D, c * D + D)
            grad = dot(turned, grad_all[:, span])
            row_sum += jnp.sum(grad * w_ref[:, span].astype(F32), axis=1, keepdims=True)
            scr[0, :, c * 128 : c * 128 + 128] = grad[:, 0:128]
            scr[1, :, c * 128 : c * 128 + 128] = grad[:, 128:256]
            singles.append(grad[:, 256:384])
        gain = jnp.broadcast_to(row_sum, (D, HD))
        for t in range(2):
            own = [s[:, t * HD : t * HD + HD] for s in singles]
            scr[t, :, 384:512] = jnp.concatenate(own[:2], axis=1)
            scr[t, :, 512:640] = jnp.concatenate([own[2], gain], axis=1)
        for p, t, where in rows_of(places, rows):
            out_ref[p] = scr[t, where, :].astype(BF16)


def input_grad_kernel(grad_ref, w_ref, x_ref, mg_ref, gain_ref, out_ref):
    xhat, rstd = normalize(x_ref[0].astype(F32))
    back = dot(grad_ref[0], w_ref[...], NT)
    out_ref[0] = mg_ref[0] + norm_back(back, xhat, rstd, gain_ref[0:1, :])


def layer_out_kernel(hid_ref, fc2_ref, mid_ref, out_ref):
    out_ref[0] = (mid_ref[0] + dot(hid_ref[0], fc2_ref[...], NT)).astype(BF16)


def whole(*shape):
    return pl.BlockSpec(shape, lambda i: (0,) * len(shape))


def per_image(images, *shape):
    return pl.BlockSpec((1,) + shape, lambda i: (jnp.minimum(i, images - 1),) + (0,) * len(shape))


def call(kernel, grid, ins, outs, scratch, args, name, flops, nbytes):
    return pl.pallas_call(
        kernel,
        grid=(grid,),
        in_specs=ins,
        out_specs=[spec for spec, _ in outs],
        out_shape=[shape for _, shape in outs],
        scratch_shapes=scratch,
        compiler_params=pltpu.CompilerParams(vmem_limit_bytes=VMEM_LIMIT),
        cost_estimate=pl.CostEstimate(flops=flops, bytes_accessed=nbytes, transcendentals=0),
        name=name,
    )(*args)


def shape_of(*shape, dtype=BF16):
    return jax.ShapeDtypeStruct(shape, dtype)


def local(sizes, tokens, ln1_gain, qkv_weight, out_weight, ln2_gain, fc1_weight, fc2_weight, out_grad):
    stages = stage_bits(sizes["wide"])
    places = relative(stages)
    n = len(places)
    rows = qkv_weight.shape[0]
    images = tokens.shape[0] // SEQ
    fs = fc1_weight.shape[1]
    ff = 2 * fs
    rc = 256 + 2 * fs

    gains = jnp.stack([ln1_gain, ln2_gain], axis=1).astype(BF16)
    first = jnp.concatenate(
        [qkv_weight[:, c, 0:128] for c in range(3)]
        + [qkv_weight[:, c, 128:192] for c in range(3)]
        + [gains, jnp.zeros((rows, HD - 2), BF16)],
        axis=1,
    )
    rest = jnp.concatenate(
        [out_weight.T, jnp.zeros((rows, HD), BF16), fc1_weight, fc2_weight.T], axis=1
    )
    first_all = gather(first, stages, sizes)
    rest_all = gather(rest, stages, sizes)
    own_rows = rows
    if rows % 8 != 0:
        first_all, rest_all = in_order(places, first_all), in_order(places, rest_all)
        n, rows = 16, 48

    pads = ((0, 0), (0, PAD - SEQ), (0, 0))
    x = jnp.pad(tokens.reshape(images, SEQ, D), pads)
    og = jnp.pad(out_grad.reshape(images, SEQ, D), pads)

    row = functools.partial(per_image, images)
    big = images * PAD
    qkv, probs, heads, n1, w_qkv, gain = call(
        functools.partial(attend_kernel, places, rows),
        images,
        [whole(n, rows, QC), row(PAD, D)],
        [
            (row(PAD, 3 * D), shape_of(images, PAD, 3 * D)),
            (row(6, PAD, PAD), shape_of(images, 6, PAD, PAD)),
            (row(PAD, D), shape_of(images, PAD, D)),
            (row(PAD, D), shape_of(images, PAD, D)),
            (whole(D, 3 * D), shape_of(D, 3 * D)),
            (whole(8, D), shape_of(8, D, dtype=F32)),
        ],
        [pltpu.VMEM((2, D, QC), F32)],
        (first_all, x),
        "attend",
        8 * 10**9,
        20 * 10**6,
    )
    middle, hid, mg, hg, fc2_t, rest_grad = call(
        functools.partial(mlp_kernel, places, rows, images, fs),
        images + 1,
        [whole(n, rows, rc), row(PAD, D), row(PAD, D), row(PAD, D), whole(8, D)],
        [
            (row(PAD, D), shape_of(images, PAD, D, dtype=F32)),
            (row(PAD, ff), shape_of(images, PAD, ff)),
            (row(PAD, D), shape_of(images, PAD, D, dtype=F32)),
            (row(PAD, D), shape_of(images, PAD, D)),
            (whole(D, ff), shape_of(D, ff)),
            (whole(n, rows, rc), shape_of(n, rows, rc)),
        ],
        [
            pltpu.VMEM((2, D, rc), F32),
            pltpu.VMEM((D, D), BF16),
            pltpu.VMEM((D, ff), BF16),
            pltpu.VMEM((big, D), BF16),
            pltpu.VMEM((big, ff), BF16),
            pltpu.VMEM((big, ff), BF16),
            pltpu.VMEM((big, D), BF16),
            pltpu.VMEM((big, D), BF16),
            pltpu.VMEM((big, D), BF16),
        ],
        (rest_all, x, og, heads, gain),
        "mlp",
        14 * 10**9,
        30 * 10**6,
    )
    grads, first_grad = call(
        functools.partial(attend_back_kernel, places, rows, images),
        images + 1,
        [row(PAD, 3 * D), row(6, PAD, PAD), row(PAD, D), row(PAD, D), whole(D, 3 * D)],
        [
            (row(PAD, 3 * D), shape_of(images, PAD, 3 * D)),
            (whole(n, rows, QC), shape_of(n, rows, QC)),
        ],
        [
            pltpu.VMEM((2, D, QC), F32),
            pltpu.VMEM((big, D), BF16),
            pltpu.VMEM((big, 3 * D), BF16),
        ],
        (qkv, probs, hg, n1, w_qkv),
        "attend_back",
        8 * 10**9,
        20 * 10**6,
    )
    (dx,) = call(
        input_grad_kernel,
        images,
        [row(PAD, 3 * D), whole(D, 3 * D), row(PAD, D), row(PAD, D), whole(8, D)],
        [(row(PAD, D), shape_of(images, PAD, D, dtype=F32))],
        [],
        (grads, w_qkv, x, mg, gain),
        "input_grad",
        2 * 10**9,
        10 * 10**6,
    )
    (y,) = call(
        layer_out_kernel,
        images,
        [row(PAD, ff), whole(D, ff), row(PAD, D)],
        [(row(PAD, D), shape_of(images, PAD, D))],
        [],
        (hid, fc2_t, middle),
        "layer_out",
        2 * 10**9,
        10 * 10**6,
    )

    if rows != own_rows:
        rest_grad = out_of_order(places, rest_grad, own_rows)
        first_grad = out_of_order(places, first_grad, own_rows)
    rest_sum = scatter_sum(rest_grad, stages, sizes)
    first_sum = scatter_sum(first_grad, stages, sizes)
    kept1 = ln1_gain.astype(BF16).astype(F32)
    kept2 = ln2_gain.astype(BF16).astype(F32)
    qkv_shard = jnp.stack(
        [
            jnp.concatenate(
                [first_sum[:, c * 128 : c * 128 + 128], first_sum[:, 384 + c * HD : 448 + c * HD]],
                axis=1,
            )
            for c in range(3)
        ],
        axis=1,
    )
    return (
        y[:, :SEQ].reshape(-1, D),
        dx[:, :SEQ].reshape(-1, D),
        first_sum[:, 576] / kept1,
        qkv_shard,
        rest_sum[:, :192].T,
        rest_sum[:, 192] / kept2,
        rest_sum[:, 256 : 256 + fs],
        rest_sum[:, 256 + fs :].T,
    )


def solution(mesh):
    rows = P(("wide", "tensor"), None)
    weights = (
        P("wide"),
        P("wide", None, "tensor"),
        P("tensor", "wide"),
        P("wide"),
        P("wide", "tensor"),
        P("tensor", "wide"),
    )
    return jax.shard_map(
        functools.partial(local, dict(mesh.shape)),
        mesh=mesh,
        in_specs=(rows, *weights, rows),
        out_specs=(rows, rows, *weights),
        check_vma=False,
    )
```

time: 676 us -> 200 us (0.30)
  waiting for transfers between devices: 273 us -> 56.7 us
  blocking collectives: 175 us -> 0 us
  matrix products: 91.8 us -> 0 us
  Pallas kernels: 0 us -> 85 us
  local copies, waits for them, and re-layouts: 87.6 us -> 31.2 us
  starting transfers between devices: 0.67 us -> 19.9 us
  other arithmetic: 23.9 us -> 5.02 us
  between operations: 16.3 us -> 0.89 us
    unnamed x13 -> x0, waiting for transfers between devices: 181 us -> none
    all_gather x6 -> x0, blocking collectives: 105 us -> none  [the longest x1 26.6 us: local(): lax.all_gather(fc1_weight, 'wide', axis=0, tiled=True)]
    reduce_scatter x5 -> x0, waiting for transfers between devices: 92.3 us -> none  [the longest x1 61.3 us: local(): lax.psum_scatter(fc1_grad, 'wide', scatter_dimension=0, tiled=True)]
    dot_general x18 -> x0, matrix products: 91.8 us -> none  [the longest x1 10.6 us: local(): jnp.dot(out_grad, fc2_full.T, preferred_element_type=jnp.float32)]
    pallas_call x0 -> x5, Pallas kernels: none -> 85 us  [call(): pl.pallas_call(kernel, grid=(grid,), in_specs=ins, out_specs=[spec for sp...]
    unnamed x2 -> x0, blocking collectives: 64.2 us -> none
    ppermute x0 -> x20, waiting for transfers between devices: none -> 56.7 us  [swap(): return lax.ppermute(value, axis, [(i, i ^ bit) for i in range(sizes[axis])])]
    another operation x13 -> x2, local copies, waits for them, and re-layouts: 56.2 us -> 0.2 us  [local(): gains = jnp.stack([ln1_gain, ln2_gain], axis=1).astype(BF16)]
  transfers between devices with their start and end apart: 10 -> 20, of which waited for: 6 -> 11; matrix products, arithmetic and copies ran while one was open for 15% -> 12% of each run, Pallas kernels for 0% -> 18%
where the time goes in v1:
time: 200 us; the launch traced here: 199 us
  Pallas kernels  85 us (42%)
  waiting for transfers between devices  56.7 us (28%)
  local copies, waits for them, and re-layouts  31.2 us (16%)
  starting transfers between devices  19.9 us (10%)
  other arithmetic  5.02 us (3%)
    pallas_call x5, Pallas kernels, call(): pl.pallas_call(kernel, grid=(grid,), in_specs=ins, out_specs=[spec for sp...  85 us
    ppermute x20, waiting for transfers between devices, swap(): return lax.ppermute(value, axis, [(i, i ^ bit) for i in range(sizes[axis])])  56.7 us
    ppermute x20, starting transfers between devices, swap(): return lax.ppermute(value, axis, [(i, i ^ bit) for i in range(sizes[axis])])  19.9 us
    unnamed x24, local copies, waits for them, and re-layouts  7.4 us
  transfers between devices with their start and end apart: 20, of which 11 were waited for; matrix products, arithmetic and copies ran while one was open for 12% of the time, Pallas kernels for 18%

profile of v1, /device:TPU:0, one launch (start us, length us, event | category | flops | bytes accessed | tf_op | source)
XLA Modules:
  0.0 198.8 jit_solution(7869685846400455513)
XLA Ops:
  3.7 3.1 %collective-permute-start.5 = (bf16[1,24,640]{2,1,0:T(8,128)(2,1)S(1)}, bf16[1,24,640]{2,1,0:T(8,128)(2,1)S(1)}, u32[]{:S(2)}, u32[]{:S(2)}) collective-permute-start(bf16[1,24,640]{2,1,0:T(8,128)(2,1)S(1)} %bitcast.42), channel_id=1, source_target_pairs={{0,8},{2,10},{4,12},{6,14},{8,0},{10,2},{12,4},{14,6},{16,24},{18,... | collective-permute-start | bytes 92168 | tf_op jit(solution)/shard_map/ppermute | solution.py:42
  9.0 3.2 %collective-permute-done = bf16[1,24,1792]{2,1,0:T(8,128)(2,1)S(1)} collective-permute-done((bf16[1,24,1792]{2,1,0:T(8,128)(2,1)S(1)}, bf16[1,24,1792]{2,1,0:T(8,128)(2,1)S(1)}, u32[]{:S(2)}, u32[]{:S(2)}) %collective-permute-start) | collective-permute-done | bytes 86048 | tf_op jit(solution)/shard_map/ppermute | solution.py:42
  12.2 2.7 %collective-permute-start.1 = (bf16[2,24,1792]{2,1,0:T(8,128)(2,1)S(1)}, bf16[2,24,1792]{2,1,0:T(8,128)(2,1)S(1)}, u32[]{:S(2)}, u32[]{:S(2)}) collective-permute-start(bf16[2,24,1792]{2,1,0:T(8,128)(2,1)S(1)} %pad_maximum_fusion.3), channel_id=1, source_target_pairs={{0,16},{2,18},{4,20},{6,22},{8,24},{10,26},{12,28},{14,30},{16,0},... | collective-permute-start | bytes 516104 | tf_op jit(solution)/shard_map/ppermute | solution.py:42
  15.9 7.5 %collective-permute-done.1 = bf16[2,24,1792]{2,1,0:T(8,128)(2,1)S(1)} collective-permute-done((bf16[2,24,1792]{2,1,0:T(8,128)(2,1)S(1)}, bf16[2,24,1792]{2,1,0:T(8,128)(2,1)S(1)}, u32[]{:S(2)}, u32[]{:S(2)}) %collective-permute-start.1) | collective-permute-done | bytes 172064 | tf_op jit(solution)/shard_map/ppermute | solution.py:42
  23.5 1.6 collective-permute-start.2
  27.0 6.8 %collective-permute-done.2 = bf16[4,24,1792]{2,1,0:T(8,128)(2,1)S(1)} collective-permute-done((bf16[4,24,1792]{2,1,0:T(8,128)(2,1)S(1)}, bf16[4,24,1792]{2,1,0:T(8,128)(2,1)S(1)}, u32[]{:S(2)}, u32[]{:S(2)}) %collective-permute-start.2) | collective-permute-done | bytes 344096 | tf_op jit(solution)/shard_map/ppermute | solution.py:42
  33.9 1.6 collective-permute-start.3
  35.5 1.2 collective-permute-start.8
  38.9 11.8 %collective-permute-done.3 = bf16[8,24,1792]{2,1,0:T(8,128)(2,1)S(1)} collective-permute-done((bf16[8,24,1792]{2,1,0:T(8,128)(2,1)S(1)}, bf16[8,24,1792]{2,1,0:T(8,128)(2,1)S(1)}, u32[]{:S(2)}, u32[]{:S(2)}) %collective-permute-start.3) | collective-permute-done | bytes 688160 | tf_op jit(solution)/shard_map/ppermute | solution.py:42
  51.7 1.7 collective-permute-done.8
  54.2 1.6 reshape.28
  57.0 1.6 reshape.29
  58.7 1.2 pad.8.og_ref
  60.7 17.0 %attend.1 = (bf16[8,208,1152]{2,1,0:T(8,128)(2,1)}, bf16[8,6,208,208]{3,2,1,0:T(8,128)(2,1)}, bf16[8,208,384]{2,1,0:T(8,128)(2,1)}, bf16[8,208,384]{2,1,0:T(8,12...) custom-call(bf16[32,24,640]{2,1,0:T(8,128)(2,1)} %constant_dynamic-update-slice_fusion.16.buf, ...), custom_call_target="tpu_custom_call" | custom-call | flops 8000000000 | bytes 20000000 | tf_op jit(solution)/shard_map/attend/pallas_call | solution.py:314
  78.9 29.0 %mlp.1 = (f32[8,208,384]{2,1,0:T(8,128)}, bf16[8,208,1536]{2,1,0:T(8,128)(2,1)}, f32[8,208,384]{2,1,0:T(8,128)}, bf16[8,208,384]{2,1,0:T(8,128)(2,1)}, bf16[384,...) custom-call(bf16[32,24,1792]{2,1,0:T(8,128)(2,1)} %constant_dynamic-update-slice_fusion.5.buf, ...), custom_call_target="tpu_custom_call" | custom-call | flops 14000000000 | bytes 30000000 | tf_op jit(solution)/shard_map/mlp/pallas_call | solution.py:314
  107.9 20.6 %attend_back.1 = (bf16[8,208,1152]{2,1,0:T(8,128)(2,1)}, bf16[32,24,640]{2,1,0:T(8,128)(2,1)}) custom-call(bf16[8,208,1152]{2,1,0:T(8,128)(2,1)} %get-tuple-element.27.qkv_ref, bf16[8,6,208,208]{3,2,1,0:T(8,128)(2,1)} %get-tuple-element.28.probs_ref, bf16[8,208,384]{2,1,0:T(8,128)(2,1)} %get-tuple-element.29.hg_ref, ...), custom_call_target="tpu_custom_call" | custom-call | flops 8000000000 | bytes 20000000 | tf_op jit(solution)/shard_map/attend_back/pallas_call | solution.py:314
  132.0 1.5 collective-permute-start.11
  133.4 6.6 %collective-permute-done.11 = bf16[8,24,640]{2,1,0:T(8,128)(2,1)S(1)} collective-permute-done((bf16[8,24,640]{2,1,0:T(8,128)(2,1)S(1)}, bf16[8,24,640]{2,1,0:T(8,128)(2,1)S(1)}, u32[]{:S(2)}, u32[]{:S(2)}) %collective-permute-start.11) | collective-permute-done | bytes 245792 | tf_op jit(solution)/shard_map/ppermute | solution.py:42
  141.5 1.4 collective-permute-start.12
  142.9 9.4 %input_grad.1 = f32[8,208,384]{2,1,0:T(8,128)} custom-call(bf16[8,208,1152]{2,1,0:T(8,128)(2,1)} %get-tuple-element.32.grad_ref, bf16[384,1152]{1,0:T(8,128)(2,1)} %get-tuple-element.31.w_ref, bf16[8,208,384]{2,1,0:T(8,128)(2,1)} %pad.7.x_ref, f32[8,208,384]{2,1,0:T(8,128)} %get-tuple-element.33.mg_ref, f32[8,384]{1,0:T(8,128)} %get-tuple-element.23.gain_ref), custom_call_target="tpu_custom_call" | custom-call | flops 2000000000 | bytes 10000000 | tf_op jit(solution)/shard_map/input_grad/pallas_call | solution.py:314
  155.8 1.5 collective-permute-start.16
  157.3 1.3 collective-permute-done.13
  158.7 1.6 collective-permute-start.14
  160.4 9.0 %layer_out.1 = bf16[8,208,384]{2,1,0:T(8,128)(2,1)} custom-call(bf16[8,208,1536]{2,1,0:T(8,128)(2,1)} %get-tuple-element.24.hid_ref, bf16[384,1536]{1,0:T(8,128)(2,1)} %get-tuple-element.25.fc2_ref, f32[8,208,384]{2,1,0:T(8,128)} %get-tuple-element.26.mid_ref), custom_call_target="tpu_custom_call" | custom-call | flops 2000000000 | bytes 10000000 | tf_op jit(solution)/shard_map/layer_out/pallas_call | solution.py:314
  169.4 1.7 slice-done
  171.1 1.7 reshape.31
  172.8 1.3 slice-done.1
  174.1 1.4 reshape.30
  176.6 7.4 %collective-permute-done.17 = bf16[4,24,1792]{2,1,0:T(8,128)(2,1)S(1)} collective-permute-done((bf16[4,24,1792]{2,1,0:T(8,128)(2,1)S(1)}, bf16[4,24,1792]{2,1,0:T(8,128)(2,1)S(1)}, u32[]{:S(2)}, u32[]{:S(2)}) %collective-permute-start.17) | collective-permute-done | bytes 344096 | tf_op jit(solution)/shard_map/ppermute | solution.py:42
  184.2 1.4 collective-permute-start.18
  186.1 6.2 %collective-permute-done.18 = bf16[2,24,1792]{2,1,0:T(8,128)(2,1)S(1)} collective-permute-done((bf16[2,24,1792]{2,1,0:T(8,128)(2,1)S(1)}, bf16[2,24,1792]{2,1,0:T(8,128)(2,1)S(1)}, u32[]{:S(2)}, u32[]{:S(2)}) %collective-permute-start.18) | collective-permute-done | bytes 172064 | tf_op jit(solution)/shard_map/ppermute | solution.py:42
  193.0 3.8 %collective-permute-done.19 = bf16[1,24,1792]{2,1,0:T(8,128)(2,1)S(1)} collective-permute-done((bf16[1,24,1792]{2,1,0:T(8,128)(2,1)S(1)}, bf16[1,24,1792]{2,1,0:T(8,128)(2,1)S(1)}, u32[]{:S(2)}, u32[]{:S(2)}) %collective-permute-start.19) | collective-permute-done | bytes 86048 | tf_op jit(solution)/shard_map/ppermute | solution.py:42
  (98 shorter events, 28.3 us)
Async XLA Ops:
  3.7 11.2 %collective-permute-start.5 = (bf16[1,24,640]{2,1,0:T(8,128)(2,1)S(1)}, bf16[1,24,640]{2,1,0:T(8,128)(2,1)S(1)}, u32[]{:S(2)}, u32[]{:S(2)}) collective-permute-start(bf16[1,24,640]{2,1,0:T(8,128)(2,1)S(1)} %bitcast.42), channel_id=1, source_target_pairs={{0,8},{2,10},{4,12},{6,14},{8,0},{10,2},{12,4},{14,6},{16,24},{18,... | collective-permute-start | bytes 92168 | tf_op jit(solution)/shard_map/ppermute | solution.py:42
  7.7 4.5 %collective-permute-start = (bf16[1,24,1792]{2,1,0:T(8,128)(2,1)S(1)}, bf16[1,24,1792]{2,1,0:T(8,128)(2,1)S(1)}, u32[]{:S(2)}, u32[]{:S(2)}) collective-permute-start(bf16[1,24,1792]{2,1,0:T(8,128)(2,1)S(1)} %bitcast.38), channel_id=1, source_target_pairs={{0,8},{2,10},{4,12},{6,14},{8,0},{10,2},{12,4},{14,6},{16,24},{18,... | collective-permute-start | bytes 258056 | tf_op jit(solution)/shard_map/ppermute | solution.py:42
  12.2 11.2 %collective-permute-start.1 = (bf16[2,24,1792]{2,1,0:T(8,128)(2,1)S(1)}, bf16[2,24,1792]{2,1,0:T(8,128)(2,1)S(1)}, u32[]{:S(2)}, u32[]{:S(2)}) collective-permute-start(bf16[2,24,1792]{2,1,0:T(8,128)(2,1)S(1)} %pad_maximum_fusion.3), channel_id=1, source_target_pairs={{0,16},{2,18},{4,20},{6,22},{8,24},{10,26},{12,28},{14,30},{16,0},... | collective-permute-start | bytes 516104 | tf_op jit(solution)/shard_map/ppermute | solution.py:42
  14.9 10.8 %collective-permute-start.6 = (bf16[2,24,640]{2,1,0:T(8,128)(2,1)S(1)}, bf16[2,24,640]{2,1,0:T(8,128)(2,1)S(1)}, u32[]{:S(2)}, u32[]{:S(2)}) collective-permute-start(bf16[2,24,640]{2,1,0:T(8,128)(2,1)S(1)} %pad_maximum_fusion.6), channel_id=1, source_target_pairs={{0,16},{2,18},{4,20},{6,22},{8,24},{10,26},{12,28},{14,30},{16,0},... | collective-permute-start | bytes 184328 | tf_op jit(solution)/shard_map/ppermute | solution.py:42
  23.5 10.3 %collective-permute-start.2 = (bf16[4,24,1792]{2,1,0:T(8,128)(2,1)S(1)}, bf16[4,24,1792]{2,1,0:T(8,128)(2,1)S(1)}, u32[]{:S(2)}, u32[]{:S(2)}) collective-permute-start(bf16[4,24,1792]{2,1,0:T(8,128)(2,1)S(1)} %pad_maximum_fusion.1), channel_id=1, source_target_pairs={{0,4},{2,6},{4,0},{6,2},{8,12},{10,14},{12,8},{14,10},{16,20},{18,... | collective-permute-start | bytes 1032200 | tf_op jit(solution)/shard_map/ppermute | solution.py:42
  25.8 9.7 %collective-permute-start.7 = (bf16[4,24,640]{2,1,0:T(8,128)(2,1)S(1)}, bf16[4,24,640]{2,1,0:T(8,128)(2,1)S(1)}, u32[]{:S(2)}, u32[]{:S(2)}) collective-permute-start(bf16[4,24,640]{2,1,0:T(8,128)(2,1)S(1)} %pad_maximum_fusion.4), channel_id=1, source_target_pairs={{0,4},{2,6},{4,0},{6,2},{8,12},{10,14},{12,8},{14,10},{16,20},{18,... | collective-permute-start | bytes 368648 | tf_op jit(solution)/shard_map/ppermute | solution.py:42
  33.9 16.8 %collective-permute-start.3 = (bf16[8,24,1792]{2,1,0:T(8,128)(2,1)S(1)}, bf16[8,24,1792]{2,1,0:T(8,128)(2,1)S(1)}, u32[]{:S(2)}, u32[]{:S(2)}) collective-permute-start(bf16[8,24,1792]{2,1,0:T(8,128)(2,1)S(1)} %pad_maximum_fusion), channel_id=1, source_target_pairs={{0,1},{1,0},{2,3},{3,2},{4,5},{5,4},{6,7},{7,6},{8,9},{9,8},{10,11... | collective-permute-start | bytes 2064392 | tf_op jit(solution)/shard_map/ppermute | solution.py:42
  35.5 17.9 %collective-permute-start.8 = (bf16[8,24,640]{2,1,0:T(8,128)(2,1)S(1)}, bf16[8,24,640]{2,1,0:T(8,128)(2,1)S(1)}, u32[]{:S(2)}, u32[]{:S(2)}) collective-permute-start(bf16[8,24,640]{2,1,0:T(8,128)(2,1)S(1)} %pad_maximum_fusion.2), channel_id=1, source_target_pairs={{0,1},{1,0},{2,3},{3,2},{4,5},{5,4},{6,7},{7,6},{8,9},{9,8},{10,11... | collective-permute-start | bytes 737288 | tf_op jit(solution)/shard_map/ppermute | solution.py:42
  51.7 2.5 %copy-start.5 = (bf16[32,24,1792]{2,1,0:T(8,128)(2,1)}, bf16[32,24,1792]{2,1,0:T(8,128)(2,1)S(1)}, u32[]{:S(2)}) copy-start(bf16[32,24,1792]{2,1,0:T(8,128)(2,1)S(1)} %get-tuple-element.37) | copy-start | bytes 8257540
  51.7 26.1 %collective-permute-start.4 = (bf16[16,24,1792]{2,1,0:T(8,128)(2,1)}, bf16[16,24,1792]{2,1,0:T(8,128)(2,1)S(1)}, u32[]{:S(2)}, u32[]{:S(2)}) collective-permute-start(bf16[16,24,1792]{2,1,0:T(8,128)(2,1)} %get-tuple-element.36), channel_id=1, source_target_pairs={{0,2},{2,0},{4,6},{6,4},{8,10},{10,8},{12,14},{14,12},{16,18},{18,... | collective-permute-start | bytes 4128776 | tf_op jit(solution)/shard_map/ppermute | solution.py:42
  54.2 5.7 %collective-permute-start.9 = (bf16[16,24,640]{2,1,0:T(8,128)(2,1)}, bf16[16,24,640]{2,1,0:T(8,128)(2,1)S(1)}, u32[]{:S(2)}, u32[]{:S(2)}) collective-permute-start(bf16[16,24,640]{2,1,0:T(8,128)(2,1)} %get-tuple-element.40), channel_id=1, source_target_pairs={{0,2},{2,0},{4,6},{6,4},{8,10},{10,8},{12,14},{14,12},{16,18},{18,... | collective-permute-start | bytes 1474568 | tf_op jit(solution)/shard_map/ppermute | solution.py:42
  107.9 22.3 %copy-start.2 = (bf16[32,24,1792]{2,1,0:T(8,128)(2,1)S(1)}, bf16[32,24,1792]{2,1,0:T(8,128)(2,1)}, u32[]{:S(2)}) copy-start(bf16[32,24,1792]{2,1,0:T(8,128)(2,1)} %get-tuple-element.35) | copy-start | bytes 8257540
  129.6 2.1 %collective-permute-start.10 = (bf16[16,24,640]{2,1,0:T(8,128)(2,1)S(1)}, bf16[16,24,640]{2,1,0:T(8,128)(2,1)S(1)}, u32[]{:S(2)}, u32[]{:S(2)}) collective-permute-start(bf16[16,24,640]{2,1,0:T(8,128)(2,1)S(1)} %slice.126), channel_id=1, source_target_pairs={{0,2},{2,0},{4,6},{6,4},{8,10},{10,8},{12,14},{14,12},{16,18},{18,... | collective-permute-start | bytes 1474568 | tf_op jit(solution)/shard_map/ppermute | solution.py:42
  130.1 1.7 copy-start.3
  131.3 22.1 %collective-permute-start.15 = (bf16[16,24,1792]{2,1,0:T(8,128)(2,1)}, bf16[16,24,1792]{2,1,0:T(8,128)(2,1)S(1)}, u32[]{:S(2)}, u32[]{:S(2)}) collective-permute-start(bf16[16,24,1792]{2,1,0:T(8,128)(2,1)} %slice.143), channel_id=1, source_target_pairs={{0,2},{2,0},{4,6},{6,4},{8,10},{10,8},{12,14},{14,12},{16,18},{18,... | collective-permute-start | bytes 4128776 | tf_op jit(solution)/shard_map/ppermute | solution.py:42
  132.0 8.1 %collective-permute-start.11 = (bf16[8,24,640]{2,1,0:T(8,128)(2,1)S(1)}, bf16[8,24,640]{2,1,0:T(8,128)(2,1)S(1)}, u32[]{:S(2)}, u32[]{:S(2)}) collective-permute-start(bf16[8,24,640]{2,1,0:T(8,128)(2,1)S(1)} %slice.159), channel_id=1, source_target_pairs={{0,1},{1,0},{2,3},{3,2},{4,5},{5,4},{6,7},{7,6},{8,9},{9,8},{10,11... | collective-permute-start | bytes 737288 | tf_op jit(solution)/shard_map/ppermute | solution.py:42
  140.1 0.7 copy-start.4
  141.5 10.8 %collective-permute-start.12 = (bf16[4,24,640]{2,1,0:T(8,128)(2,1)}, bf16[4,24,640]{2,1,0:T(8,128)(2,1)}, u32[]{:S(2)}, u32[]{:S(2)}) collective-permute-start(bf16[4,24,640]{2,1,0:T(8,128)(2,1)} %slice.161), channel_id=1, source_target_pairs={{0,4},{2,6},{4,0},{6,2},{8,12},{10,14},{12,8},{14,10},{16,20},{18,... | collective-permute-start | bytes 368648 | tf_op jit(solution)/shard_map/ppermute | solution.py:42
  153.4 5.3 %collective-permute-start.13 = (bf16[2,24,640]{2,1,0:T(8,128)(2,1)S(1)}, bf16[2,24,640]{2,1,0:T(8,128)(2,1)S(1)}, u32[]{:S(2)}, u32[]{:S(2)}) collective-permute-start(bf16[2,24,640]{2,1,0:T(8,128)(2,1)S(1)} %slice.163), channel_id=1, source_target_pairs={{0,16},{2,18},{4,20},{6,22},{8,24},{10,26},{12,28},{14,30},{16,0},... | collective-permute-start | bytes 184328 | tf_op jit(solution)/shard_map/ppermute | solution.py:42
  153.8 1.1 copy-start
  155.8 19.8 %collective-permute-start.16 = (bf16[8,24,1792]{2,1,0:T(8,128)(2,1)}, bf16[8,24,1792]{2,1,0:T(8,128)(2,1)S(1)}, u32[]{:S(2)}, u32[]{:S(2)}) collective-permute-start(bf16[8,24,1792]{2,1,0:T(8,128)(2,1)} %slice.174), channel_id=1, source_target_pairs={{0,1},{1,0},{2,3},{3,2},{4,5},{5,4},{6,7},{7,6},{8,9},{9,8},{10,11... | collective-permute-start | bytes 2064392 | tf_op jit(solution)/shard_map/ppermute | solution.py:42
  158.7 16.8 %collective-permute-start.14 = (bf16[1,24,640]{2,1,0:T(8,128)(2,1)S(1)}, bf16[1,24,640]{2,1,0:T(8,128)(2,1)S(1)}, u32[]{:S(2)}, u32[]{:S(2)}) collective-permute-start(bf16[1,24,640]{2,1,0:T(8,128)(2,1)S(1)} %slice.165), channel_id=1, source_target_pairs={{0,8},{2,10},{4,12},{6,14},{8,0},{10,2},{12,4},{14,6},{16,24},{18,... | collective-permute-start | bytes 92168 | tf_op jit(solution)/shard_map/ppermute | solution.py:42
  169.4 1.7 slice-start
  172.8 1.3 slice-start.1
  174.1 1.5 copy-start.1
  175.8 9.8 %copy-start.6 = (f32[24]{0:T(128)S(1)}, f32[24]{0:T(128)}, u32[]{:S(2)}) copy-start(f32[24]{0:T(128)} %param.9) | copy-start | bytes 292
  175.8 8.2 %collective-permute-start.17 = (bf16[4,24,1792]{2,1,0:T(8,128)(2,1)S(1)}, bf16[4,24,1792]{2,1,0:T(8,128)(2,1)S(1)}, u32[]{:S(2)}, u32[]{:S(2)}) collective-permute-start(bf16[4,24,1792]{2,1,0:T(8,128)(2,1)S(1)} %slice.176), channel_id=1, source_target_pairs={{0,4},{2,6},{4,0},{6,2},{8,12},{10,14},{12,8},{14,10},{16,20},{18,... | collective-permute-start | bytes 1032200 | tf_op jit(solution)/shard_map/ppermute | solution.py:42
  176.6 21.7 %copy-start.7 = (f32[24]{0:T(128)S(1)}, f32[24]{0:T(128)}, u32[]{:S(2)}) copy-start(f32[24]{0:T(128)} %param.12) | copy-start | bytes 292
  184.2 8.1 %collective-permute-start.18 = (bf16[2,24,1792]{2,1,0:T(8,128)(2,1)S(1)}, bf16[2,24,1792]{2,1,0:T(8,128)(2,1)S(1)}, u32[]{:S(2)}, u32[]{:S(2)}) collective-permute-start(bf16[2,24,1792]{2,1,0:T(8,128)(2,1)S(1)} %slice.178), channel_id=1, source_target_pairs={{0,16},{2,18},{4,20},{6,22},{8,24},{10,26},{12,28},{14,30},{16,0},... | collective-permute-start | bytes 516104 | tf_op jit(solution)/shard_map/ppermute | solution.py:42
  192.3 4.6 %collective-permute-start.19 = (bf16[1,24,1792]{2,1,0:T(8,128)(2,1)S(1)}, bf16[1,24,1792]{2,1,0:T(8,128)(2,1)S(1)}, u32[]{:S(2)}, u32[]{:S(2)}) collective-permute-start(bf16[1,24,1792]{2,1,0:T(8,128)(2,1)S(1)} %slice.180), channel_id=1, source_target_pairs={{0,8},{2,10},{4,12},{6,14},{8,0},{10,2},{12,4},{14,6},{16,24},{18,... | collective-permute-start | bytes 258056 | tf_op jit(solution)/shard_map/ppermute | solution.py:42

commit v2 on v1

v2 whole, which is shorter than its diff:
```python
import functools

import jax
import jax.numpy as jnp
from jax import lax
from jax.experimental import pallas as pl
from jax.experimental.pallas import tpu as pltpu
from jax.sharding import PartitionSpec as P

HD = 64
SEQ = 197
PAD = 208
PER = 2
D = 384
QC = 640
F32 = jnp.float32
BF16 = jnp.bfloat16
NT = (((1,), (1,)), ((), ()))
GELU_C = 0.7978845608028654
VMEM_LIMIT = 60 * 1024 * 1024


def dot(a, b, dims=(((1,), (0,)), ((), ()))):
    return lax.dot_general(a, b, dims, preferred_element_type=F32)


def stage_bits(wide):
    bits = [("wide", 1 << k) for k in range(1, wide.bit_length() - 1)]
    bits = bits[:0:-1] + bits[:1]
    return bits + [("tensor", 1), ("wide", 1)]


def relative(stages):
    places = [(0, 0)]
    for axis, bit in stages:
        places = places + [(w ^ bit, t) if axis == "wide" else (w, t ^ bit) for w, t in places]
    return places


def swap(value, stage, sizes):
    axis, bit = stage
    return lax.ppermute(value, axis, [(i, i ^ bit) for i in range(sizes[axis])])


def gather(block, stages, sizes):
    held = block
    for stage in stages[:-2]:
        got = swap(held, stage, sizes)
        held = jnp.concatenate([held, got], axis=0)
    got = swap(held, stages[-2], sizes)
    return [held, got, swap(held, stages[-1], sizes), swap(got, stages[-1], sizes)]


def half_sum(keep, send, stage, sizes):
    got = swap(send, stage, sizes)
    total = (keep.astype(F32) + got.astype(F32)).astype(BF16)
    half = total.shape[0] // 2
    return total[:half], total[half:]


def in_order(places, held):
    me_w, me_t = lax.axis_index("wide"), lax.axis_index("tensor")
    at = {place: p for p, place in enumerate(places)}
    wide = len(places) // 2
    table = jnp.array([[at[w, t] for w in range(wide)] for t in range(2)], jnp.int32)
    order = table[me_t ^ jnp.arange(2)[:, None], me_w ^ jnp.arange(wide)[None, :]]
    return held[order.reshape(-1)].reshape(16, 48, held.shape[2])


def out_of_order(places, blocks, rows):
    me_w, me_t = lax.axis_index("wide"), lax.axis_index("tensor")
    wide = len(places) // 2
    order = jnp.array([w for w, _ in places], jnp.int32) ^ me_w
    order += wide * (jnp.array([t for _, t in places], jnp.int32) ^ me_t)
    return blocks.reshape(len(places), rows, blocks.shape[2])[order]


def rows_of(places, rows):
    if rows == 48:
        me_w, me_t = 0, 0
        places = [(w, t) for t in range(2) for w in range(8)]
    else:
        me_w, me_t = lax.axis_index("wide"), lax.axis_index("tensor")
    for p, (w, t) in enumerate(places):
        yield p, me_t ^ t, pl.ds(pl.multiple_of((me_w ^ w) * rows, 8), rows)


def unpack(places, rows, pieces, scr, at=0):
    size = len(pieces[0])
    width = pieces[0].shape[-1]
    for p, t, where in rows_of(places, rows):
        scr[t, where, at : at + width] = pieces[p // size][p % size].astype(F32)


def repack(places, rows, scr, pieces, at=0):
    size = len(pieces[0])
    width = pieces[0].shape[-1]
    for p, t, where in rows_of(places, rows):
        pieces[p // size][p % size] = scr[t, where, at : at + width].astype(BF16)


def normalize(v):
    center = v - jnp.mean(v, axis=-1, keepdims=True)
    rstd = lax.rsqrt(jnp.mean(center * center, axis=-1, keepdims=True) + 1e-06)
    return center * rstd, rstd


def norm_back(grad, xhat, rstd, gain):
    g = grad * gain
    return rstd * (
        g
        - jnp.mean(g, axis=-1, keepdims=True)
        - xhat * jnp.mean(g * xhat, axis=-1, keepdims=True)
    )


def low_lanes():
    return lax.broadcasted_iota(jnp.int32, (PAD, 128), 1) < HD


def pick(value, low, side):
    zero = jnp.zeros_like(value)
    return jnp.where(low, value, zero) if side == 0 else jnp.where(low, zero, value)


def tall(ref):
    return ref[...].reshape(PER * PAD, ref.shape[-1])


def column(row):
    n = row.shape[1]
    own = lax.broadcasted_iota(jnp.int32, (n, n), 0) == lax.broadcasted_iota(jnp.int32, (n, n), 1)
    return jnp.sum(jnp.where(own, jnp.broadcast_to(row, (n, n)), 0.0), axis=1, keepdims=True)


def line(col):
    n = col.shape[0]
    own = lax.broadcasted_iota(jnp.int32, (n, n), 0) == lax.broadcasted_iota(jnp.int32, (n, n), 1)
    return jnp.sum(jnp.where(own, jnp.broadcast_to(col, (n, n)), 0.0), axis=0, keepdims=True)


def pack_kernel(qkv, gain1, gain2, out, fc1, fc2, first, rest):
    rows = out.shape[0]
    fs = fc1.shape[1]
    lane = lax.broadcasted_iota(jnp.int32, (rows, HD), 1)
    gains = jnp.where(lane == 0, column(gain1[...]), jnp.where(lane == 1, column(gain2[...]), 0.0))
    for c in range(3):
        first[0, :, c * 128 : c * 128 + 128] = qkv[c, :, 0:128]
    single = [qkv[c, :, 128:192].astype(F32) for c in range(3)]
    first[0, :, 384:512] = jnp.concatenate(single[:2], axis=1).astype(BF16)
    first[0, :, 512:640] = jnp.concatenate([single[2], gains], axis=1).astype(BF16)
    rest[0, :, 0:128] = out[:, 0:128]
    pad = jnp.zeros((rows, HD), F32)
    rest[0, :, 128:256] = jnp.concatenate([out[:, 128:192].astype(F32), pad], axis=1).astype(BF16)
    rest[0, :, 256 : 256 + fs] = fc1[...]
    rest[0, :, 256 + fs :] = fc2[...]


def attend_kernel(places, rows, p0, p1, p2, p3, x_ref, qkv_ref, probs_ref, heads_ref, n1_ref, w_ref, gain_ref, scr):
    @pl.when(pl.program_id(0) == 0)
    def _():
        unpack(places, rows, (p0, p1, p2, p3), scr)
        for c in range(3):
            at = c * D
            w_ref[:, at : at + 128] = scr[0, :, c * 128 : c * 128 + 128].astype(BF16)
            w_ref[:, at + 128 : at + 256] = scr[1, :, c * 128 : c * 128 + 128].astype(BF16)
            one = 384 + c * HD
            last = jnp.concatenate([scr[0, :, one : one + HD], scr[1, :, one : one + HD]], axis=1)
            w_ref[:, at + 256 : at + 384] = last.astype(BF16)
        turned = scr[0, :, 512:640].T
        gain_ref[...] = turned[HD : HD + 8, :]

    xhat, _ = normalize(tall(x_ref).astype(F32))
    n1 = (xhat * gain_ref[0:1, :]).astype(BF16)
    n1_ref[...] = n1.reshape(PER, PAD, D)
    proj = dot(n1, w_ref[...])
    low = low_lanes()
    key_ok = lax.broadcasted_iota(jnp.int32, (PAD, PAD), 0) < SEQ
    for i in range(PER):
        mine = slice(i * PAD, i * PAD + PAD)
        for c in range(3):
            at = slice(c * 128, c * 128 + 128)
            q = (proj[mine, at] * (HD**-0.5)).astype(BF16)
            k = proj[mine, D + c * 128 : D + c * 128 + 128].astype(BF16)
            v = proj[mine, 2 * D + c * 128 : 2 * D + c * 128 + 128].astype(BF16)
            qkv_ref[i, :, at] = q
            qkv_ref[i, :, D + c * 128 : D + c * 128 + 128] = k
            qkv_ref[i, :, 2 * D + c * 128 : 2 * D + c * 128 + 128] = v
            v_turned = v.T
            parts = []
            for side in range(2):
                scores = dot(pick(k, low, side), q, NT)
                scores = jnp.where(key_ok, scores, -1e30)
                expon = jnp.exp(scores - jnp.max(scores, axis=0, keepdims=True))
                probs = expon * (1.0 / jnp.sum(expon, axis=0, keepdims=True))
                probs = probs.astype(BF16)
                probs_ref[i, 2 * c + side] = probs
                parts.append(dot(v_turned[side * HD : side * HD + HD, :], probs))
            heads_ref[i, :, at] = jnp.concatenate(parts, axis=0).T.astype(BF16)


def mlp_kernel(
    places, places2, rows, blocks, fs, p0, p1, p2, p3, x_ref, og_ref, h_ref, gain_ref,
    mid_ref, hid_ref, mg_ref, hg_ref, fc2_ref, keep1, send1, keep2, send2,
    scr, w_out, w_back, w_fc1, w_fc1_turned, n2_all, pg_all, hid_all, og_all, ml_all, h_all,
):
    step = pl.program_id(0)

    @pl.when(step == 0)
    def _():
        unpack(places, rows, (p0, p1, p2, p3), scr)
        last = jnp.concatenate([scr[0, :, 128:192], scr[1, :, 128:192]], axis=1)
        for b, value in enumerate((scr[0, :, 0:128], scr[1, :, 0:128], last)):
            w_back[:, b * 128 : b * 128 + 128] = value.astype(BF16)
            w_out[b * 128 : b * 128 + 128, :] = value.T.astype(BF16)
        for t in range(2):
            at = slice(t * fs, t * fs + fs)
            w_fc1[:, at] = scr[t, :, 256 : 256 + fs].astype(BF16)
            w_fc1_turned[at, :] = scr[t, :, 256 : 256 + fs].T.astype(BF16)
            fc2_ref[:, at] = scr[t, :, 256 + fs :].astype(BF16)

    @pl.when(step < blocks)
    def _():
        size = PER * PAD
        at = pl.ds(pl.multiple_of(step * size, size), size)
        gain = gain_ref[1:2, :]
        h = tall(h_ref)
        og = tall(og_ref)
        h_all[at, :] = h
        og_all[at, :] = og
        middle = tall(x_ref).astype(F32) + dot(h, w_out[...])
        mid_ref[...] = middle.reshape(PER, PAD, D)
        xhat, rstd = normalize(middle)
        n2 = (xhat * gain).astype(BF16)
        n2_all[at, :] = n2
        width = fs // 2
        back = None
        for c in range(4):
            cols = slice(c * width, c * width + width)
            u = dot(n2, w_fc1[:, cols])
            square = u * u
            bent = jnp.tanh(u * (GELU_C + (GELU_C * 0.044715) * square))
            plus = 0.5 + 0.5 * bent
            hid = (u * plus).astype(BF16)
            hid_ref[:, :, cols] = hid.reshape(PER, PAD, width)
            hid_all[at, cols] = hid
            slope = plus * (1.0 + u * (1.0 - bent) * (GELU_C + (GELU_C * 0.134145) * square))
            pg = (dot(og, fc2_ref[:, cols]) * slope).astype(BF16)
            pg_all[at, cols] = pg
            part = dot(pg, w_fc1_turned[cols, :])
            back = part if back is None else back + part
        mg = og.astype(F32) + norm_back(back, xhat, rstd, gain)
        mg_ref[...] = mg.reshape(PER, PAD, D)
        ml = mg.astype(BF16)
        ml_all[at, :] = ml
        hg_ref[...] = dot(ml, w_back[...]).astype(BF16).reshape(PER, PAD, D)

    @pl.when(step == blocks)
    def _():
        turned = n2_all[...].T
        row_sum = jnp.zeros((D, 1), F32)
        chunk = fs // 3
        for t in range(2):
            for c in range(3):
                cols = slice(t * fs + c * chunk, t * fs + c * chunk + chunk)
                grad = dot(turned, pg_all[:, cols])
                scr[t, :, 256 + c * chunk : 256 + c * chunk + chunk] = grad
                row_sum += jnp.sum(grad * w_fc1[:, cols].astype(F32), axis=1, keepdims=True)
        turned = og_all[...].T
        for t in range(2):
            for c in range(3):
                cols = slice(t * fs + c * chunk, t * fs + c * chunk + chunk)
                scr[t, :, 256 + fs + c * chunk : 256 + fs + c * chunk + chunk] = dot(turned, hid_all[:, cols])
        grad = dot(ml_all[...].T, h_all[...])
        scr[0, :, 0:128] = grad[:, 0:128]
        scr[1, :, 0:128] = grad[:, 128:256]
        gain = jnp.broadcast_to(row_sum, (D, HD))
        scr[0, :, 128:256] = jnp.concatenate([grad[:, 256 : 256 + HD], gain], axis=1)
        scr[1, :, 128:256] = jnp.concatenate([grad[:, 256 + HD : 384], gain], axis=1)
        repack(places, rows, scr, (keep1, send1))
        repack(places2, rows, scr, (keep2, send2), 256 + fs)


def attend_back(qkv_ref, probs_ref, hg_ref, grad_ref, grad_all, at):
    low = low_lanes()
    for i in range(PER):
        for c in range(3):
            cols = slice(c * 128, c * 128 + 128)
            kcols = slice(D + c * 128, D + c * 128 + 128)
            vcols = slice(2 * D + c * 128, 2 * D + c * 128 + 128)
            q, k, v = qkv_ref[i, :, cols], qkv_ref[i, :, kcols], qkv_ref[i, :, vcols]
            do = hg_ref[i, :, cols]
            k_turned = k.T
            dq, dk, dv = [], [], []
            for side in range(2):
                probs_low = probs_ref[i, 2 * c + side]
                probs = probs_low.astype(F32)
                dp = dot(pick(v, low, side), do, NT)
                ds = probs * (dp - jnp.sum(probs * dp, axis=0, keepdims=True))
                ds = ds.astype(BF16)
                dv.append(dot(probs_low, do))
                dk.append(dot(ds, q))
                dq.append(dot(k_turned[side * HD : side * HD + HD, :], ds))
            for span, value in (
                (cols, jnp.concatenate(dq, axis=0).T * (HD**-0.5)),
                (kcols, jnp.where(low, dk[0], dk[1])),
                (vcols, jnp.where(low, dv[0], dv[1])),
            ):
                value = value.astype(BF16)
                grad_ref[i, :, span] = value
                if grad_all is not None:
                    grad_all[pl.ds(pl.multiple_of(at + i * PAD, PAD), PAD), span] = value


def attend_back_kernel(qkv_ref, probs_ref, hg_ref, grad_ref):
    attend_back(qkv_ref, probs_ref, hg_ref, grad_ref, None, 0)


def attend_last_kernel(
    places, rows, blocks, qkv_ref, probs_ref, hg_ref, n1_ref, w_ref, *refs
):
    *earlier, grad_ref, keep, send, scr, grad_all = refs
    step = pl.program_id(0)
    early = sum(ref.shape[0] for ref in earlier) * PAD

    @pl.when(step == 0)
    def _():
        at = 0
        for ref in earlier:
            size = ref.shape[0] * PAD
            grad_all[at : at + size, :] = ref[...].reshape(size, 3 * D)
            at += size

    @pl.when(step < blocks)
    def _():
        attend_back(qkv_ref, probs_ref, hg_ref, grad_ref, grad_all, early + step * PER * PAD)

    @pl.when(step == blocks)
    def _():
        turned = n1_ref[...].reshape(-1, D).T
        row_sum = jnp.zeros((D, 1), F32)
        singles = []
        for c in range(3):
            span = slice(c * D, c * D + D)
            grad = dot(turned, grad_all[:, span])
            row_sum += jnp.sum(grad * w_ref[:, span].astype(F32), axis=1, keepdims=True)
            scr[0, :, c * 128 : c * 128 + 128] = grad[:, 0:128]
            scr[1, :, c * 128 : c * 128 + 128] = grad[:, 128:256]
            singles.append(grad[:, 256:384])
        gain = jnp.broadcast_to(row_sum, (D, HD))
        for t in range(2):
            own = [s[:, t * HD : t * HD + HD] for s in singles]
            scr[t, :, 384:512] = jnp.concatenate(own[:2], axis=1)
            scr[t, :, 512:640] = jnp.concatenate([own[2], gain], axis=1)
        repack(places, rows, scr, (keep, send))


def store_rows(ref, value, step, steps):
    for s in range(steps):

        @pl.when(step == s)
        def _(s=s):
            for i in range(PER):
                at = (s * PER + i) * SEQ
                ref[at : at + SEQ, :] = value[i * PAD : i * PAD + SEQ]


def input_grad_kernel(cuts, *refs):
    *pieces, w_ref, x_ref, mg_ref, gain_ref, out_ref, w_turned, grad = refs
    step = pl.program_id(0)

    @pl.when(step == 0)
    def _():
        w_turned[...] = w_ref[...].T

    at = 0
    for ref, count in zip(pieces, cuts, strict=True):

        @pl.when((step >= at) & (step < at + count))
        def _(ref=ref):
            grad[...] = tall(ref)

        at += count
    xhat, rstd = normalize(tall(x_ref).astype(F32))
    back = dot(grad[...], w_turned[...])
    dx = tall(mg_ref) + norm_back(back, xhat, rstd, gain_ref[0:1, :])
    store_rows(out_ref, dx, step, sum(cuts))


def layer_out_kernel(blocks, hid_ref, fc2_ref, mid_ref, out_ref, w_turned, all_rows):
    step = pl.program_id(0)

    @pl.when(step == 0)
    def _():
        w_turned[...] = fc2_ref[...].T

    y = tall(mid_ref) + dot(tall(hid_ref), w_turned[...])
    store_rows(all_rows, y, step, blocks)

    @pl.when(step == blocks - 1)
    def _():
        out_ref[...] = all_rows[...].astype(BF16)


def finish_first_kernel(mine, got, gain_ref, gain_grad, qkv_grad):
    total = mine[0].astype(F32) + got[0].astype(F32)
    for c in range(3):
        qkv_grad[c, :, 0:128] = total[:, c * 128 : c * 128 + 128]
        qkv_grad[c, :, 128:192] = total[:, 384 + c * HD : 448 + c * HD]
    gain_grad[...] = line(total[:, 576:577]) / gain_ref[...].astype(BF16).astype(F32)


def finish_rest_kernel(fs, mine, got, gain_ref, gain_grad, out_grad, fc1_grad, fc2_grad):
    total = mine[0].astype(F32) + got[0].astype(F32)
    out_grad[...] = total[:, :192]
    fc1_grad[...] = total[:, 256 : 256 + fs]
    fc2_grad[...] = total[:, 256 + fs :]
    gain_grad[...] = line(total[:, 192:193]) / gain_ref[...].astype(BF16).astype(F32)


def whole(*shape):
    return pl.BlockSpec(shape, lambda *i: (0,) * len(shape))


def part(first, count, *shape):
    return pl.BlockSpec((PER,) + shape, lambda i: (first + jnp.minimum(i, count - 1),) + (0,) * len(shape))


def late(first, count, *shape):
    return pl.BlockSpec((PER,) + shape, lambda i: (jnp.clip(i - first, 0, count - 1),) + (0,) * len(shape))


def call(kernel, grid, ins, outs, scratch, args, mflops=0, kbytes=0):
    return pl.pallas_call(
        kernel,
        grid=(grid,) if grid else (),
        in_specs=ins,
        out_specs=[spec for spec, _ in outs],
        out_shape=[shape for _, shape in outs],
        scratch_shapes=scratch,
        compiler_params=pltpu.CompilerParams(vmem_limit_bytes=VMEM_LIMIT),
        cost_estimate=pl.CostEstimate(flops=mflops * 10**6, bytes_accessed=kbytes * 1000, transcendentals=0),
    )(*args)


def shape_of(*shape, dtype=BF16):
    return jax.ShapeDtypeStruct(shape, dtype)


def padded(v, images):
    return jnp.pad(v.reshape(images, SEQ, D), ((0, 0), (0, PAD - SEQ), (0, 0)))


def local(sizes, tokens, ln1_gain, qkv_weight, out_weight, ln2_gain, fc1_weight, fc2_weight, out_grad):
    return layer(sizes, tokens, ln1_gain, qkv_weight, out_weight, ln2_gain, fc1_weight, fc2_weight, out_grad)


def layer(sizes, tokens, ln1_gain, qkv_weight, out_weight, ln2_gain, fc1_weight, fc2_weight, out_grad):
    stages = stage_bits(sizes["wide"])
    stages2 = stages[:-3] + [stages[-2], stages[-3], stages[-1]]
    places, places2 = relative(stages), relative(stages2)
    n = len(places)
    rows = own_rows = qkv_weight.shape[0]
    images = tokens.shape[0] // SEQ
    blocks = images // PER
    fs = fc1_weight.shape[1]
    ff = 2 * fs
    rc = 256 + 2 * fs
    big = images * PAD
    gain1, gain2 = ln1_gain.reshape(1, rows), ln2_gain.reshape(1, rows)

    first, rest = call(
        pack_kernel,
        0,
        [whole(3, rows, 192), whole(1, rows), whole(1, rows), whole(rows, 192), whole(rows, fs), whole(rows, fs)],
        [(whole(1, rows, QC), shape_of(1, rows, QC)), (whole(1, rows, rc), shape_of(1, rows, rc))],
        [],
        (qkv_weight.transpose(1, 0, 2), gain1, gain2, out_weight.T, fc1_weight, fc2_weight.T),
    )
    first_all = gather(first, stages, sizes)
    rest_all = gather(rest, stages, sizes)
    if rows % 8 != 0:
        n, rows = 16, 48
        first_all, rest_all = (
            jnp.split(in_order(places, jnp.concatenate(v, axis=0)), 4) for v in (first_all, rest_all)
        )

    x = padded(tokens, images)
    og = padded(out_grad, images)

    def row(*shape):
        return part(0, blocks, *shape)

    qkv, probs, heads, n1, w_qkv, gain = call(
        functools.partial(attend_kernel, places, rows),
        blocks,
        [whole(n // 4, rows, QC)] * 4 + [row(PAD, D)],
        [
            (row(PAD, 3 * D), shape_of(images, PAD, 3 * D)),
            (row(6, PAD, PAD), shape_of(images, 6, PAD, PAD)),
            (row(PAD, D), shape_of(images, PAD, D)),
            (row(PAD, D), shape_of(images, PAD, D)),
            (whole(D, 3 * D), shape_of(D, 3 * D)),
            (whole(8, D), shape_of(8, D, dtype=F32)),
        ],
        [pltpu.VMEM((2, D, QC), F32)],
        (*first_all, x),
        8000,
        20000,
    )
    wide1, wide2 = 256 + fs, fs
    middle, hid, mg, hg, fc2_t, keep1, send1, keep2, send2 = call(
        functools.partial(mlp_kernel, places, places2, rows, blocks, fs),
        blocks + 1,
        [whole(n // 4, rows, rc)] * 4 + [row(PAD, D), row(PAD, D), row(PAD, D), whole(8, D)],
        [
            (row(PAD, D), shape_of(images, PAD, D, dtype=F32)),
            (row(PAD, ff), shape_of(images, PAD, ff)),
            (row(PAD, D), shape_of(images, PAD, D, dtype=F32)),
            (row(PAD, D), shape_of(images, PAD, D)),
            (whole(D, ff), shape_of(D, ff)),
        ]
        + [(whole(n // 2, rows, w), shape_of(n // 2, rows, w)) for w in (wide1, wide1, wide2, wide2)],
        [
            pltpu.VMEM((2, D, rc), F32),
            pltpu.VMEM((D, D), BF16),
            pltpu.VMEM((D, D), BF16),
            pltpu.VMEM((D, ff), BF16),
            pltpu.VMEM((ff, D), BF16),
            pltpu.VMEM((big, D), BF16),
            pltpu.VMEM((big, ff), BF16),
            pltpu.VMEM((big, ff), BF16),
            pltpu.VMEM((big, D), BF16),
            pltpu.VMEM((big, D), BF16),
            pltpu.VMEM((big, D), BF16),
        ],
        (*rest_all, x, og, heads, gain),
        14000,
        30000,
    )

    if rows != own_rows:
        keep1, send1 = jnp.split(out_of_order(places, jnp.concatenate([keep1, send1], axis=0), own_rows), 2)
        keep2, send2 = jnp.split(out_of_order(places2, jnp.concatenate([keep2, send2], axis=0), own_rows), 2)
    back, back2 = stages[::-1], stages2[::-1]
    for s in range(3):
        keep1, send1 = half_sum(keep1, send1, back[s], sizes)
        keep2, send2 = half_sum(keep2, send2, back2[s], sizes)
    keep = jnp.concatenate([keep1, keep2], axis=2)
    send = jnp.concatenate([send1, send2], axis=2)
    for s in range(3, len(back) - 1):
        keep, send = half_sum(keep, send, back[s], sizes)
    got = swap(send, back[-1], sizes)
    ln2_grad, out_wgrad, fc1_grad, fc2_grad = call(
        functools.partial(finish_rest_kernel, fs),
        0,
        [whole(1, own_rows, rc)] * 2 + [whole(1, own_rows)],
        [
            (whole(1, own_rows), shape_of(1, own_rows, dtype=F32)),
            (whole(own_rows, 192), shape_of(own_rows, 192, dtype=F32)),
            (whole(own_rows, fs), shape_of(own_rows, fs, dtype=F32)),
            (whole(own_rows, fs), shape_of(own_rows, fs, dtype=F32)),
        ],
        [],
        (keep, got, gain2),
    )

    cuts = (1, blocks - 2, 1)
    pieces = []
    at = 0
    for count in cuts[:-1]:
        pieces += call(
            attend_back_kernel,
            count,
            [part(at, count, *s) for s in ((PAD, 3 * D), (6, PAD, PAD), (PAD, D))],
            [(part(0, count, PAD, 3 * D), shape_of(count * PER, PAD, 3 * D))],
            [],
            (qkv, probs, hg),
            1800 * count,
            4000 * count,
        )
        at += count
    left = cuts[-1]
    last, keep, send = call(
        functools.partial(attend_last_kernel, places, rows, left),
        left + 1,
        [part(at, left, *s) for s in ((PAD, 3 * D), (6, PAD, PAD), (PAD, D))]
        + [whole(images, PAD, D), whole(D, 3 * D)]
        + [whole(count * PER, PAD, 3 * D) for count in cuts[:-1]],
        [(part(0, left, PAD, 3 * D), shape_of(left * PER, PAD, 3 * D))]
        + [(whole(n // 2, rows, QC), shape_of(n // 2, rows, QC))] * 2,
        [pltpu.VMEM((2, D, QC), F32), pltpu.VMEM((big, 3 * D), BF16)],
        (qkv, probs, hg, n1, w_qkv, *pieces),
        3500,
        8000,
    )
    pieces.append(last)
    starts = [sum(cuts[:c]) for c in range(len(cuts))]
    (dx,) = call(
        functools.partial(input_grad_kernel, cuts),
        blocks,
        [late(at, count, PAD, 3 * D) for at, count in zip(starts, cuts, strict=True)]
        + [whole(D, 3 * D), row(PAD, D), row(PAD, D), whole(8, D)],
        [(whole(images * SEQ, D), shape_of(images * SEQ, D, dtype=F32))],
        [pltpu.VMEM((3 * D, D), BF16), pltpu.VMEM((PER * PAD, 3 * D), BF16)],
        (*pieces, w_qkv, x, mg, gain),
        2000,
        10000,
    )
    (y,) = call(
        functools.partial(layer_out_kernel, blocks),
        blocks,
        [row(PAD, ff), whole(D, ff), row(PAD, D)],
        [(whole(images * SEQ, D), shape_of(images * SEQ, D))],
        [pltpu.VMEM((ff, D), BF16), pltpu.VMEM((images * SEQ, D), F32)],
        (hid, fc2_t, middle),
        2000,
        10000,
    )

    if rows != own_rows:
        keep, send = jnp.split(out_of_order(places, jnp.concatenate([keep, send], axis=0), own_rows), 2)
    for stage in back[:-1]:
        keep, send = half_sum(keep, send, stage, sizes)
    got = swap(send, back[-1], sizes)
    ln1_grad, qkv_grad = call(
        finish_first_kernel,
        0,
        [whole(1, own_rows, QC)] * 2 + [whole(1, own_rows)],
        [
            (whole(1, own_rows), shape_of(1, own_rows, dtype=F32)),
            (whole(3, own_rows, 192), shape_of(3, own_rows, 192, dtype=F32)),
        ],
        [],
        (keep, got, gain1),
    )
    return (
        y,
        dx,
        ln1_grad.reshape(own_rows),
        qkv_grad.transpose(1, 0, 2),
        out_wgrad.T,
        ln2_grad.reshape(own_rows),
        fc1_grad,
        fc2_grad.T,
    )


def solution(mesh):
    rows = P(("wide", "tensor"), None)
    weights = (
        P("wide"),
        P("wide", None, "tensor"),
        P("tensor", "wide"),
        P("wide"),
        P("wide", "tensor"),
        P("tensor", "wide"),
    )
    return jax.shard_map(
        functools.partial(local, dict(mesh.shape)),
        mesh=mesh,
        in_specs=(rows, *weights, rows),
        out_specs=(rows, rows, *weights),
        check_vma=False,
    )
```

time: 200 us -> 187 us (0.935)
  local copies, waits for them, and re-layouts: 31.2 us -> 9.9 us
  starting transfers between devices: 19.9 us -> 37 us
  waiting for transfers between devices: 56.7 us -> 43.9 us
  Pallas kernels: 85 us -> 91.3 us
    ppermute x20 -> x25, starting transfers between devices: 19.9 us -> 37 us  [swap(): return lax.ppermute(value, axis, [(i, i ^ bit) for i in range(sizes[axis])])]
    ppermute x20 -> x25, waiting for transfers between devices: 56.7 us -> 43.9 us  [swap(): return lax.ppermute(value, axis, [(i, i ^ bit) for i in range(sizes[axis])])]
    pallas_call x5 -> x10, Pallas kernels: 85 us -> 91.3 us  [call(): pl.pallas_call(kernel, grid=(grid,) if grid else (), in_specs=ins, out_sp...]
    slice x18 -> x11, local copies, waits for them, and re-layouts: 7.33 us -> 1.4 us  [half_sum(): return (total[:half], total[half:])]
    concatenate x6 -> x2, local copies, waits for them, and re-layouts: 4.73 us -> 0.04 us  [gather(): held = jnp.concatenate([held, got], axis=0)]
    reshape x4 -> x2, local copies, waits for them, and re-layouts: 6.39 us -> 2.01 us  [padded(): return jnp.pad(v.reshape(images, SEQ, D), ((0, 0), (0, PAD - SEQ), (0, 0)))]
    unnamed x24 -> x32, local copies, waits for them, and re-layouts: 7.4 us -> 4.06 us
    concatenate x6 -> x5, other arithmetic: 0.19 us -> 2.62 us  [the longest x4 2.61 us: gather(): held = jnp.concatenate([held, got], axis=0)]
  transfers between devices with their start and end apart: 20 -> 25, of which waited for: 11 -> 10; matrix products, arithmetic and copies ran while one was open for 12% -> 6% of each run, Pallas kernels for 18% -> 18%
where the time goes in v2:
time: 187 us
  Pallas kernels  91.3 us (49%)
  waiting for transfers between devices  43.9 us (23%)
  starting transfers between devices  37 us (20%)
  local copies, waits for them, and re-layouts  9.9 us (5%)
  other arithmetic  3.63 us (2%)
    pallas_call x10, Pallas kernels, call(): pl.pallas_call(kernel, grid=(grid,) if grid else (), in_specs=ins, out_sp...  91.3 us
    ppermute x25, waiting for transfers between devices, swap(): return lax.ppermute(value, axis, [(i, i ^ bit) for i in range(sizes[axis])])  43.9 us
    ppermute x25, starting transfers between devices, swap(): return lax.ppermute(value, axis, [(i, i ^ bit) for i in range(sizes[axis])])  37 us
    unnamed x32, local copies, waits for them, and re-layouts  4.06 us
  transfers between devices with their start and end apart: 25, of which 10 were waited for; matrix products, arithmetic and copies ran while one was open for 6% of the time, Pallas kernels for 18%

profile of v2, /device:TPU:0, one launch (start us, length us, event | category | flops | bytes accessed | tf_op | source)
XLA Modules:
  0.0 186.7 jit_solution(8313669708837863217)
XLA Ops:
  0.6 1.6 shard_map.143
  2.3 4.1 %collective-permute-start.6 = (bf16[1,24,640]{2,1,0:T(8,128)(2,1)}, bf16[1,24,640]{2,1,0:T(8,128)(2,1)S(1)}, u32[]{:S(2)}, u32[]{:S(2)}) collective-permute-start(bf16[1,24,640]{2,1,0:T(8,128)(2,1)} %get-tuple-element.35), channel_id=1, source_target_pairs={{0,16},{2,18},{4,20},{6,22},{8,24},{10,26},{12,28},{14,30},{16,0},... | collective-permute-start | bytes 92168 | tf_op jit(solution)/shard_map/ppermute | solution.py:42
  9.6 2.4 %collective-permute-start.7 = (bf16[2,24,640]{2,1,0:T(8,128)(2,1)S(1)}, bf16[2,24,640]{2,1,0:T(8,128)(2,1)S(1)}, u32[]{:S(2)}, u32[]{:S(2)}) collective-permute-start(bf16[2,24,640]{2,1,0:T(8,128)(2,1)S(1)} %pad_maximum_fusion.4), channel_id=1, source_target_pairs={{0,8},{2,10},{4,12},{6,14},{8,0},{10,2},{12,4},{14,6},{16,24},{18,... | collective-permute-start | bytes 184328 | tf_op jit(solution)/shard_map/ppermute | solution.py:42
  12.0 1.6 collective-permute-done
  14.6 5.4 %collective-permute-done.1 = bf16[2,24,1792]{2,1,0:T(8,128)(2,1)S(1)} collective-permute-done((bf16[2,24,1792]{2,1,0:T(8,128)(2,1)S(1)}, bf16[2,24,1792]{2,1,0:T(8,128)(2,1)S(1)}, u32[]{:S(2)}, u32[]{:S(2)}) %collective-permute-start.1) | collective-permute-done | bytes 172064 | tf_op jit(solution)/shard_map/ppermute | solution.py:42
  20.9 1.6 collective-permute-start.2
  23.1 6.0 %collective-permute-done.2 = bf16[4,24,1792]{2,1,0:T(8,128)(2,1)S(1)} collective-permute-done((bf16[4,24,1792]{2,1,0:T(8,128)(2,1)S(1)}, bf16[4,24,1792]{2,1,0:T(8,128)(2,1)S(1)}, u32[]{:S(2)}, u32[]{:S(2)}) %collective-permute-start.2) | collective-permute-done | bytes 344096 | tf_op jit(solution)/shard_map/ppermute | solution.py:42
  29.1 1.6 collective-permute-start.3
  32.0 14.7 %collective-permute-done.9.p1 = bf16[8,24,640]{2,1,0:T(8,128)(2,1)} collective-permute-done((bf16[8,24,640]{2,1,0:T(8,128)(2,1)S(1)}, bf16[8,24,640]{2,1,0:T(8,128)(2,1)}, u32[]{:S(2)}, u32[]{:S(2)}) %collective-permute-start.9) | collective-permute-done | bytes 245792 | tf_op jit(solution)/shard_map/ppermute | solution.py:42
  47.1 1.6 reshape.37
  51.7 16.3 %shard_map.144 = (bf16[8,208,1152]{2,1,0:T(8,128)(2,1)}, bf16[8,6,208,208]{3,2,1,0:T(8,128)(2,1)}, bf16[8,208,384]{2,1,0:T(8,128)(2,1)}, bf16[8,208,384]{2,1,0:T...) custom-call(bf16[8,24,640]{2,1,0:T(8,128)(2,1)} %copy-done.8, bf16[8,24,640]{2,1,0:T(8,128)(2,1)} %collective-permute-done.9.p1, ...), custom_call_target="tpu_custom_call" | custom-call | flops 8000000000 | bytes 20000000 | tf_op jit(solution)/shard_map/pallas_call | solution.py:434
  69.1 28.0 %shard_map.145 = (f32[8,208,384]{2,1,0:T(8,128)}, bf16[8,208,1536]{2,1,0:T(8,128)(2,1)}, f32[8,208,384]{2,1,0:T(8,128)}, bf16[8,208,384]{2,1,0:T(8,128)(2,1)}, b...) custom-call(bf16[8,24,1792]{2,1,0:T(8,128)(2,1)} %copy-done.7, ...), custom_call_target="tpu_custom_call" | custom-call | flops 14000000000 | bytes 30000000 | tf_op jit(solution)/shard_map/pallas_call | solution.py:434
  97.1 5.8 %shard_map.147.refs_0_ = bf16[2,208,1152]{2,1,0:T(8,128)(2,1)} custom-call(bf16[8,208,1152]{2,1,0:T(8,128)(2,1)} %get-tuple-element.41.qkv_ref, bf16[8,6,208,208]{3,2,1,0:T(8,128)(2,1)} %get-tuple-element.42.probs_ref, bf16[8,208,384]{2,1,0:T(8,128)(2,1)} %get-tuple-element.43.hg_ref), custom_call_target="tpu_custom_call" | custom-call | flops 1800000000 | bytes 4000000 | tf_op jit(solution)/shard_map/pallas_call | solution.py:434
  102.9 9.1 %shard_map.148.refs_1_ = bf16[4,208,1152]{2,1,0:T(8,128)(2,1)} custom-call(bf16[8,208,1152]{2,1,0:T(8,128)(2,1)} %get-tuple-element.41.qkv_ref, bf16[8,6,208,208]{3,2,1,0:T(8,128)(2,1)} %get-tuple-element.42.probs_ref, bf16[8,208,384]{2,1,0:T(8,128)(2,1)} %get-tuple-element.43.hg_ref), custom_call_target="tpu_custom_call" | custom-call | flops 3600000000 | bytes 8000000 | tf_op jit(solution)/shard_map/pallas_call | solution.py:434
  112.1 10.9 %shard_map.149 = (bf16[2,208,1152]{2,1,0:T(8,128)(2,1)}, bf16[16,24,640]{2,1,0:T(8,128)(2,1)}, bf16[16,24,640]{2,1,0:T(8,128)(2,1)}) custom-call(bf16[8,208,1152]{2,1,0:T(8,128)(2,1)} %get-tuple-element.41.qkv_ref, bf16[8,6,208,208]{3,2,1,0:T(8,128)(2,1)} %get-tuple-element.42.probs_ref, bf16[8,208,384]{2,1,0:T(8,128)(2,1)} %get-tuple-element.43.hg_ref, ...), custom_call_target="tpu_custom_call" | custom-call | flops 3500000000 | bytes 8000000 | tf_op jit(solution)/shard_map/pallas_call | solution.py:434
  123.9 8.7 %shard_map.150 = f32[1576,384]{1,0:T(8,128)} custom-call(bf16[2,208,1152]{2,1,0:T(8,128)(2,1)} %shard_map.147.refs_0_, bf16[4,208,1152]{2,1,0:T(8,128)(2,1)} %shard_map.148.refs_1_, bf16[2,208,1152]{2,1,0:T(8,128)(2,1)} %get-tuple-element.46.refs_2_, bf16[384,1152]{1,0:T(8,128)(2,1)} %get-tuple-element.45.w_ref.refs_3_, ...), custom_call_target="tpu_custom_call" | custom-call | flops 2000000000 | bytes 10000000 | tf_op jit(solution)/shard_map/pallas_call | solution.py:434
  132.8 1.6 collective-permute-start.13
  134.6 1.6 collective-permute-start.21
  136.2 4.7 %collective-permute-done.13 = bf16[8,24,640]{2,1,0:T(8,128)(2,1)S(1)} collective-permute-done((bf16[8,24,640]{2,1,0:T(8,128)(2,1)S(1)}, bf16[8,24,640]{2,1,0:T(8,128)(2,1)S(1)}, u32[]{:S(2)}, u32[]{:S(2)}) %collective-permute-start.13) | collective-permute-done | bytes 245792 | tf_op jit(solution)/shard_map/ppermute | solution.py:42
  140.9 1.6 collective-permute-start.14
  142.8 1.6 collective-permute-start.18
  144.4 1.6 collective-permute-done.14
  146.0 4.0 %collective-permute-start.15 = (bf16[2,24,640]{2,1,0:T(8,128)(2,1)S(1)}, bf16[2,24,640]{2,1,0:T(8,128)(2,1)S(1)}, u32[]{:S(2)}, u32[]{:S(2)}) collective-permute-start(bf16[2,24,640]{2,1,0:T(8,128)(2,1)S(1)} %slice.93), channel_id=1, source_target_pairs={{0,8},{2,10},{4,12},{6,14},{8,0},{10,2},{12,4},{14,6},{16,24},{18,... | collective-permute-start | bytes 184328 | tf_op jit(solution)/shard_map/ppermute | solution.py:42
  150.1 1.4 collective-permute-start.22
  152.2 3.8 %collective-permute-done.22 = bf16[4,24,768]{2,1,0:T(8,128)(2,1)S(1)} collective-permute-done((bf16[4,24,768]{2,1,0:T(8,128)(2,1)S(1)}, bf16[4,24,768]{2,1,0:T(8,128)(2,1)S(1)}, u32[]{:S(2)}, u32[]{:S(2)}) %collective-permute-start.22) | collective-permute-done | bytes 147488 | tf_op jit(solution)/shard_map/ppermute | solution.py:42
  157.1 4.8 %collective-permute-done.19 = bf16[4,24,1024]{2,1,0:T(8,128)(2,1)S(1)} collective-permute-done((bf16[4,24,1024]{2,1,0:T(8,128)(2,1)S(1)}, bf16[4,24,1024]{2,1,0:T(8,128)(2,1)S(1)}, u32[]{:S(2)}, u32[]{:S(2)}) %collective-permute-start.19) | collective-permute-done | bytes 196640 | tf_op jit(solution)/shard_map/ppermute | solution.py:42
  162.1 4.0 %collective-permute-start.23 = (bf16[2,24,1792]{2,1,0:T(8,128)(2,1)S(1)}, bf16[2,24,1792]{2,1,0:T(8,128)(2,1)S(1)}, u32[]{:S(2)}, u32[]{:S(2)}) collective-permute-start(bf16[2,24,1792]{2,1,0:T(8,128)(2,1)S(1)} %pad_maximum_fusion.2), channel_id=1, source_target_pairs={{0,8},{2,10},{4,12},{6,14},{8,0},{10,2},{12,4},{14,6},{16,24},{18,... | collective-permute-start | bytes 516104 | tf_op jit(solution)/shard_map/ppermute | solution.py:42
  166.7 4.2 %collective-permute-start.16 = (bf16[1,24,640]{2,1,0:T(8,128)(2,1)S(1)}, bf16[1,24,640]{2,1,0:T(8,128)(2,1)S(1)}, u32[]{:S(2)}, u32[]{:S(2)}) collective-permute-start(bf16[1,24,640]{2,1,0:T(8,128)(2,1)S(1)} %get-tuple-element.66), channel_id=1, source_target_pairs={{0,16},{2,18},{4,20},{6,22},{8,24},{10,26},{12,28},{14,30},{16,0},... | collective-permute-start | bytes 92168 | tf_op jit(solution)/shard_map/ppermute | solution.py:42
  171.6 3.1 %collective-permute-start.24 = (bf16[1,24,1792]{2,1,0:T(8,128)(2,1)S(1)}, bf16[1,24,1792]{2,1,0:T(8,128)(2,1)S(1)}, u32[]{:S(2)}, u32[]{:S(2)}) collective-permute-start(bf16[1,24,1792]{2,1,0:T(8,128)(2,1)S(1)} %get-tuple-element.62), channel_id=1, source_target_pairs={{0,16},{2,18},{4,20},{6,22},{8,24},{10,26},{12,28},{14,30},{16,0},... | collective-permute-start | bytes 258056 | tf_op jit(solution)/shard_map/ppermute | solution.py:42
  174.7 7.7 %shard_map.146 = bf16[1576,384]{1,0:T(8,128)(2,1)} custom-call(bf16[8,208,1536]{2,1,0:T(8,128)(2,1)} %get-tuple-element.38.hid_ref, bf16[384,1536]{1,0:T(8,128)(2,1)} %get-tuple-element.39.fc2_ref, f32[8,208,384]{2,1,0:T(8,128)} %get-tuple-element.40.mid_ref), custom_call_target="tpu_custom_call" | custom-call | flops 2000000000 | bytes 10000000 | tf_op jit(solution)/shard_map/pallas_call | solution.py:434
  182.9 1.5 shard_map.151
  185.1 1.6 shard_map.152
  (93 shorter events, 17.7 us)
Async XLA Ops:
  2.3 20.2 %copy-start.4 = (bf16[1,24,640]{2,1,0:T(8,128)(2,1)S(1)}, bf16[1,24,640]{2,1,0:T(8,128)(2,1)}, u32[]{:S(2)}) copy-start(bf16[1,24,640]{2,1,0:T(8,128)(2,1)} %get-tuple-element.35) | copy-start | bytes 92164
  2.3 6.5 %collective-permute-start.6 = (bf16[1,24,640]{2,1,0:T(8,128)(2,1)}, bf16[1,24,640]{2,1,0:T(8,128)(2,1)S(1)}, u32[]{:S(2)}, u32[]{:S(2)}) collective-permute-start(bf16[1,24,640]{2,1,0:T(8,128)(2,1)} %get-tuple-element.35), channel_id=1, source_target_pairs={{0,16},{2,18},{4,20},{6,22},{8,24},{10,26},{12,28},{14,30},{16,0},... | collective-permute-start | bytes 92168 | tf_op jit(solution)/shard_map/ppermute | solution.py:42
  6.3 7.2 %collective-permute-start = (bf16[1,24,1792]{2,1,0:T(8,128)(2,1)}, bf16[1,24,1792]{2,1,0:T(8,128)(2,1)S(1)}, u32[]{:S(2)}, u32[]{:S(2)}) collective-permute-start(bf16[1,24,1792]{2,1,0:T(8,128)(2,1)} %get-tuple-element.34), channel_id=1, source_target_pairs={{0,16},{2,18},{4,20},{6,22},{8,24},{10,26},{12,28},{14,30},{16,0},... | collective-permute-start | bytes 258056 | tf_op jit(solution)/shard_map/ppermute | solution.py:42
  9.6 12.8 %collective-permute-start.7 = (bf16[2,24,640]{2,1,0:T(8,128)(2,1)S(1)}, bf16[2,24,640]{2,1,0:T(8,128)(2,1)S(1)}, u32[]{:S(2)}, u32[]{:S(2)}) collective-permute-start(bf16[2,24,640]{2,1,0:T(8,128)(2,1)S(1)} %pad_maximum_fusion.4), channel_id=1, source_target_pairs={{0,8},{2,10},{4,12},{6,14},{8,0},{10,2},{12,4},{14,6},{16,24},{18,... | collective-permute-start | bytes 184328 | tf_op jit(solution)/shard_map/ppermute | solution.py:42
  14.4 32.3 %copy-start = (bf16[1576,384]{1,0:T(8,128)(2,1)S(1)}, bf16[1576,384]{1,0:T(8,128)(2,1)}, u32[]{:S(2)}) copy-start(bf16[1576,384]{1,0:T(8,128)(2,1)} %param.8) | copy-start | bytes 3631108
  14.5 5.5 %collective-permute-start.1 = (bf16[2,24,1792]{2,1,0:T(8,128)(2,1)S(1)}, bf16[2,24,1792]{2,1,0:T(8,128)(2,1)S(1)}, u32[]{:S(2)}, u32[]{:S(2)}) collective-permute-start(bf16[2,24,1792]{2,1,0:T(8,128)(2,1)S(1)} %pad_maximum_fusion.1), channel_id=1, source_target_pairs={{0,8},{2,10},{4,12},{6,14},{8,0},{10,2},{12,4},{14,6},{16,24},{18,... | collective-permute-start | bytes 516104 | tf_op jit(solution)/shard_map/ppermute | solution.py:42
  20.9 8.2 %collective-permute-start.2 = (bf16[4,24,1792]{2,1,0:T(8,128)(2,1)S(1)}, bf16[4,24,1792]{2,1,0:T(8,128)(2,1)S(1)}, u32[]{:S(2)}, u32[]{:S(2)}) collective-permute-start(bf16[4,24,1792]{2,1,0:T(8,128)(2,1)S(1)} %pad_maximum_fusion), channel_id=1, source_target_pairs={{0,4},{2,6},{4,0},{6,2},{8,12},{10,14},{12,8},{14,10},{16,20},{18,... | collective-permute-start | bytes 1032200 | tf_op jit(solution)/shard_map/ppermute | solution.py:42
  22.4 8.3 %collective-permute-start.8 = (bf16[4,24,640]{2,1,0:T(8,128)(2,1)S(1)}, bf16[4,24,640]{2,1,0:T(8,128)(2,1)S(1)}, u32[]{:S(2)}, u32[]{:S(2)}) collective-permute-start(bf16[4,24,640]{2,1,0:T(8,128)(2,1)S(1)} %pad_maximum_fusion.3), channel_id=1, source_target_pairs={{0,4},{2,6},{4,0},{6,2},{8,12},{10,14},{12,8},{14,10},{16,20},{18,... | collective-permute-start | bytes 368648 | tf_op jit(solution)/shard_map/ppermute | solution.py:42
  29.1 22.0 %copy-start.7 = (bf16[8,24,1792]{2,1,0:T(8,128)(2,1)}, bf16[8,24,1792]{2,1,0:T(8,128)(2,1)S(1)}, u32[]{:S(2)}) copy-start(bf16[8,24,1792]{2,1,0:T(8,128)(2,1)S(1)} %constant_dynamic-update-slice_fusion.p0) | copy-start | bytes 2064388
  29.1 22.5 %collective-permute-start.3 = (bf16[8,24,1792]{2,1,0:T(8,128)(2,1)S(1)}, bf16[8,24,1792]{2,1,0:T(8,128)(2,1)}, u32[]{:S(2)}, u32[]{:S(2)}) collective-permute-start(bf16[8,24,1792]{2,1,0:T(8,128)(2,1)S(1)} %constant_dynamic-update-slice_fusion.p0), channel_id=1, source_target_pairs={{0,1},{1,0},{2,3},{3,2},{4,5},{5,4},{6,7},{7,6},{8,9},{9,8},{10,11... | collective-permute-start | bytes 2064392 | tf_op jit(solution)/shard_map/ppermute | solution.py:42
  30.7 18.0 %copy-start.8 = (bf16[8,24,640]{2,1,0:T(8,128)(2,1)}, bf16[8,24,640]{2,1,0:T(8,128)(2,1)S(1)}, u32[]{:S(2)}) copy-start(bf16[8,24,640]{2,1,0:T(8,128)(2,1)S(1)} %constant_dynamic-update-slice_fusion.4.p0) | copy-start | bytes 737284
  30.7 16.0 %collective-permute-start.9 = (bf16[8,24,640]{2,1,0:T(8,128)(2,1)S(1)}, bf16[8,24,640]{2,1,0:T(8,128)(2,1)}, u32[]{:S(2)}, u32[]{:S(2)}) collective-permute-start(bf16[8,24,640]{2,1,0:T(8,128)(2,1)S(1)} %constant_dynamic-update-slice_fusion.4.p0), channel_id=1, source_target_pairs={{0,1},{1,0},{2,3},{3,2},{4,5},{5,4},{6,7},{7,6},{8,9},{9,8},{10,11... | collective-permute-start | bytes 737288 | tf_op jit(solution)/shard_map/ppermute | solution.py:42
  32.0 19.7 %collective-permute-start.10 = (bf16[8,24,640]{2,1,0:T(8,128)(2,1)S(1)}, bf16[8,24,640]{2,1,0:T(8,128)(2,1)}, u32[]{:S(2)}, u32[]{:S(2)}) collective-permute-start(bf16[8,24,640]{2,1,0:T(8,128)(2,1)S(1)} %constant_dynamic-update-slice_fusion.4.p0), channel_id=1, source_target_pairs={{0,2},{2,0},{4,6},{6,4},{8,10},{10,8},{12,14},{14,12},{16,18},{18,... | collective-permute-start | bytes 737288 | tf_op jit(solution)/shard_map/ppermute | solution.py:42
  46.7 5.0 %collective-permute-start.11 = (bf16[8,24,640]{2,1,0:T(8,128)(2,1)}, bf16[8,24,640]{2,1,0:T(8,128)(2,1)}, u32[]{:S(2)}, u32[]{:S(2)}) collective-permute-start(bf16[8,24,640]{2,1,0:T(8,128)(2,1)} %collective-permute-done.9.p1), channel_id=1, source_target_pairs={{0,2},{2,0},{4,6},{6,4},{8,10},{10,8},{12,14},{14,12},{16,18},{18,... | collective-permute-start | bytes 737288 | tf_op jit(solution)/shard_map/ppermute | solution.py:42
  51.1 16.9 %collective-permute-start.4 = (bf16[8,24,1792]{2,1,0:T(8,128)(2,1)S(1)}, bf16[8,24,1792]{2,1,0:T(8,128)(2,1)S(1)}, u32[]{:S(2)}, u32[]{:S(2)}) collective-permute-start(bf16[8,24,1792]{2,1,0:T(8,128)(2,1)S(1)} %constant_dynamic-update-slice_fusion.p0), channel_id=1, source_target_pairs={{0,2},{2,0},{4,6},{6,4},{8,10},{10,8},{12,14},{14,12},{16,18},{18,... | collective-permute-start | bytes 2064392 | tf_op jit(solution)/shard_map/ppermute | solution.py:42
  51.6 16.4 %collective-permute-start.5 = (bf16[8,24,1792]{2,1,0:T(8,128)(2,1)}, bf16[8,24,1792]{2,1,0:T(8,128)(2,1)S(1)}, u32[]{:S(2)}, u32[]{:S(2)}) collective-permute-start(bf16[8,24,1792]{2,1,0:T(8,128)(2,1)} %collective-permute-done.3.p1), channel_id=1, source_target_pairs={{0,2},{2,0},{4,6},{6,4},{8,10},{10,8},{12,14},{14,12},{16,18},{18,... | collective-permute-start | bytes 2064392 | tf_op jit(solution)/shard_map/ppermute | solution.py:42
  112.1 11.4 %copy-start.12 = (bf16[16,24,768]{2,1,0:T(8,128)(2,1)S(1)}, bf16[16,24,768]{2,1,0:T(8,128)(2,1)}, u32[]{:S(2)}) copy-start(bf16[16,24,768]{2,1,0:T(8,128)(2,1)} %get-tuple-element.55) | copy-start | bytes 1769476
  112.1 11.4 %copy-start.9 = (bf16[16,24,1024]{2,1,0:T(8,128)(2,1)S(1)}, bf16[16,24,1024]{2,1,0:T(8,128)(2,1)}, u32[]{:S(2)}) copy-start(bf16[16,24,1024]{2,1,0:T(8,128)(2,1)} %get-tuple-element.53) | copy-start | bytes 2359300
  123.0 9.7 %collective-permute-start.12 = (bf16[16,24,640]{2,1,0:T(8,128)(2,1)}, bf16[16,24,640]{2,1,0:T(8,128)(2,1)S(1)}, u32[]{:S(2)}, u32[]{:S(2)}) collective-permute-start(bf16[16,24,640]{2,1,0:T(8,128)(2,1)} %get-tuple-element.49), channel_id=1, source_target_pairs={{0,2},{2,0},{4,6},{6,4},{8,10},{10,8},{12,14},{14,12},{16,18},{18,... | collective-permute-start | bytes 1474568 | tf_op jit(solution)/shard_map/ppermute | solution.py:42
  123.4 11.0 %collective-permute-start.20 = (bf16[16,24,768]{2,1,0:T(8,128)(2,1)S(1)}, bf16[16,24,768]{2,1,0:T(8,128)(2,1)S(1)}, u32[]{:S(2)}, u32[]{:S(2)}) collective-permute-start(bf16[16,24,768]{2,1,0:T(8,128)(2,1)S(1)} %copy-done.12), channel_id=1, source_target_pairs={{0,2},{2,0},{4,6},{6,4},{8,10},{10,8},{12,14},{14,12},{16,18},{18,... | collective-permute-start | bytes 1769480 | tf_op jit(solution)/shard_map/ppermute | solution.py:42
  123.5 19.0 %collective-permute-start.17 = (bf16[16,24,1024]{2,1,0:T(8,128)(2,1)S(1)}, bf16[16,24,1024]{2,1,0:T(8,128)(2,1)S(1)}, u32[]{:S(2)}, u32[]{:S(2)}) collective-permute-start(bf16[16,24,1024]{2,1,0:T(8,128)(2,1)S(1)} %copy-done.9), channel_id=1, source_target_pairs={{0,2},{2,0},{4,6},{6,4},{8,10},{10,8},{12,14},{14,12},{16,18},{18,... | collective-permute-start | bytes 2359304 | tf_op jit(solution)/shard_map/ppermute | solution.py:42
  123.9 8.7 %copy-start.3 = (bf16[16,24,640]{2,1,0:T(8,128)(2,1)S(1)}, bf16[16,24,640]{2,1,0:T(8,128)(2,1)}, u32[]{:S(2)}) copy-start(bf16[16,24,640]{2,1,0:T(8,128)(2,1)} %get-tuple-element.48) | copy-start | bytes 1474564
  132.8 8.0 %collective-permute-start.13 = (bf16[8,24,640]{2,1,0:T(8,128)(2,1)S(1)}, bf16[8,24,640]{2,1,0:T(8,128)(2,1)S(1)}, u32[]{:S(2)}, u32[]{:S(2)}) collective-permute-start(bf16[8,24,640]{2,1,0:T(8,128)(2,1)S(1)} %slice.89), channel_id=1, source_target_pairs={{0,1},{1,0},{2,3},{3,2},{4,5},{5,4},{6,7},{7,6},{8,9},{9,8},{10,11... | collective-permute-start | bytes 737288 | tf_op jit(solution)/shard_map/ppermute | solution.py:42
  134.6 15.4 %collective-permute-start.21 = (bf16[8,24,768]{2,1,0:T(8,128)(2,1)S(1)}, bf16[8,24,768]{2,1,0:T(8,128)(2,1)S(1)}, u32[]{:S(2)}, u32[]{:S(2)}) collective-permute-start(bf16[8,24,768]{2,1,0:T(8,128)(2,1)S(1)} %slice.102), channel_id=1, source_target_pairs={{0,4},{2,6},{4,0},{6,2},{8,12},{10,14},{12,8},{14,10},{16,20},{18,... | collective-permute-start | bytes 884744 | tf_op jit(solution)/shard_map/ppermute | solution.py:42
  140.9 5.1 %collective-permute-start.14 = (bf16[4,24,640]{2,1,0:T(8,128)(2,1)S(1)}, bf16[4,24,640]{2,1,0:T(8,128)(2,1)S(1)}, u32[]{:S(2)}, u32[]{:S(2)}) collective-permute-start(bf16[4,24,640]{2,1,0:T(8,128)(2,1)S(1)} %slice.91), channel_id=1, source_target_pairs={{0,4},{2,6},{4,0},{6,2},{8,12},{10,14},{12,8},{14,10},{16,20},{18,... | collective-permute-start | bytes 368648 | tf_op jit(solution)/shard_map/ppermute | solution.py:42
  142.8 13.2 %collective-permute-start.18 = (bf16[8,24,1024]{2,1,0:T(8,128)(2,1)S(1)}, bf16[8,24,1024]{2,1,0:T(8,128)(2,1)S(1)}, u32[]{:S(2)}, u32[]{:S(2)}) collective-permute-start(bf16[8,24,1024]{2,1,0:T(8,128)(2,1)S(1)} %slice.97), channel_id=1, source_target_pairs={{0,1},{1,0},{2,3},{3,2},{4,5},{5,4},{6,7},{7,6},{8,9},{9,8},{10,11... | collective-permute-start | bytes 1179656 | tf_op jit(solution)/shard_map/ppermute | solution.py:42
  146.0 6.2 %collective-permute-start.15 = (bf16[2,24,640]{2,1,0:T(8,128)(2,1)S(1)}, bf16[2,24,640]{2,1,0:T(8,128)(2,1)S(1)}, u32[]{:S(2)}, u32[]{:S(2)}) collective-permute-start(bf16[2,24,640]{2,1,0:T(8,128)(2,1)S(1)} %slice.93), channel_id=1, source_target_pairs={{0,8},{2,10},{4,12},{6,14},{8,0},{10,2},{12,4},{14,6},{16,24},{18,... | collective-permute-start | bytes 184328 | tf_op jit(solution)/shard_map/ppermute | solution.py:42
  150.1 5.9 %collective-permute-start.22 = (bf16[4,24,768]{2,1,0:T(8,128)(2,1)S(1)}, bf16[4,24,768]{2,1,0:T(8,128)(2,1)S(1)}, u32[]{:S(2)}, u32[]{:S(2)}) collective-permute-start(bf16[4,24,768]{2,1,0:T(8,128)(2,1)S(1)} %slice.104), channel_id=1, source_target_pairs={{0,1},{1,0},{2,3},{3,2},{4,5},{5,4},{6,7},{7,6},{8,9},{9,8},{10,11... | collective-permute-start | bytes 442376 | tf_op jit(solution)/shard_map/ppermute | solution.py:42
  156.2 5.7 %collective-permute-start.19 = (bf16[4,24,1024]{2,1,0:T(8,128)(2,1)S(1)}, bf16[4,24,1024]{2,1,0:T(8,128)(2,1)S(1)}, u32[]{:S(2)}, u32[]{:S(2)}) collective-permute-start(bf16[4,24,1024]{2,1,0:T(8,128)(2,1)S(1)} %slice.99), channel_id=1, source_target_pairs={{0,4},{2,6},{4,0},{6,2},{8,12},{10,14},{12,8},{14,10},{16,20},{18,... | collective-permute-start | bytes 589832 | tf_op jit(solution)/shard_map/ppermute | solution.py:42
  162.1 8.8 %collective-permute-start.23 = (bf16[2,24,1792]{2,1,0:T(8,128)(2,1)S(1)}, bf16[2,24,1792]{2,1,0:T(8,128)(2,1)S(1)}, u32[]{:S(2)}, u32[]{:S(2)}) collective-permute-start(bf16[2,24,1792]{2,1,0:T(8,128)(2,1)S(1)} %pad_maximum_fusion.2), channel_id=1, source_target_pairs={{0,8},{2,10},{4,12},{6,14},{8,0},{10,2},{12,4},{14,6},{16,24},{18,... | collective-permute-start | bytes 516104 | tf_op jit(solution)/shard_map/ppermute | solution.py:42
  166.7 15.7 %collective-permute-start.16 = (bf16[1,24,640]{2,1,0:T(8,128)(2,1)S(1)}, bf16[1,24,640]{2,1,0:T(8,128)(2,1)S(1)}, u32[]{:S(2)}, u32[]{:S(2)}) collective-permute-start(bf16[1,24,640]{2,1,0:T(8,128)(2,1)S(1)} %get-tuple-element.66), channel_id=1, source_target_pairs={{0,16},{2,18},{4,20},{6,22},{8,24},{10,26},{12,28},{14,30},{16,0},... | collective-permute-start | bytes 92168 | tf_op jit(solution)/shard_map/ppermute | solution.py:42
  171.6 12.8 %collective-permute-start.24 = (bf16[1,24,1792]{2,1,0:T(8,128)(2,1)S(1)}, bf16[1,24,1792]{2,1,0:T(8,128)(2,1)S(1)}, u32[]{:S(2)}, u32[]{:S(2)}) collective-permute-start(bf16[1,24,1792]{2,1,0:T(8,128)(2,1)S(1)} %get-tuple-element.62), channel_id=1, source_target_pairs={{0,16},{2,18},{4,20},{6,22},{8,24},{10,26},{12,28},{14,30},{16,0},... | collective-permute-start | bytes 258056 | tf_op jit(solution)/shard_map/ppermute | solution.py:42
  (6 other events, 13.0 us)

commit v3 on v2

--- a/solution.py
+++ b/solution.py
@@ -11,6 +11,7 @@
 SEQ = 197
 PAD = 208
 PER = 2
+CUT = 192
 D = 384
 QC = 640
 F32 = jnp.float32
@@ -121,6 +122,10 @@
 def pick(value, low, side):
     zero = jnp.zeros_like(value)
     return jnp.where(low, value, zero) if side == 0 else jnp.where(low, zero, value)
+
+
+def lanes(kind, c):
+    return slice((3 * c + kind) * 128, (3 * c + kind) * 128 + 128)
 
 
 def tall(ref):
@@ -160,43 +165,56 @@
     @pl.when(pl.program_id(0) == 0)
     def _():
         unpack(places, rows, (p0, p1, p2, p3), scr)
-        for c in range(3):
-            at = c * D
-            w_ref[:, at : at + 128] = scr[0, :, c * 128 : c * 128 + 128].astype(BF16)
-            w_ref[:, at + 128 : at + 256] = scr[1, :, c * 128 : c * 128 + 128].astype(BF16)
-            one = 384 + c * HD
-            last = jnp.concatenate([scr[0, :, one : one + HD], scr[1, :, one : one + HD]], axis=1)
-            w_ref[:, at + 256 : at + 384] = last.astype(BF16)
+        for t in range(2):
+            w_ref[:, t * D : t * D + D] = scr[t, :, 0:D].astype(BF16)
+        for kind in range(3):
+            one = slice(D + kind * HD, D + kind * HD + HD)
+            last = jnp.concatenate([scr[0, :, one], scr[1, :, one]], axis=1)
+            w_ref[:, lanes(kind, 2)] = last.astype(BF16)
         turned = scr[0, :, 512:640].T
         gain_ref[...] = turned[HD : HD + 8, :]
 
     xhat, _ = normalize(tall(x_ref).astype(F32))
     n1 = (xhat * gain_ref[0:1, :]).astype(BF16)
     n1_ref[...] = n1.reshape(PER, PAD, D)
-    proj = dot(n1, w_ref[...])
     low = low_lanes()
-    key_ok = lax.broadcasted_iota(jnp.int32, (PAD, PAD), 0) < SEQ
-    for i in range(PER):
-        mine = slice(i * PAD, i * PAD + PAD)
-        for c in range(3):
-            at = slice(c * 128, c * 128 + 128)
-            q = (proj[mine, at] * (HD**-0.5)).astype(BF16)
-            k = proj[mine, D + c * 128 : D + c * 128 + 128].astype(BF16)
-            v = proj[mine, 2 * D + c * 128 : 2 * D + c * 128 + 128].astype(BF16)
-            qkv_ref[i, :, at] = q
-            qkv_ref[i, :, D + c * 128 : D + c * 128 + 128] = k
-            qkv_ref[i, :, 2 * D + c * 128 : 2 * D + c * 128 + 128] = v
-            v_turned = v.T
-            parts = []
-            for side in range(2):
-                scores = dot(pick(k, low, side), q, NT)
-                scores = jnp.where(key_ok, scores, -1e30)
-                expon = jnp.exp(scores - jnp.max(scores, axis=0, keepdims=True))
-                probs = expon * (1.0 / jnp.sum(expon, axis=0, keepdims=True))
-                probs = probs.astype(BF16)
-                probs_ref[i, 2 * c + side] = probs
-                parts.append(dot(v_turned[side * HD : side * HD + HD, :], probs))
-            heads_ref[i, :, at] = jnp.concatenate(parts, axis=0).T.astype(BF16)
+    tail_ok = lax.broadcasted_iota(jnp.int32, (PAD - CUT, PAD), 0) < SEQ - CUT
+
+    def project(c):
+        for b in {0: (0, 1), 1: (2,), 2: (3, 4)}[c]:
+            at = slice(b * 256, min(b * 256 + 256, 3 * D))
+            value = dot(n1, w_ref[:, at])
+            for piece in range((at.stop - at.start) // 128):
+                kind = (b * 2 + piece) % 3
+                here = value[:, piece * 128 : piece * 128 + 128]
+                if kind == 0:
+                    here = here * (HD**-0.5)
+                span = slice(at.start + piece * 128, at.start + piece * 128 + 128)
+                qkv_ref[:, :, span] = here.astype(BF16).reshape(PER, PAD, 128)
+
+    def enter(i, c):
+        q, k, v = (qkv_ref[i, :, lanes(kind, c)] for kind in range(3))
+        return [dot(pick(k, low, side), q, NT) for side in range(2)], v.T
+
+    units = [(i, c) for c in range(3) for i in range(PER)]
+    project(0)
+    ahead = enter(*units[0])
+    for j, (i, c) in enumerate(units):
+        all_scores, v_turned = ahead
+        if j + 1 < len(units):
+            if i == 0 and c < 2:
+                project(c + 1)
+            ahead = enter(*units[j + 1])
+        parts = []
+        for side in range(2):
+            scores = all_scores[side]
+            scores = jnp.concatenate([scores[:CUT], jnp.where(tail_ok, scores[CUT:], -1e30)], axis=0)
+            expon = jnp.exp(scores - jnp.max(scores, axis=0, keepdims=True))
+            probs = expon * (1.0 / jnp.sum(expon, axis=0, keepdims=True))
+            probs = probs.astype(BF16)
+            probs_ref[i, 2 * c + side] = probs
+            parts.append(dot(v_turned[side * HD : side * HD + HD, :], probs))
+        heads_ref[i, :, c * 128 : c * 128 + 128] = jnp.concatenate(parts, axis=0).T.astype(BF16)
 
 
 def mlp_kernel(
@@ -233,19 +251,25 @@
         xhat, rstd = normalize(middle)
         n2 = (xhat * gain).astype(BF16)
         n2_all[at, :] = n2
-        width = fs // 2
+        width = 256
         back = None
-        for c in range(4):
+        count = 2 * fs // width
+        ahead = dot(n2, w_fc1[:, :width]), dot(og, fc2_ref[:, :width])
+        for c in range(count):
             cols = slice(c * width, c * width + width)
-            u = dot(n2, w_fc1[:, cols])
+            u, dh = ahead
+            if c + 1 < count:
+                after = slice(c * width + width, c * width + 2 * width)
+                ahead = dot(n2, w_fc1[:, after]), dot(og, fc2_ref[:, after])
             square = u * u
             bent = jnp.tanh(u * (GELU_C + (GELU_C * 0.044715) * square))
             plus = 0.5 + 0.5 * bent
-            hid = (u * plus).astype(BF16)
+            full = u * plus
+            hid = full.astype(BF16)
             hid_ref[:, :, cols] = hid.reshape(PER, PAD, width)
             hid_all[at, cols] = hid
-            slope = plus * (1.0 + u * (1.0 - bent) * (GELU_C + (GELU_C * 0.134145) * square))
-            pg = (dot(og, fc2_ref[:, cols]) * slope).astype(BF16)
+            slope = plus + full * (1.0 - plus) * ((2.0 * GELU_C) + (GELU_C * 0.26829) * square)
+            pg = (dh * slope).astype(BF16)
             pg_all[at, cols] = pg
             part = dot(pg, w_fc1_turned[cols, :])
             back = part if back is None else back + part
@@ -283,33 +307,38 @@
 
 def attend_back(qkv_ref, probs_ref, hg_ref, grad_ref, grad_all, at):
     low = low_lanes()
-    for i in range(PER):
-        for c in range(3):
-            cols = slice(c * 128, c * 128 + 128)
-            kcols = slice(D + c * 128, D + c * 128 + 128)
-            vcols = slice(2 * D + c * 128, 2 * D + c * 128 + 128)
-            q, k, v = qkv_ref[i, :, cols], qkv_ref[i, :, kcols], qkv_ref[i, :, vcols]
-            do = hg_ref[i, :, cols]
-            k_turned = k.T
-            dq, dk, dv = [], [], []
-            for side in range(2):
-                probs_low = probs_ref[i, 2 * c + side]
-                probs = probs_low.astype(F32)
-                dp = dot(pick(v, low, side), do, NT)
-                ds = probs * (dp - jnp.sum(probs * dp, axis=0, keepdims=True))
-                ds = ds.astype(BF16)
-                dv.append(dot(probs_low, do))
-                dk.append(dot(ds, q))
-                dq.append(dot(k_turned[side * HD : side * HD + HD, :], ds))
-            for span, value in (
-                (cols, jnp.concatenate(dq, axis=0).T * (HD**-0.5)),
-                (kcols, jnp.where(low, dk[0], dk[1])),
-                (vcols, jnp.where(low, dv[0], dv[1])),
-            ):
-                value = value.astype(BF16)
-                grad_ref[i, :, span] = value
-                if grad_all is not None:
-                    grad_all[pl.ds(pl.multiple_of(at + i * PAD, PAD), PAD), span] = value
+    units = [(i, c) for i in range(PER) for c in range(3)]
+
+    def enter(i, c):
+        v, do = qkv_ref[i, :, lanes(2, c)], hg_ref[i, :, c * 128 : c * 128 + 128]
+        return [dot(pick(v, low, side), do, NT) for side in range(2)]
+
+    ahead = enter(*units[0])
+    for j, (i, c) in enumerate(units):
+        grads = ahead
+        if j + 1 < len(units):
+            ahead = enter(*units[j + 1])
+        low_probs = [probs_ref[i, 2 * c + side] for side in range(2)]
+        ds = []
+        for side in range(2):
+            probs = low_probs[side].astype(F32)
+            weighted = probs * grads[side]
+            ds.append((weighted - probs * jnp.sum(weighted, axis=0, keepdims=True)).astype(BF16))
+        q, k = qkv_ref[i, :, lanes(0, c)], qkv_ref[i, :, lanes(1, c)]
+        do = hg_ref[i, :, c * 128 : c * 128 + 128]
+        k_turned = k.T
+        dv = [dot(p, do) for p in low_probs]
+        dk = [dot(d, q) for d in ds]
+        dq = [dot(k_turned[side * HD : side * HD + HD, :], ds[side]) for side in range(2)]
+        for kind, value in (
+            (0, jnp.concatenate(dq, axis=0).T * (HD**-0.5)),
+            (1, jnp.where(low, dk[0], dk[1])),
+            (2, jnp.where(low, dv[0], dv[1])),
+        ):
+            value = value.astype(BF16)
+            grad_ref[i, :, lanes(kind, c)] = value
+            if grad_all is not None:
+                grad_all[pl.ds(pl.multiple_of(at + i * PAD, PAD), PAD), lanes(kind, c)] = value
 
 
 def attend_back_kernel(qkv_ref, probs_ref, hg_ref, grad_ref):
@@ -339,19 +368,24 @@
     def _():
         turned = n1_ref[...].reshape(-1, D).T
         row_sum = jnp.zeros((D, 1), F32)
-        singles = []
-        for c in range(3):
-            span = slice(c * D, c * D + D)
+        singles = [None] * 3
+        for b in (8, 6, 0, 2, 4):
+            blocks_here = range(b, min(b + 2, 9))
+            span = slice(b * 128, blocks_here.stop * 128)
             grad = dot(turned, grad_all[:, span])
             row_sum += jnp.sum(grad * w_ref[:, span].astype(F32), axis=1, keepdims=True)
-            scr[0, :, c * 128 : c * 128 + 128] = grad[:, 0:128]
-            scr[1, :, c * 128 : c * 128 + 128] = grad[:, 128:256]
-            singles.append(grad[:, 256:384])
-        gain = jnp.broadcast_to(row_sum, (D, HD))
-        for t in range(2):
-            own = [s[:, t * HD : t * HD + HD] for s in singles]
-            scr[t, :, 384:512] = jnp.concatenate(own[:2], axis=1)
-            scr[t, :, 512:640] = jnp.concatenate([own[2], gain], axis=1)
+            for at in blocks_here:
+                here = grad[:, (at - b) * 128 : (at - b) * 128 + 128]
+                if at < 6:
+                    scr[at // 3, :, at % 3 * 128 : at % 3 * 128 + 128] = here
+                else:
+                    singles[at - 6] = here
+            if b == 6:
+                for t in range(2):
+                    own = [s[:, t * HD : t * HD + HD] for s in singles]
+                    scr[t, :, 384:512] = jnp.concatenate(own[:2], axis=1)
+                    scr[t, :, 512 : 512 + HD] = own[2]
+        scr[:, :, 512 + HD : 640] = jnp.broadcast_to(row_sum[None], (2, D, HD))
         repack(places, rows, scr, (keep, send))
 
 

time: 187 us -> 174 us (0.930)
  Pallas kernels: 91.3 us -> 77.7 us
    pallas_call x10, Pallas kernels: 91.3 us -> 77.7 us  [call(): pl.pallas_call(kernel, grid=(grid,) if grid else (), in_specs=ins, out_sp...]
where the time goes in v3:
time: 174 us; the launch traced here: 173 us
  Pallas kernels  77.7 us (45%)
  waiting for transfers between devices  43.9 us (25%)
  starting transfers between devices  37 us (21%)
  local copies, waits for them, and re-layouts  9.9 us (6%)
  other arithmetic  3.63 us (2%)
    pallas_call x10, Pallas kernels, call(): pl.pallas_call(kernel, grid=(grid,) if grid else (), in_specs=ins, out_sp...  77.7 us
    ppermute x25, waiting for transfers between devices, swap(): return lax.ppermute(value, axis, [(i, i ^ bit) for i in range(sizes[axis])])  43.9 us
    ppermute x25, starting transfers between devices, swap(): return lax.ppermute(value, axis, [(i, i ^ bit) for i in range(sizes[axis])])  37 us
    unnamed x32, local copies, waits for them, and re-layouts  4.06 us
  transfers between devices with their start and end apart: 25, of which 10 were waited for; matrix products, arithmetic and copies ran while one was open for 6% of the time, Pallas kernels for 18%

profile of v3, /device:TPU:0, one launch (start us, length us, event | category | flops | bytes accessed | tf_op | source)
XLA Modules:
  0.0 173.1 jit_solution(6095984975465416897)
XLA Ops:
  0.6 1.6 shard_map.143
  2.3 4.1 %collective-permute-start.6 = (bf16[1,24,640]{2,1,0:T(8,128)(2,1)}, bf16[1,24,640]{2,1,0:T(8,128)(2,1)S(1)}, u32[]{:S(2)}, u32[]{:S(2)}) collective-permute-start(bf16[1,24,640]{2,1,0:T(8,128)(2,1)} %get-tuple-element.35), channel_id=1, source_target_pairs={{0,16},{2,18},{4,20},{6,22},{8,24},{10,26},{12,28},{14,30},{16,0},... | collective-permute-start | bytes 92168 | tf_op jit(solution)/shard_map/ppermute | solution.py:43
  9.6 2.4 %collective-permute-start.7 = (bf16[2,24,640]{2,1,0:T(8,128)(2,1)S(1)}, bf16[2,24,640]{2,1,0:T(8,128)(2,1)S(1)}, u32[]{:S(2)}, u32[]{:S(2)}) collective-permute-start(bf16[2,24,640]{2,1,0:T(8,128)(2,1)S(1)} %pad_maximum_fusion.4), channel_id=1, source_target_pairs={{0,8},{2,10},{4,12},{6,14},{8,0},{10,2},{12,4},{14,6},{16,24},{18,... | collective-permute-start | bytes 184328 | tf_op jit(solution)/shard_map/ppermute | solution.py:43
  12.0 1.6 collective-permute-done
  14.6 5.4 %collective-permute-done.1 = bf16[2,24,1792]{2,1,0:T(8,128)(2,1)S(1)} collective-permute-done((bf16[2,24,1792]{2,1,0:T(8,128)(2,1)S(1)}, bf16[2,24,1792]{2,1,0:T(8,128)(2,1)S(1)}, u32[]{:S(2)}, u32[]{:S(2)}) %collective-permute-start.1) | collective-permute-done | bytes 172064 | tf_op jit(solution)/shard_map/ppermute | solution.py:43
  20.9 1.6 collective-permute-start.2
  23.1 6.0 %collective-permute-done.2 = bf16[4,24,1792]{2,1,0:T(8,128)(2,1)S(1)} collective-permute-done((bf16[4,24,1792]{2,1,0:T(8,128)(2,1)S(1)}, bf16[4,24,1792]{2,1,0:T(8,128)(2,1)S(1)}, u32[]{:S(2)}, u32[]{:S(2)}) %collective-permute-start.2) | collective-permute-done | bytes 344096 | tf_op jit(solution)/shard_map/ppermute | solution.py:43
  29.1 1.6 collective-permute-start.3
  32.0 14.7 %collective-permute-done.9.p1 = bf16[8,24,640]{2,1,0:T(8,128)(2,1)} collective-permute-done((bf16[8,24,640]{2,1,0:T(8,128)(2,1)S(1)}, bf16[8,24,640]{2,1,0:T(8,128)(2,1)}, u32[]{:S(2)}, u32[]{:S(2)}) %collective-permute-start.9) | collective-permute-done | bytes 245792 | tf_op jit(solution)/shard_map/ppermute | solution.py:43
  47.1 1.6 reshape.37
  51.7 12.5 %shard_map.144 = (bf16[8,208,1152]{2,1,0:T(8,128)(2,1)}, bf16[8,6,208,208]{3,2,1,0:T(8,128)(2,1)}, bf16[8,208,384]{2,1,0:T(8,128)(2,1)}, bf16[8,208,384]{2,1,0:T...) custom-call(bf16[8,24,640]{2,1,0:T(8,128)(2,1)} %copy-done.8, bf16[8,24,640]{2,1,0:T(8,128)(2,1)} %collective-permute-done.9.p1, ...), custom_call_target="tpu_custom_call" | custom-call | flops 8000000000 | bytes 20000000 | tf_op jit(solution)/shard_map/pallas_call | solution.py:468
  65.3 24.6 %shard_map.145 = (f32[8,208,384]{2,1,0:T(8,128)}, bf16[8,208,1536]{2,1,0:T(8,128)(2,1)}, f32[8,208,384]{2,1,0:T(8,128)}, bf16[8,208,384]{2,1,0:T(8,128)(2,1)}, b...) custom-call(bf16[8,24,1792]{2,1,0:T(8,128)(2,1)} %copy-done.7, ...), custom_call_target="tpu_custom_call" | custom-call | flops 14000000000 | bytes 30000000 | tf_op jit(solution)/shard_map/pallas_call | solution.py:468
  89.9 4.4 %shard_map.147.refs_0_ = bf16[2,208,1152]{2,1,0:T(8,128)(2,1)} custom-call(bf16[8,208,1152]{2,1,0:T(8,128)(2,1)} %get-tuple-element.41.qkv_ref, bf16[8,6,208,208]{3,2,1,0:T(8,128)(2,1)} %get-tuple-element.42.probs_ref, bf16[8,208,384]{2,1,0:T(8,128)(2,1)} %get-tuple-element.43.hg_ref), custom_call_target="tpu_custom_call" | custom-call | flops 1800000000 | bytes 4000000 | tf_op jit(solution)/shard_map/pallas_call | solution.py:468
  94.3 6.2 %shard_map.148.refs_1_ = bf16[4,208,1152]{2,1,0:T(8,128)(2,1)} custom-call(bf16[8,208,1152]{2,1,0:T(8,128)(2,1)} %get-tuple-element.41.qkv_ref, bf16[8,6,208,208]{3,2,1,0:T(8,128)(2,1)} %get-tuple-element.42.probs_ref, bf16[8,208,384]{2,1,0:T(8,128)(2,1)} %get-tuple-element.43.hg_ref), custom_call_target="tpu_custom_call" | custom-call | flops 3600000000 | bytes 8000000 | tf_op jit(solution)/shard_map/pallas_call | solution.py:468
  100.5 8.9 %shard_map.149 = (bf16[2,208,1152]{2,1,0:T(8,128)(2,1)}, bf16[16,24,640]{2,1,0:T(8,128)(2,1)}, bf16[16,24,640]{2,1,0:T(8,128)(2,1)}) custom-call(bf16[8,208,1152]{2,1,0:T(8,128)(2,1)} %get-tuple-element.41.qkv_ref, bf16[8,6,208,208]{3,2,1,0:T(8,128)(2,1)} %get-tuple-element.42.probs_ref, bf16[8,208,384]{2,1,0:T(8,128)(2,1)} %get-tuple-element.43.hg_ref, ...), custom_call_target="tpu_custom_call" | custom-call | flops 3500000000 | bytes 8000000 | tf_op jit(solution)/shard_map/pallas_call | solution.py:468
  110.4 8.7 %shard_map.150 = f32[1576,384]{1,0:T(8,128)} custom-call(bf16[2,208,1152]{2,1,0:T(8,128)(2,1)} %shard_map.147.refs_0_, bf16[4,208,1152]{2,1,0:T(8,128)(2,1)} %shard_map.148.refs_1_, bf16[2,208,1152]{2,1,0:T(8,128)(2,1)} %get-tuple-element.46.refs_2_, bf16[384,1152]{1,0:T(8,128)(2,1)} %get-tuple-element.45.w_ref.refs_3_, ...), custom_call_target="tpu_custom_call" | custom-call | flops 2000000000 | bytes 10000000 | tf_op jit(solution)/shard_map/pallas_call | solution.py:468
  119.3 1.6 collective-permute-start.13
  121.0 1.6 collective-permute-start.21
  122.6 4.7 %collective-permute-done.13 = bf16[8,24,640]{2,1,0:T(8,128)(2,1)S(1)} collective-permute-done((bf16[8,24,640]{2,1,0:T(8,128)(2,1)S(1)}, bf16[8,24,640]{2,1,0:T(8,128)(2,1)S(1)}, u32[]{:S(2)}, u32[]{:S(2)}) %collective-permute-start.13) | collective-permute-done | bytes 245792 | tf_op jit(solution)/shard_map/ppermute | solution.py:43
  127.4 1.6 collective-permute-start.14
  129.3 1.6 collective-permute-start.18
  130.9 1.6 collective-permute-done.14
  132.5 4.0 %collective-permute-start.15 = (bf16[2,24,640]{2,1,0:T(8,128)(2,1)S(1)}, bf16[2,24,640]{2,1,0:T(8,128)(2,1)S(1)}, u32[]{:S(2)}, u32[]{:S(2)}) collective-permute-start(bf16[2,24,640]{2,1,0:T(8,128)(2,1)S(1)} %slice.93), channel_id=1, source_target_pairs={{0,8},{2,10},{4,12},{6,14},{8,0},{10,2},{12,4},{14,6},{16,24},{18,... | collective-permute-start | bytes 184328 | tf_op jit(solution)/shard_map/ppermute | solution.py:43
  136.6 1.4 collective-permute-start.22
  138.7 3.8 %collective-permute-done.22 = bf16[4,24,768]{2,1,0:T(8,128)(2,1)S(1)} collective-permute-done((bf16[4,24,768]{2,1,0:T(8,128)(2,1)S(1)}, bf16[4,24,768]{2,1,0:T(8,128)(2,1)S(1)}, u32[]{:S(2)}, u32[]{:S(2)}) %collective-permute-start.22) | collective-permute-done | bytes 147488 | tf_op jit(solution)/shard_map/ppermute | solution.py:43
  143.6 4.9 %collective-permute-done.19 = bf16[4,24,1024]{2,1,0:T(8,128)(2,1)S(1)} collective-permute-done((bf16[4,24,1024]{2,1,0:T(8,128)(2,1)S(1)}, bf16[4,24,1024]{2,1,0:T(8,128)(2,1)S(1)}, u32[]{:S(2)}, u32[]{:S(2)}) %collective-permute-start.19) | collective-permute-done | bytes 196640 | tf_op jit(solution)/shard_map/ppermute | solution.py:43
  148.5 4.0 %collective-permute-start.23 = (bf16[2,24,1792]{2,1,0:T(8,128)(2,1)S(1)}, bf16[2,24,1792]{2,1,0:T(8,128)(2,1)S(1)}, u32[]{:S(2)}, u32[]{:S(2)}) collective-permute-start(bf16[2,24,1792]{2,1,0:T(8,128)(2,1)S(1)} %pad_maximum_fusion.2), channel_id=1, source_target_pairs={{0,8},{2,10},{4,12},{6,14},{8,0},{10,2},{12,4},{14,6},{16,24},{18,... | collective-permute-start | bytes 516104 | tf_op jit(solution)/shard_map/ppermute | solution.py:43
  153.1 4.2 %collective-permute-start.16 = (bf16[1,24,640]{2,1,0:T(8,128)(2,1)S(1)}, bf16[1,24,640]{2,1,0:T(8,128)(2,1)S(1)}, u32[]{:S(2)}, u32[]{:S(2)}) collective-permute-start(bf16[1,24,640]{2,1,0:T(8,128)(2,1)S(1)} %get-tuple-element.66), channel_id=1, source_target_pairs={{0,16},{2,18},{4,20},{6,22},{8,24},{10,26},{12,28},{14,30},{16,0},... | collective-permute-start | bytes 92168 | tf_op jit(solution)/shard_map/ppermute | solution.py:43
  158.0 3.1 %collective-permute-start.24 = (bf16[1,24,1792]{2,1,0:T(8,128)(2,1)S(1)}, bf16[1,24,1792]{2,1,0:T(8,128)(2,1)S(1)}, u32[]{:S(2)}, u32[]{:S(2)}) collective-permute-start(bf16[1,24,1792]{2,1,0:T(8,128)(2,1)S(1)} %get-tuple-element.62), channel_id=1, source_target_pairs={{0,16},{2,18},{4,20},{6,22},{8,24},{10,26},{12,28},{14,30},{16,0},... | collective-permute-start | bytes 258056 | tf_op jit(solution)/shard_map/ppermute | solution.py:43
  161.1 7.7 %shard_map.146 = bf16[1576,384]{1,0:T(8,128)(2,1)} custom-call(bf16[8,208,1536]{2,1,0:T(8,128)(2,1)} %get-tuple-element.38.hid_ref, bf16[384,1536]{1,0:T(8,128)(2,1)} %get-tuple-element.39.fc2_ref, f32[8,208,384]{2,1,0:T(8,128)} %get-tuple-element.40.mid_ref), custom_call_target="tpu_custom_call" | custom-call | flops 2000000000 | bytes 10000000 | tf_op jit(solution)/shard_map/pallas_call | solution.py:468
  169.4 1.5 shard_map.151
  171.5 1.6 shard_map.152
  (93 shorter events, 17.6 us)
Async XLA Ops:
  2.3 20.2 %copy-start.4 = (bf16[1,24,640]{2,1,0:T(8,128)(2,1)S(1)}, bf16[1,24,640]{2,1,0:T(8,128)(2,1)}, u32[]{:S(2)}) copy-start(bf16[1,24,640]{2,1,0:T(8,128)(2,1)} %get-tuple-element.35) | copy-start | bytes 92164
  2.3 6.5 %collective-permute-start.6 = (bf16[1,24,640]{2,1,0:T(8,128)(2,1)}, bf16[1,24,640]{2,1,0:T(8,128)(2,1)S(1)}, u32[]{:S(2)}, u32[]{:S(2)}) collective-permute-start(bf16[1,24,640]{2,1,0:T(8,128)(2,1)} %get-tuple-element.35), channel_id=1, source_target_pairs={{0,16},{2,18},{4,20},{6,22},{8,24},{10,26},{12,28},{14,30},{16,0},... | collective-permute-start | bytes 92168 | tf_op jit(solution)/shard_map/ppermute | solution.py:43
  6.3 7.2 %collective-permute-start = (bf16[1,24,1792]{2,1,0:T(8,128)(2,1)}, bf16[1,24,1792]{2,1,0:T(8,128)(2,1)S(1)}, u32[]{:S(2)}, u32[]{:S(2)}) collective-permute-start(bf16[1,24,1792]{2,1,0:T(8,128)(2,1)} %get-tuple-element.34), channel_id=1, source_target_pairs={{0,16},{2,18},{4,20},{6,22},{8,24},{10,26},{12,28},{14,30},{16,0},... | collective-permute-start | bytes 258056 | tf_op jit(solution)/shard_map/ppermute | solution.py:43
  9.6 12.8 %collective-permute-start.7 = (bf16[2,24,640]{2,1,0:T(8,128)(2,1)S(1)}, bf16[2,24,640]{2,1,0:T(8,128)(2,1)S(1)}, u32[]{:S(2)}, u32[]{:S(2)}) collective-permute-start(bf16[2,24,640]{2,1,0:T(8,128)(2,1)S(1)} %pad_maximum_fusion.4), channel_id=1, source_target_pairs={{0,8},{2,10},{4,12},{6,14},{8,0},{10,2},{12,4},{14,6},{16,24},{18,... | collective-permute-start | bytes 184328 | tf_op jit(solution)/shard_map/ppermute | solution.py:43
  14.4 32.3 %copy-start = (bf16[1576,384]{1,0:T(8,128)(2,1)S(1)}, bf16[1576,384]{1,0:T(8,128)(2,1)}, u32[]{:S(2)}) copy-start(bf16[1576,384]{1,0:T(8,128)(2,1)} %param.8) | copy-start | bytes 3631108
  14.5 5.5 %collective-permute-start.1 = (bf16[2,24,1792]{2,1,0:T(8,128)(2,1)S(1)}, bf16[2,24,1792]{2,1,0:T(8,128)(2,1)S(1)}, u32[]{:S(2)}, u32[]{:S(2)}) collective-permute-start(bf16[2,24,1792]{2,1,0:T(8,128)(2,1)S(1)} %pad_maximum_fusion.1), channel_id=1, source_target_pairs={{0,8},{2,10},{4,12},{6,14},{8,0},{10,2},{12,4},{14,6},{16,24},{18,... | collective-permute-start | bytes 516104 | tf_op jit(solution)/shard_map/ppermute | solution.py:43
  20.9 8.2 %collective-permute-start.2 = (bf16[4,24,1792]{2,1,0:T(8,128)(2,1)S(1)}, bf16[4,24,1792]{2,1,0:T(8,128)(2,1)S(1)}, u32[]{:S(2)}, u32[]{:S(2)}) collective-permute-start(bf16[4,24,1792]{2,1,0:T(8,128)(2,1)S(1)} %pad_maximum_fusion), channel_id=1, source_target_pairs={{0,4},{2,6},{4,0},{6,2},{8,12},{10,14},{12,8},{14,10},{16,20},{18,... | collective-permute-start | bytes 1032200 | tf_op jit(solution)/shard_map/ppermute | solution.py:43
  22.4 8.3 %collective-permute-start.8 = (bf16[4,24,640]{2,1,0:T(8,128)(2,1)S(1)}, bf16[4,24,640]{2,1,0:T(8,128)(2,1)S(1)}, u32[]{:S(2)}, u32[]{:S(2)}) collective-permute-start(bf16[4,24,640]{2,1,0:T(8,128)(2,1)S(1)} %pad_maximum_fusion.3), channel_id=1, source_target_pairs={{0,4},{2,6},{4,0},{6,2},{8,12},{10,14},{12,8},{14,10},{16,20},{18,... | collective-permute-start | bytes 368648 | tf_op jit(solution)/shard_map/ppermute | solution.py:43
  29.1 22.0 %copy-start.7 = (bf16[8,24,1792]{2,1,0:T(8,128)(2,1)}, bf16[8,24,1792]{2,1,0:T(8,128)(2,1)S(1)}, u32[]{:S(2)}) copy-start(bf16[8,24,1792]{2,1,0:T(8,128)(2,1)S(1)} %constant_dynamic-update-slice_fusion.p0) | copy-start | bytes 2064388
  29.1 22.5 %collective-permute-start.3 = (bf16[8,24,1792]{2,1,0:T(8,128)(2,1)S(1)}, bf16[8,24,1792]{2,1,0:T(8,128)(2,1)}, u32[]{:S(2)}, u32[]{:S(2)}) collective-permute-start(bf16[8,24,1792]{2,1,0:T(8,128)(2,1)S(1)} %constant_dynamic-update-slice_fusion.p0), channel_id=1, source_target_pairs={{0,1},{1,0},{2,3},{3,2},{4,5},{5,4},{6,7},{7,6},{8,9},{9,8},{10,11... | collective-permute-start | bytes 2064392 | tf_op jit(solution)/shard_map/ppermute | solution.py:43
  30.7 18.0 %copy-start.8 = (bf16[8,24,640]{2,1,0:T(8,128)(2,1)}, bf16[8,24,640]{2,1,0:T(8,128)(2,1)S(1)}, u32[]{:S(2)}) copy-start(bf16[8,24,640]{2,1,0:T(8,128)(2,1)S(1)} %constant_dynamic-update-slice_fusion.4.p0) | copy-start | bytes 737284
  30.7 16.0 %collective-permute-start.9 = (bf16[8,24,640]{2,1,0:T(8,128)(2,1)S(1)}, bf16[8,24,640]{2,1,0:T(8,128)(2,1)}, u32[]{:S(2)}, u32[]{:S(2)}) collective-permute-start(bf16[8,24,640]{2,1,0:T(8,128)(2,1)S(1)} %constant_dynamic-update-slice_fusion.4.p0), channel_id=1, source_target_pairs={{0,1},{1,0},{2,3},{3,2},{4,5},{5,4},{6,7},{7,6},{8,9},{9,8},{10,11... | collective-permute-start | bytes 737288 | tf_op jit(solution)/shard_map/ppermute | solution.py:43
  32.0 19.7 %collective-permute-start.10 = (bf16[8,24,640]{2,1,0:T(8,128)(2,1)S(1)}, bf16[8,24,640]{2,1,0:T(8,128)(2,1)}, u32[]{:S(2)}, u32[]{:S(2)}) collective-permute-start(bf16[8,24,640]{2,1,0:T(8,128)(2,1)S(1)} %constant_dynamic-update-slice_fusion.4.p0), channel_id=1, source_target_pairs={{0,2},{2,0},{4,6},{6,4},{8,10},{10,8},{12,14},{14,12},{16,18},{18,... | collective-permute-start | bytes 737288 | tf_op jit(solution)/shard_map/ppermute | solution.py:43
  46.7 5.0 %collective-permute-start.11 = (bf16[8,24,640]{2,1,0:T(8,128)(2,1)}, bf16[8,24,640]{2,1,0:T(8,128)(2,1)}, u32[]{:S(2)}, u32[]{:S(2)}) collective-permute-start(bf16[8,24,640]{2,1,0:T(8,128)(2,1)} %collective-permute-done.9.p1), channel_id=1, source_target_pairs={{0,2},{2,0},{4,6},{6,4},{8,10},{10,8},{12,14},{14,12},{16,18},{18,... | collective-permute-start | bytes 737288 | tf_op jit(solution)/shard_map/ppermute | solution.py:43
  51.1 13.1 %collective-permute-start.4 = (bf16[8,24,1792]{2,1,0:T(8,128)(2,1)S(1)}, bf16[8,24,1792]{2,1,0:T(8,128)(2,1)S(1)}, u32[]{:S(2)}, u32[]{:S(2)}) collective-permute-start(bf16[8,24,1792]{2,1,0:T(8,128)(2,1)S(1)} %constant_dynamic-update-slice_fusion.p0), channel_id=1, source_target_pairs={{0,2},{2,0},{4,6},{6,4},{8,10},{10,8},{12,14},{14,12},{16,18},{18,... | collective-permute-start | bytes 2064392 | tf_op jit(solution)/shard_map/ppermute | solution.py:43
  51.6 12.6 %collective-permute-start.5 = (bf16[8,24,1792]{2,1,0:T(8,128)(2,1)}, bf16[8,24,1792]{2,1,0:T(8,128)(2,1)S(1)}, u32[]{:S(2)}, u32[]{:S(2)}) collective-permute-start(bf16[8,24,1792]{2,1,0:T(8,128)(2,1)} %collective-permute-done.3.p1), channel_id=1, source_target_pairs={{0,2},{2,0},{4,6},{6,4},{8,10},{10,8},{12,14},{14,12},{16,18},{18,... | collective-permute-start | bytes 2064392 | tf_op jit(solution)/shard_map/ppermute | solution.py:43
  100.5 9.4 %copy-start.12 = (bf16[16,24,768]{2,1,0:T(8,128)(2,1)S(1)}, bf16[16,24,768]{2,1,0:T(8,128)(2,1)}, u32[]{:S(2)}) copy-start(bf16[16,24,768]{2,1,0:T(8,128)(2,1)} %get-tuple-element.55) | copy-start | bytes 1769476
  100.5 9.5 %copy-start.9 = (bf16[16,24,1024]{2,1,0:T(8,128)(2,1)S(1)}, bf16[16,24,1024]{2,1,0:T(8,128)(2,1)}, u32[]{:S(2)}) copy-start(bf16[16,24,1024]{2,1,0:T(8,128)(2,1)} %get-tuple-element.53) | copy-start | bytes 2359300
  109.4 9.6 %collective-permute-start.12 = (bf16[16,24,640]{2,1,0:T(8,128)(2,1)}, bf16[16,24,640]{2,1,0:T(8,128)(2,1)S(1)}, u32[]{:S(2)}, u32[]{:S(2)}) collective-permute-start(bf16[16,24,640]{2,1,0:T(8,128)(2,1)} %get-tuple-element.49), channel_id=1, source_target_pairs={{0,2},{2,0},{4,6},{6,4},{8,10},{10,8},{12,14},{14,12},{16,18},{18,... | collective-permute-start | bytes 1474568 | tf_op jit(solution)/shard_map/ppermute | solution.py:43
  109.8 11.0 %collective-permute-start.20 = (bf16[16,24,768]{2,1,0:T(8,128)(2,1)S(1)}, bf16[16,24,768]{2,1,0:T(8,128)(2,1)S(1)}, u32[]{:S(2)}, u32[]{:S(2)}) collective-permute-start(bf16[16,24,768]{2,1,0:T(8,128)(2,1)S(1)} %copy-done.12), channel_id=1, source_target_pairs={{0,2},{2,0},{4,6},{6,4},{8,10},{10,8},{12,14},{14,12},{16,18},{18,... | collective-permute-start | bytes 1769480 | tf_op jit(solution)/shard_map/ppermute | solution.py:43
  110.0 19.0 %collective-permute-start.17 = (bf16[16,24,1024]{2,1,0:T(8,128)(2,1)S(1)}, bf16[16,24,1024]{2,1,0:T(8,128)(2,1)S(1)}, u32[]{:S(2)}, u32[]{:S(2)}) collective-permute-start(bf16[16,24,1024]{2,1,0:T(8,128)(2,1)S(1)} %copy-done.9), channel_id=1, source_target_pairs={{0,2},{2,0},{4,6},{6,4},{8,10},{10,8},{12,14},{14,12},{16,18},{18,... | collective-permute-start | bytes 2359304 | tf_op jit(solution)/shard_map/ppermute | solution.py:43
  110.4 8.7 %copy-start.3 = (bf16[16,24,640]{2,1,0:T(8,128)(2,1)S(1)}, bf16[16,24,640]{2,1,0:T(8,128)(2,1)}, u32[]{:S(2)}) copy-start(bf16[16,24,640]{2,1,0:T(8,128)(2,1)} %get-tuple-element.48) | copy-start | bytes 1474564
  119.3 8.0 %collective-permute-start.13 = (bf16[8,24,640]{2,1,0:T(8,128)(2,1)S(1)}, bf16[8,24,640]{2,1,0:T(8,128)(2,1)S(1)}, u32[]{:S(2)}, u32[]{:S(2)}) collective-permute-start(bf16[8,24,640]{2,1,0:T(8,128)(2,1)S(1)} %slice.89), channel_id=1, source_target_pairs={{0,1},{1,0},{2,3},{3,2},{4,5},{5,4},{6,7},{7,6},{8,9},{9,8},{10,11... | collective-permute-start | bytes 737288 | tf_op jit(solution)/shard_map/ppermute | solution.py:43
  121.0 15.5 %collective-permute-start.21 = (bf16[8,24,768]{2,1,0:T(8,128)(2,1)S(1)}, bf16[8,24,768]{2,1,0:T(8,128)(2,1)S(1)}, u32[]{:S(2)}, u32[]{:S(2)}) collective-permute-start(bf16[8,24,768]{2,1,0:T(8,128)(2,1)S(1)} %slice.102), channel_id=1, source_target_pairs={{0,4},{2,6},{4,0},{6,2},{8,12},{10,14},{12,8},{14,10},{16,20},{18,... | collective-permute-start | bytes 884744 | tf_op jit(solution)/shard_map/ppermute | solution.py:43
  127.4 5.1 %collective-permute-start.14 = (bf16[4,24,640]{2,1,0:T(8,128)(2,1)S(1)}, bf16[4,24,640]{2,1,0:T(8,128)(2,1)S(1)}, u32[]{:S(2)}, u32[]{:S(2)}) collective-permute-start(bf16[4,24,640]{2,1,0:T(8,128)(2,1)S(1)} %slice.91), channel_id=1, source_target_pairs={{0,4},{2,6},{4,0},{6,2},{8,12},{10,14},{12,8},{14,10},{16,20},{18,... | collective-permute-start | bytes 368648 | tf_op jit(solution)/shard_map/ppermute | solution.py:43
  129.3 13.2 %collective-permute-start.18 = (bf16[8,24,1024]{2,1,0:T(8,128)(2,1)S(1)}, bf16[8,24,1024]{2,1,0:T(8,128)(2,1)S(1)}, u32[]{:S(2)}, u32[]{:S(2)}) collective-permute-start(bf16[8,24,1024]{2,1,0:T(8,128)(2,1)S(1)} %slice.97), channel_id=1, source_target_pairs={{0,1},{1,0},{2,3},{3,2},{4,5},{5,4},{6,7},{7,6},{8,9},{9,8},{10,11... | collective-permute-start | bytes 1179656 | tf_op jit(solution)/shard_map/ppermute | solution.py:43
  132.5 6.2 %collective-permute-start.15 = (bf16[2,24,640]{2,1,0:T(8,128)(2,1)S(1)}, bf16[2,24,640]{2,1,0:T(8,128)(2,1)S(1)}, u32[]{:S(2)}, u32[]{:S(2)}) collective-permute-start(bf16[2,24,640]{2,1,0:T(8,128)(2,1)S(1)} %slice.93), channel_id=1, source_target_pairs={{0,8},{2,10},{4,12},{6,14},{8,0},{10,2},{12,4},{14,6},{16,24},{18,... | collective-permute-start | bytes 184328 | tf_op jit(solution)/shard_map/ppermute | solution.py:43
  136.6 5.9 %collective-permute-start.22 = (bf16[4,24,768]{2,1,0:T(8,128)(2,1)S(1)}, bf16[4,24,768]{2,1,0:T(8,128)(2,1)S(1)}, u32[]{:S(2)}, u32[]{:S(2)}) collective-permute-start(bf16[4,24,768]{2,1,0:T(8,128)(2,1)S(1)} %slice.104), channel_id=1, source_target_pairs={{0,1},{1,0},{2,3},{3,2},{4,5},{5,4},{6,7},{7,6},{8,9},{9,8},{10,11... | collective-permute-start | bytes 442376 | tf_op jit(solution)/shard_map/ppermute | solution.py:43
  142.7 5.7 %collective-permute-start.19 = (bf16[4,24,1024]{2,1,0:T(8,128)(2,1)S(1)}, bf16[4,24,1024]{2,1,0:T(8,128)(2,1)S(1)}, u32[]{:S(2)}, u32[]{:S(2)}) collective-permute-start(bf16[4,24,1024]{2,1,0:T(8,128)(2,1)S(1)} %slice.99), channel_id=1, source_target_pairs={{0,4},{2,6},{4,0},{6,2},{8,12},{10,14},{12,8},{14,10},{16,20},{18,... | collective-permute-start | bytes 589832 | tf_op jit(solution)/shard_map/ppermute | solution.py:43
  148.5 8.8 %collective-permute-start.23 = (bf16[2,24,1792]{2,1,0:T(8,128)(2,1)S(1)}, bf16[2,24,1792]{2,1,0:T(8,128)(2,1)S(1)}, u32[]{:S(2)}, u32[]{:S(2)}) collective-permute-start(bf16[2,24,1792]{2,1,0:T(8,128)(2,1)S(1)} %pad_maximum_fusion.2), channel_id=1, source_target_pairs={{0,8},{2,10},{4,12},{6,14},{8,0},{10,2},{12,4},{14,6},{16,24},{18,... | collective-permute-start | bytes 516104 | tf_op jit(solution)/shard_map/ppermute | solution.py:43
  153.1 15.7 %collective-permute-start.16 = (bf16[1,24,640]{2,1,0:T(8,128)(2,1)S(1)}, bf16[1,24,640]{2,1,0:T(8,128)(2,1)S(1)}, u32[]{:S(2)}, u32[]{:S(2)}) collective-permute-start(bf16[1,24,640]{2,1,0:T(8,128)(2,1)S(1)} %get-tuple-element.66), channel_id=1, source_target_pairs={{0,16},{2,18},{4,20},{6,22},{8,24},{10,26},{12,28},{14,30},{16,0},... | collective-permute-start | bytes 92168 | tf_op jit(solution)/shard_map/ppermute | solution.py:43
  158.0 12.8 %collective-permute-start.24 = (bf16[1,24,1792]{2,1,0:T(8,128)(2,1)S(1)}, bf16[1,24,1792]{2,1,0:T(8,128)(2,1)S(1)}, u32[]{:S(2)}, u32[]{:S(2)}) collective-permute-start(bf16[1,24,1792]{2,1,0:T(8,128)(2,1)S(1)} %get-tuple-element.62), channel_id=1, source_target_pairs={{0,16},{2,18},{4,20},{6,22},{8,24},{10,26},{12,28},{14,30},{16,0},... | collective-permute-start | bytes 258056 | tf_op jit(solution)/shard_map/ppermute | solution.py:43
  (6 other events, 13.0 us)

commit v4 on v3

v4 whole, which is shorter than its diff:
```python
import functools

import jax
import jax.numpy as jnp
from jax import lax
from jax.experimental import pallas as pl
from jax.experimental.pallas import tpu as pltpu
from jax.sharding import PartitionSpec as P

HD = 64
SEQ = 197
PAD = 208
PER = 2
CUT = 192
WIDE = 512
LANES = 256
D = 384
QC = 640
F32 = jnp.float32
BF16 = jnp.bfloat16
NT = (((1,), (1,)), ((), ()))
GELU_C = 0.7978845608028654


def dot(a, b, dims=(((1,), (0,)), ((), ()))):
    return lax.dot_general(a, b, dims, preferred_element_type=F32)


def stage_bits(wide):
    bits = [("wide", 1 << k) for k in range(1, wide.bit_length() - 1)]
    bits = bits[:0:-1] + bits[:1]
    return bits + [("tensor", 1), ("wide", 1)]


def relative(stages):
    places = [(0, 0)]
    for axis, bit in stages:
        places = places + [(w ^ bit, t) if axis == "wide" else (w, t ^ bit) for w, t in places]
    return places


def swap(value, stage, sizes):
    axis, bit = stage
    return lax.ppermute(value, axis, [(i, i ^ bit) for i in range(sizes[axis])])


def gather(held, stages, sizes):
    for stage in stages[:-2]:
        held = grow(held, stage, sizes)
    got = swap(held, stages[-2], sizes)
    return [held, got, swap(held, stages[-1], sizes), swap(got, stages[-1], sizes)]


def grow(held, stage, sizes):
    got = swap(held, stage, sizes)
    return jnp.concatenate([held, got], axis=0)


def reduce_stage(total, stage, sizes):
    half = total.shape[0] // 2
    return add_got(total[:half], swap(total[half:], stage, sizes))


def add_got(keep, got):
    return (keep.astype(F32) + got.astype(F32)).astype(BF16)


def in_order(places, held):
    me_w, me_t = lax.axis_index("wide"), lax.axis_index("tensor")
    at = {place: p for p, place in enumerate(places)}
    wide = len(places) // 2
    table = jnp.array([[at[w, t] for w in range(wide)] for t in range(2)], jnp.int32)
    order = table[me_t ^ jnp.arange(2)[:, None], me_w ^ jnp.arange(wide)[None, :]]
    return held[order.reshape(-1)].reshape(16, 48, held.shape[2])


def out_of_order(places, blocks, rows):
    me_w, me_t = lax.axis_index("wide"), lax.axis_index("tensor")
    wide = len(places) // 2
    order = jnp.array([w for w, _ in places], jnp.int32) ^ me_w
    order += wide * (jnp.array([t for _, t in places], jnp.int32) ^ me_t)
    return blocks.reshape(len(places), rows, blocks.shape[2])[order]


def rows_of(places, rows):
    if rows == 48:
        me_w, me_t = 0, 0
        places = [(w, t) for t in range(2) for w in range(8)]
    else:
        me_w, me_t = lax.axis_index("wide"), lax.axis_index("tensor")
    for p, (w, t) in enumerate(places):
        yield p, me_t ^ t, pl.ds(pl.multiple_of((me_w ^ w) * rows, 8), rows)


def unpack(places, rows, pieces, scr, at=0):
    size = len(pieces[0])
    width = pieces[0].shape[-1]
    for p, t, where in rows_of(places, rows):
        scr[t, where, at : at + width] = pieces[p // size][p % size].astype(F32)


def repack(places, rows, scr, pieces, at=0):
    size = len(pieces[0])
    width = pieces[0].shape[-1]
    for p, t, where in rows_of(places, rows):
        pieces[p // size][p % size] = scr[t, where, at : at + width].astype(BF16)


def normalize(v):
    center = v - jnp.mean(v, axis=-1, keepdims=True)
    rstd = lax.rsqrt(jnp.mean(center * center, axis=-1, keepdims=True) + 1e-06)
    return center * rstd, rstd


def norm_back(grad, xhat, rstd, gain):
    g = grad * gain
    return rstd * (
        g
        - jnp.mean(g, axis=-1, keepdims=True)
        - xhat * jnp.mean(g * xhat, axis=-1, keepdims=True)
    )


def low_lanes():
    return lax.broadcasted_iota(jnp.int32, (PAD, 128), 1) < HD


def both_heads(value, low):
    zero = jnp.zeros_like(value)
    gap = jnp.zeros((LANES - PAD, 128), value.dtype)
    return jnp.concatenate([jnp.where(low, value, zero), gap, jnp.where(low, zero, value), gap], axis=0)


def own_heads(value):
    own = jnp.concatenate([value[:HD, :LANES], value[HD:, LANES:]], axis=0)
    return own.T[:PAD]


def lanes(kind, c):
    return slice((3 * c + kind) * 128, (3 * c + kind) * 128 + 128)


def tall(ref):
    return ref[...].reshape(PER * PAD, ref.shape[-1])


def column(row):
    n = row.shape[1]
    own = lax.broadcasted_iota(jnp.int32, (n, n), 0) == lax.broadcasted_iota(jnp.int32, (n, n), 1)
    return jnp.sum(jnp.where(own, jnp.broadcast_to(row, (n, n)), 0.0), axis=1, keepdims=True)


def line(col):
    n = col.shape[0]
    own = lax.broadcasted_iota(jnp.int32, (n, n), 0) == lax.broadcasted_iota(jnp.int32, (n, n), 1)
    return jnp.sum(jnp.where(own, jnp.broadcast_to(col, (n, n)), 0.0), axis=0, keepdims=True)


def pack_kernel(qkv, gain1, gain2, out, fc1, fc2, first, rest):
    rows = out.shape[0]
    fs = fc1.shape[1]
    lane = lax.broadcasted_iota(jnp.int32, (rows, HD), 1)
    gains = jnp.where(lane == 0, column(gain1[...]), jnp.where(lane == 1, column(gain2[...]), 0.0))
    for c in range(3):
        first[0, :, c * 128 : c * 128 + 128] = qkv[c, :, 0:128]
    single = [qkv[c, :, 128:192].astype(F32) for c in range(3)]
    first[0, :, 384:512] = jnp.concatenate(single[:2], axis=1).astype(BF16)
    first[0, :, 512:640] = jnp.concatenate([single[2], gains], axis=1).astype(BF16)
    rest[0, :, 0:128] = out[:, 0:128]
    pad = jnp.zeros((rows, HD), F32)
    rest[0, :, 128:256] = jnp.concatenate([out[:, 128:192].astype(F32), pad], axis=1).astype(BF16)
    rest[0, :, 256 : 256 + fs] = fc1[...]
    rest[0, :, 256 + fs :] = fc2[...]


def attend_kernel(places, rows, p0, p1, p2, p3, x_ref, qkv_ref, probs_ref, heads_ref, n1_ref, w_ref, gain_ref, scr):
    @pl.when(pl.program_id(0) == 0)
    def _():
        unpack(places, rows, (p0, p1, p2, p3), scr)
        for t in range(2):
            w_ref[:, t * D : t * D + D] = scr[t, :, 0:D].astype(BF16)
        for kind in range(3):
            one = slice(D + kind * HD, D + kind * HD + HD)
            last = jnp.concatenate([scr[0, :, one], scr[1, :, one]], axis=1)
            w_ref[:, lanes(kind, 2)] = last.astype(BF16)
        turned = scr[0, :, 512:640].T
        gain_ref[...] = turned[HD : HD + 8, :]

    xhat, _ = normalize(tall(x_ref).astype(F32))
    n1 = (xhat * gain_ref[0:1, :]).astype(BF16)
    n1_ref[...] = n1.reshape(PER, PAD, D)
    low = low_lanes()
    tail_ok = lax.broadcasted_iota(jnp.int32, (PAD - CUT, WIDE), 0) < SEQ - CUT

    def project(c):
        at = slice(c * WIDE, min(c * WIDE + WIDE, 3 * D))
        value = dot(n1, w_ref[:, at])
        for piece in range((at.stop - at.start) // 128):
            here = value[:, piece * 128 : piece * 128 + 128]
            if (c * 4 + piece) % 3 == 0:
                here = here * (HD**-0.5)
            span = slice(at.start + piece * 128, at.start + piece * 128 + 128)
            qkv_ref[:, :, span] = here.astype(BF16).reshape(PER, PAD, 128)

    def enter(i, c):
        q, k, v = (qkv_ref[i, :, lanes(kind, c)] for kind in range(3))
        return dot(k, both_heads(q, low), NT), v.T

    units = [(i, c) for c in range(3) for i in range(PER)]
    project(0)
    ahead = enter(*units[0])
    for j, (i, c) in enumerate(units):
        scores, v_turned = ahead
        if j + 1 < len(units):
            if i == 0 and c < 2:
                project(c + 1)
            ahead = enter(*units[j + 1])
        scores = jnp.concatenate([scores[:CUT], jnp.where(tail_ok, scores[CUT:], -1e30)], axis=0)
        expon = jnp.exp(scores - jnp.max(scores, axis=0, keepdims=True))
        probs = (expon * (1.0 / jnp.sum(expon, axis=0, keepdims=True))).astype(BF16)
        probs_ref[i, c] = probs
        heads_ref[i, :, c * 128 : c * 128 + 128] = own_heads(dot(v_turned, probs)).astype(BF16)


def mlp_kernel(
    places, places2, rows, blocks, fs, p0, p1, p2, p3, r0, r1, r2, r3, x_ref, og_ref, h_ref, gain_ref,
    y_ref, mg_ref, hg_ref, keep1, send1, keep2, send2,
    scr, w_out, w_back, w_fc1, w_fc1_turned, fc2_ref, w_fc2_turned, n2_all, pg_all, hid_all, og_all, ml_all, h_all, y_all,
):
    step = pl.program_id(0)

    @pl.when(step == 0)
    def _():
        unpack(places2, rows, (p0, p1, p2, p3), scr)
        unpack(places, rows, (r0, r1, r2, r3), scr, 256 + fs)
        last = jnp.concatenate([scr[0, :, 128:192], scr[1, :, 128:192]], axis=1)
        h_all[:, D:] = jnp.zeros((h_all.shape[0], WIDE - D), BF16)
        for b, value in enumerate((scr[0, :, 0:128], scr[1, :, 0:128], last)):
            value = value.astype(BF16)
            w_back[:, b * 128 : b * 128 + 128] = value
            w_out[b * 128 : b * 128 + 128, :] = value.T
        for t in range(2):
            at = slice(t * fs, t * fs + fs)
            value = scr[t, :, 256 : 256 + fs].astype(BF16)
            w_fc1[:, at] = value
            w_fc1_turned[at, :] = value.T
            value = scr[t, :, 256 + fs :].astype(BF16)
            fc2_ref[:, at] = value
            w_fc2_turned[at, :] = value.T

    @pl.when(step < blocks)
    def _():
        size = PER * PAD
        at = pl.ds(pl.multiple_of(step * size, size), size)
        gain = gain_ref[1:2, :]
        h = tall(h_ref)
        og = tall(og_ref)
        h_all[at, :D] = h
        og_all[at, :] = og
        middle = tall(x_ref).astype(F32) + dot(h, w_out[...])
        xhat, rstd = normalize(middle)
        n2 = (xhat * gain).astype(BF16)
        n2_all[at, :] = n2
        width = 256
        back = None
        count = 2 * fs // width
        ahead = dot(n2, w_fc1[:, :width]), dot(og, fc2_ref[:, :width])
        for c in range(count):
            cols = slice(c * width, c * width + width)
            u, dh = ahead
            if c + 1 < count:
                after = slice(c * width + width, c * width + 2 * width)
                ahead = dot(n2, w_fc1[:, after]), dot(og, fc2_ref[:, after])
            square = u * u
            bent = jnp.tanh(u * (GELU_C + (GELU_C * 0.044715) * square))
            plus = 0.5 + 0.5 * bent
            full = u * plus
            hid = full.astype(BF16)
            hid_all[at, cols] = hid
            slope = plus + full * (1.0 - plus) * ((2.0 * GELU_C) + (GELU_C * 0.26829) * square)
            pg = (dh * slope).astype(BF16)
            pg_all[at, cols] = pg
            part = dot(pg, w_fc1_turned[cols, :])
            back = part if back is None else back + part
            middle += dot(hid, w_fc2_turned[cols, :])
        store_rows(y_all, middle, step, blocks)
        mg = og.astype(F32) + norm_back(back, xhat, rstd, gain)
        mg_ref[...] = mg.reshape(PER, PAD, D)
        ml = mg.astype(BF16)
        ml_all[at, :] = ml
        hg_ref[...] = dot(ml, w_back[...]).astype(BF16).reshape(PER, PAD, D)

    @pl.when(step == blocks)
    def _():
        row_sum = jnp.zeros((D, 1), F32)
        for base, left, right in ((256, n2_all, pg_all), (256 + fs, og_all, hid_all)):
            turned = left[...].T
            for c in range(2 * fs // WIDE):
                cols = slice(c * WIDE, c * WIDE + WIDE)
                grad = dot(turned, right[:, cols])
                for piece in range(2):
                    t, at = divmod(c * WIDE + piece * 256, fs)
                    scr[t, :, base + at : base + at + 256] = grad[:, piece * 256 : piece * 256 + 256]
                if right is pg_all:
                    row_sum += jnp.sum(grad * w_fc1[:, cols].astype(F32), axis=1, keepdims=True)
        grad = dot(ml_all[...].T, h_all[...])
        scr[0, :, 0:128] = grad[:, 0:128]
        scr[1, :, 0:128] = grad[:, 128:256]
        gain = jnp.broadcast_to(row_sum, (D, HD))
        scr[0, :, 128:256] = jnp.concatenate([grad[:, 256 : 256 + HD], gain], axis=1)
        scr[1, :, 128:256] = jnp.concatenate([grad[:, 256 + HD : 384], gain], axis=1)
        repack(places, rows, scr, (keep1, send1))
        repack(places2, rows, scr, (keep2, send2), 256 + fs)
        y_ref[...] = y_all[...].astype(BF16)


def attend_back(qkv_ref, probs_ref, hg_ref, grad_ref, grad_all, at):
    low = low_lanes()
    units = [(i, c) for i in range(PER) for c in range(3)]

    def enter(i, c):
        do = both_heads(hg_ref[i, :, c * 128 : c * 128 + 128], low)
        return dot(qkv_ref[i, :, lanes(2, c)], do, NT), do

    ahead = enter(*units[0])
    for j, (i, c) in enumerate(units):
        dp, do = ahead
        if j + 1 < len(units):
            ahead = enter(*units[j + 1])
        low_probs = probs_ref[i, c]
        probs = low_probs.astype(F32)
        weighted = probs * dp
        ds = (weighted - probs * jnp.sum(weighted, axis=0, keepdims=True)).astype(BF16)
        q, k = qkv_ref[i, :, lanes(0, c)], qkv_ref[i, :, lanes(1, c)]
        dv = dot(low_probs, do)
        dk = dot(ds, both_heads(q, low))
        dq = own_heads(dot(k.T, ds)) * (HD**-0.5)
        for kind, value in enumerate((dq, dk, dv)):
            value = value.astype(BF16)
            grad_ref[i, :, lanes(kind, c)] = value
            if grad_all is not None:
                grad_all[pl.ds(pl.multiple_of(at + i * PAD, PAD), PAD), lanes(kind, c)] = value


def attend_back_kernel(qkv_ref, probs_ref, hg_ref, grad_ref):
    attend_back(qkv_ref, probs_ref, hg_ref, grad_ref, None, 0)


def attend_last_kernel(
    places, rows, blocks, qkv_ref, probs_ref, hg_ref, n1_ref, w_ref, *refs
):
    *earlier, grad_ref, keep, send, scr, grad_all = refs
    step = pl.program_id(0)
    early = sum(ref.shape[0] for ref in earlier) * PAD

    @pl.when(step == 0)
    def _():
        at = 0
        for ref in earlier:
            size = ref.shape[0] * PAD
            grad_all[at : at + size, :] = ref[...].reshape(size, 3 * D)
            at += size

    @pl.when(step < blocks)
    def _():
        attend_back(qkv_ref, probs_ref, hg_ref, grad_ref, grad_all, early + step * PER * PAD)

    @pl.when(step == blocks)
    def _():
        turned = n1_ref[...].reshape(-1, D).T
        row_sum = jnp.zeros((D, 1), F32)
        singles = [None] * 3
        for b in (8, 4, 0):
            some = range(b, min(b + 4, 9))
            span = slice(b * 128, some.stop * 128)
            grad = dot(turned, grad_all[:, span])
            row_sum += jnp.sum(grad * w_ref[:, span].astype(F32), axis=1, keepdims=True)
            for at in some:
                here = grad[:, (at - b) * 128 : (at - b) * 128 + 128]
                if at < 6:
                    scr[at // 3, :, at % 3 * 128 : at % 3 * 128 + 128] = here
                else:
                    singles[at - 6] = here
            if b == 4:
                for t in range(2):
                    own = [s[:, t * HD : t * HD + HD] for s in singles]
                    scr[t, :, 384:512] = jnp.concatenate(own[:2], axis=1)
                    scr[t, :, 512 : 512 + HD] = own[2]
        scr[:, :, 512 + HD : 640] = jnp.broadcast_to(row_sum[None], (2, D, HD))
        repack(places, rows, scr, (keep, send))


def store_rows(ref, value, step, steps):
    for s in range(steps):

        @pl.when(step == s)
        def _(s=s):
            for i in range(PER):
                at = (s * PER + i) * SEQ
                ref[at : at + SEQ, :] = value[i * PAD : i * PAD + SEQ]


def input_grad_kernel(cuts, *refs):
    *pieces, w_ref, x_ref, mg_ref, gain_ref, out_ref, w_turned, grad = refs
    step = pl.program_id(0)

    @pl.when(step == 0)
    def _():
        w_turned[:, :D] = w_ref[...].T
        w_turned[:, D:] = jnp.zeros((w_turned.shape[0], WIDE - D), BF16)

    at = 0
    for ref, count in zip(pieces, cuts, strict=True):

        @pl.when((step >= at) & (step < at + count))
        def _(ref=ref):
            grad[...] = tall(ref)

        at += count
    xhat, rstd = normalize(tall(x_ref).astype(F32))
    back = dot(grad[...], w_turned[...])[:, :D]
    dx = tall(mg_ref) + norm_back(back, xhat, rstd, gain_ref[0:1, :])
    store_rows(out_ref, dx, step, sum(cuts))


def finish_kernel(fs, mine_q, got_q, mine, got, gain1, gain2, ln1, qkv_grad, ln2, out_grad, fc1_grad, fc2_grad):
    total = mine_q[0].astype(F32) + got_q[0].astype(F32)
    for c in range(3):
        qkv_grad[c, :, 0:128] = total[:, c * 128 : c * 128 + 128]
        qkv_grad[c, :, 128:192] = total[:, 384 + c * HD : 448 + c * HD]
    ln1[...] = line(total[:, 576:577]) / gain1[...].astype(BF16).astype(F32)
    total = mine[0].astype(F32) + got[0].astype(F32)
    out_grad[...] = total[:, :192]
    fc1_grad[...] = total[:, 256 : 256 + fs]
    fc2_grad[...] = total[:, 256 + fs :]
    ln2[...] = line(total[:, 192:193]) / gain2[...].astype(BF16).astype(F32)


def whole(*shape):
    return pl.BlockSpec(shape, lambda *i: (0,) * len(shape))


def once(*shape):
    return pl.BlockSpec(shape, lambda *i: (0,) * len(shape), pipeline_mode=pl.Buffered(1))


def part(first, count, *shape):
    return pl.BlockSpec((PER,) + shape, lambda i: (first + jnp.minimum(i, count - 1),) + (0,) * len(shape))


def late(first, count, *shape):
    return pl.BlockSpec((PER,) + shape, lambda i: (jnp.clip(i - first, 0, count - 1),) + (0,) * len(shape))


def call(kernel, grid, ins, outs, scratch, args, mflops=0, kbytes=0, vmem=8):
    return pl.pallas_call(
        kernel,
        grid=(grid,) if grid else (),
        in_specs=ins,
        out_specs=[spec for spec, _ in outs],
        out_shape=[shape for _, shape in outs],
        scratch_shapes=scratch,
        compiler_params=pltpu.CompilerParams(vmem_limit_bytes=vmem * 1024 * 1024),
        cost_estimate=pl.CostEstimate(flops=mflops * 10**6, bytes_accessed=kbytes * 1000, transcendentals=0),
    )(*args)


def shape_of(*shape, dtype=BF16):
    return jax.ShapeDtypeStruct(shape, dtype)


def padded(v, images):
    return jnp.pad(v.reshape(images, SEQ, D), ((0, 0), (0, PAD - SEQ), (0, 0)))


def local(sizes, tokens, ln1_gain, qkv_weight, out_weight, ln2_gain, fc1_weight, fc2_weight, out_grad):
    return layer(sizes, tokens, ln1_gain, qkv_weight, out_weight, ln2_gain, fc1_weight, fc2_weight, out_grad)


def layer(sizes, tokens, ln1_gain, qkv_weight, out_weight, ln2_gain, fc1_weight, fc2_weight, out_grad):
    stages = stage_bits(sizes["wide"])
    stages2 = stages[:-3] + [stages[-2], stages[-3], stages[-1]]
    places, places2 = relative(stages), relative(stages2)
    n = len(places)
    rows = own_rows = qkv_weight.shape[0]
    images = tokens.shape[0] // SEQ
    blocks = images // PER
    fs = fc1_weight.shape[1]
    ff = 2 * fs
    rc = 256 + 2 * fs
    big = images * PAD
    gain1, gain2 = ln1_gain.reshape(1, rows), ln2_gain.reshape(1, rows)

    first, rest = call(
        pack_kernel,
        0,
        [whole(3, rows, 192), whole(1, rows), whole(1, rows), whole(rows, 192), whole(rows, fs), whole(rows, fs)],
        [(whole(1, rows, QC), shape_of(1, rows, QC)), (whole(1, rows, rc), shape_of(1, rows, rc))],
        [],
        (qkv_weight.transpose(1, 0, 2), gain1, gain2, out_weight.T, fc1_weight, fc2_weight.T),
        vmem=60,
    )
    first_all = gather(first, stages, sizes)
    for stage in stages[:-3]:
        rest = grow(rest, stage, sizes)
    rest1_all = gather(rest[:, :, : 256 + fs], stages2[-3:], sizes)
    rest2_all = gather(rest[:, :, 256 + fs :], stages[-3:], sizes)
    if rows % 8 != 0:
        n, rows = 16, 48
        first_all, rest1_all, rest2_all = (
            jnp.split(in_order(order, jnp.concatenate(v, axis=0)), 4)
            for order, v in ((places, first_all), (places2, rest1_all), (places, rest2_all))
        )

    x = padded(tokens, images)
    og = padded(out_grad, images)

    def row(*shape):
        return part(0, blocks, *shape)

    qkv, probs, heads, n1, w_qkv, gain = call(
        functools.partial(attend_kernel, places, rows),
        blocks,
        [once(n // 4, rows, QC)] * 4 + [row(PAD, D)],
        [
            (row(PAD, 3 * D), shape_of(images, PAD, 3 * D)),
            (row(3, PAD, WIDE), shape_of(images, 3, PAD, WIDE)),
            (row(PAD, D), shape_of(images, PAD, D)),
            (row(PAD, D), shape_of(images, PAD, D)),
            (whole(D, 3 * D), shape_of(D, 3 * D)),
            (whole(8, D), shape_of(8, D, dtype=F32)),
        ],
        [pltpu.VMEM((2, D, QC), F32)],
        (*first_all, x),
        8000,
        20000,
        24,
    )
    wide1, wide2 = 256 + fs, fs
    y, mg, hg, keep1, send1, keep2, send2 = call(
        functools.partial(mlp_kernel, places, places2, rows, blocks, fs),
        blocks + 1,
        [once(n // 4, rows, wide1)] * 4
        + [once(n // 4, rows, wide2)] * 4
        + [row(PAD, D), row(PAD, D), row(PAD, D), whole(8, D)],
        [
            (once(images * SEQ, D), shape_of(images * SEQ, D)),
            (row(PAD, D), shape_of(images, PAD, D, dtype=F32)),
            (row(PAD, D), shape_of(images, PAD, D)),
        ]
        + [(once(n // 2, rows, w), shape_of(n // 2, rows, w)) for w in (wide1, wide1, wide2, wide2)],
        [
            pltpu.VMEM((2, D, rc), F32),
            pltpu.VMEM((D, D), BF16),
            pltpu.VMEM((D, D), BF16),
            pltpu.VMEM((D, ff), BF16),
            pltpu.VMEM((ff, D), BF16),
            pltpu.VMEM((D, ff), BF16),
            pltpu.VMEM((ff, D), BF16),
            pltpu.VMEM((big, D), BF16),
            pltpu.VMEM((big, ff), BF16),
            pltpu.VMEM((big, ff), BF16),
            pltpu.VMEM((big, D), BF16),
            pltpu.VMEM((big, D), BF16),
            pltpu.VMEM((big, WIDE), BF16),
            pltpu.VMEM((images * SEQ, D), F32),
        ],
        (*rest1_all, *rest2_all, x, og, heads, gain),
        16000,
        30000,
        44,
    )
    if rows != own_rows:
        keep1, send1 = jnp.split(out_of_order(places, jnp.concatenate([keep1, send1], axis=0), own_rows), 2)
        keep2, send2 = jnp.split(out_of_order(places2, jnp.concatenate([keep2, send2], axis=0), own_rows), 2)
    back, back2 = stages[::-1], stages2[::-1]
    total1 = add_got(keep1, swap(send1, back[0], sizes))
    total2 = add_got(keep2, swap(send2, back[0], sizes))
    for s in (1, 2):
        total1 = reduce_stage(total1, back[s], sizes)
        total2 = reduce_stage(total2, back2[s], sizes)
    total = jnp.concatenate([total1, total2], axis=2)
    for stage in back[3:-1]:
        total = reduce_stage(total, stage, sizes)
    got = swap(total[1:], back[-1], sizes)

    cuts = (blocks // 2, blocks - blocks // 2)
    pieces = []
    at = 0
    for count in cuts[:-1]:
        pieces += call(
            attend_back_kernel,
            count,
            [part(at, count, *s) for s in ((PAD, 3 * D), (3, PAD, WIDE), (PAD, D))],
            [(part(0, count, PAD, 3 * D), shape_of(count * PER, PAD, 3 * D))],
            [],
            (qkv, probs, hg),
            1800 * count,
            4000 * count,
            20,
        )
        at += count
    left = cuts[-1]
    last, keep_q, send_q = call(
        functools.partial(attend_last_kernel, places, rows, left),
        left + 1,
        [part(at, left, *s) for s in ((PAD, 3 * D), (3, PAD, WIDE), (PAD, D))]
        + [once(images, PAD, D), once(D, 3 * D)]
        + [once(count * PER, PAD, 3 * D) for count in cuts[:-1]],
        [(part(0, left, PAD, 3 * D), shape_of(left * PER, PAD, 3 * D))]
        + [(whole(n // 2, rows, QC), shape_of(n // 2, rows, QC))] * 2,
        [pltpu.VMEM((2, D, QC), F32), pltpu.VMEM((big, 3 * D), BF16)],
        (qkv, probs, hg, n1, w_qkv, *pieces),
        3500,
        8000,
        32,
    )
    pieces.append(last)
    starts = [sum(cuts[:c]) for c in range(len(cuts))]
    (dx,) = call(
        functools.partial(input_grad_kernel, cuts),
        blocks,
        [late(at, count, PAD, 3 * D) for at, count in zip(starts, cuts, strict=True)]
        + [whole(D, 3 * D), row(PAD, D), row(PAD, D), whole(8, D)],
        [(once(images * SEQ, D), shape_of(images * SEQ, D, dtype=F32))],
        [pltpu.VMEM((3 * D, WIDE), BF16), pltpu.VMEM((PER * PAD, 3 * D), BF16)],
        (*pieces, w_qkv, x, mg, gain),
        2000,
        10000,
        24,
    )
    if rows != own_rows:
        keep_q, send_q = jnp.split(out_of_order(places, jnp.concatenate([keep_q, send_q], axis=0), own_rows), 2)
    total_q = add_got(keep_q, swap(send_q, back[0], sizes))
    for stage in back[1:-1]:
        total_q = reduce_stage(total_q, stage, sizes)
    got_q = swap(total_q[1:], back[-1], sizes)
    ln1_grad, qkv_grad, ln2_grad, out_wgrad, fc1_grad, fc2_grad = call(
        functools.partial(finish_kernel, fs),
        0,
        [whole(2, own_rows, QC), whole(1, own_rows, QC), whole(2, own_rows, rc), whole(1, own_rows, rc)]
        + [whole(1, own_rows)] * 2,
        [
            (whole(*shape), shape_of(*shape, dtype=F32))
            for shape in (
                (1, own_rows),
                (3, own_rows, 192),
                (1, own_rows),
                (own_rows, 192),
                (own_rows, fs),
                (own_rows, fs),
            )
        ],
        [],
        (total_q, got_q, total, got, gain1, gain2),
    )
    return (
        y,
        dx,
        ln1_grad.reshape(own_rows),
        qkv_grad.transpose(1, 0, 2),
        out_wgrad.T,
        ln2_grad.reshape(own_rows),
        fc1_grad,
        fc2_grad.T,
    )


def solution(mesh):
    rows = P(("wide", "tensor"), None)
    weights = (
        P("wide"),
        P("wide", None, "tensor"),
        P("tensor", "wide"),
        P("wide"),
        P("wide", "tensor"),
        P("tensor", "wide"),
    )
    return jax.shard_map(
        functools.partial(local, dict(mesh.shape)),
        mesh=mesh,
        in_specs=(rows, *weights, rows),
        out_specs=(rows, rows, *weights),
        check_vma=False,
    )
```

time: 174 us -> 138 us (0.79)
  Pallas kernels: 77.7 us -> 52.7 us
  waiting for transfers between devices: 43.9 us -> 31 us
  local copies, waits for them, and re-layouts: 9.9 us -> 15.1 us
  starting transfers between devices: 37 us -> 33.1 us
    pallas_call x10 -> x7, Pallas kernels: 77.7 us -> 52.7 us  [call(): pl.pallas_call(kernel, grid=(grid,) if grid else (), in_specs=ins, out_sp...]
    ppermute x25 -> x29, waiting for transfers between devices: 43.9 us -> 31 us  [swap(): return lax.ppermute(value, axis, [(i, i ^ bit) for i in range(sizes[axis])])]
    unnamed x32 -> x45, local copies, waits for them, and re-layouts: 4.06 us -> 10.4 us
    ppermute x25 -> x29, starting transfers between devices: 37 us -> 33.1 us  [swap(): return lax.ppermute(value, axis, [(i, i ^ bit) for i in range(sizes[axis])])]
  transfers between devices with their start and end apart: 25 -> 29, of which waited for: 10 -> 12; matrix products, arithmetic and copies ran while one was open for 6% -> 8% of each run, Pallas kernels for 18% -> 11%
where the time goes in v4:
time: 138 us; the launch traced here: 137 us
  Pallas kernels  52.7 us (38%)
  starting transfers between devices  33.1 us (24%)
  waiting for transfers between devices  31 us (22%)
  local copies, waits for them, and re-layouts  15.1 us (11%)
  other arithmetic  4.25 us (3%)
    pallas_call x7, Pallas kernels, call(): pl.pallas_call(kernel, grid=(grid,) if grid else (), in_specs=ins, out_sp...  52.7 us
    ppermute x29, starting transfers between devices, swap(): return lax.ppermute(value, axis, [(i, i ^ bit) for i in range(sizes[axis])])  33.1 us
    ppermute x29, waiting for transfers between devices, swap(): return lax.ppermute(value, axis, [(i, i ^ bit) for i in range(sizes[axis])])  31 us
    unnamed x45, local copies, waits for them, and re-layouts  10.4 us
    concatenate x5, other arithmetic, grow(): return jnp.concatenate([held, got], axis=0)  3.21 us
    reshape x2, local copies, waits for them, and re-layouts, padded(): return jnp.pad(v.reshape(images, SEQ, D), ((0, 0), (0, PAD - SEQ), (0, 0)))  3.04 us
  transfers between devices with their start and end apart: 29, of which 12 were waited for; matrix products, arithmetic and copies ran while one was open for 8% of the time, Pallas kernels for 11%

profile of v4, /device:TPU:0, one launch (start us, length us, event | category | flops | bytes accessed | tf_op | source)
XLA Modules:
  0.0 137.1 jit_solution(6841972658253323994)
XLA Ops:
  0.6 1.6 %shard_map.143 = (bf16[1,24,640]{2,1,0:T(8,128)(2,1)}, bf16[1,24,1792]{2,1,0:T(8,128)(2,1)}) custom-call(bf16[3,24,192]{2,1,0:T(8,128)(2,1)} %bitcast.14, f32[1,24]{1,0:T(1,128)} %bitcast.10, f32[1,24]{1,0:T(1,128)} %bitcast.12, bf16[24,192]{1,0:T(8,128)(2,1)} %bitcast.16, bf16[24,768]{1,0:T(8,128)(2,1)} %fc1.1, bf16[24,768]{1,0:T(8,128)(2,1)} %bitcast.15), custom_call_target="tpu_custom_call" | custom-call | tf_op jit(solution)/shard_map/pallas_call | solution.py:456
  2.3 4.1 %collective-permute-start.10 = (bf16[1,24,640]{2,1,0:T(8,128)(2,1)}, bf16[1,24,640]{2,1,0:T(8,128)(2,1)S(1)}, u32[]{:S(2)}, u32[]{:S(2)}) collective-permute-start(bf16[1,24,640]{2,1,0:T(8,128)(2,1)} %get-tuple-element.33), channel_id=1, source_target_pairs={{0,16},{2,18},{4,20},{6,22},{8,24},{10,26},{12,28},{14,30},{16,0},... | collective-permute-start | bytes 92168 | tf_op jit(solution)/shard_map/ppermute | solution.py:44
  9.5 2.5 %collective-permute-start.11 = (bf16[2,24,640]{2,1,0:T(8,128)(2,1)S(1)}, bf16[2,24,640]{2,1,0:T(8,128)(2,1)S(1)}, u32[]{:S(2)}, u32[]{:S(2)}) collective-permute-start(bf16[2,24,640]{2,1,0:T(8,128)(2,1)S(1)} %pad_maximum_fusion.5), channel_id=1, source_target_pairs={{0,8},{2,10},{4,12},{6,14},{8,0},{10,2},{12,4},{14,6},{16,24},{18,... | collective-permute-start | bytes 184328 | tf_op jit(solution)/shard_map/ppermute | solution.py:44
  12.0 1.6 %collective-permute-done = bf16[1,24,1792]{2,1,0:T(8,128)(2,1)S(1)} collective-permute-done((bf16[1,24,1792]{2,1,0:T(8,128)(2,1)}, bf16[1,24,1792]{2,1,0:T(8,128)(2,1)S(1)}, u32[]{:S(2)}, u32[]{:S(2)}) %collective-permute-start) | collective-permute-done | bytes 86048 | tf_op jit(solution)/shard_map/ppermute | solution.py:44
  15.3 1.6 %collective-permute-start.12 = (bf16[4,24,640]{2,1,0:T(8,128)(2,1)S(1)}, bf16[4,24,640]{2,1,0:T(8,128)(2,1)S(1)}, u32[]{:S(2)}, u32[]{:S(2)}) collective-permute-start(bf16[4,24,640]{2,1,0:T(8,128)(2,1)S(1)} %pad_maximum_fusion.4), channel_id=1, source_target_pairs={{0,4},{2,6},{4,0},{6,2},{8,12},{10,14},{12,8},{14,10},{16,20},{18,... | collective-permute-start | bytes 368648 | tf_op jit(solution)/shard_map/ppermute | solution.py:44
  16.9 3.0 %collective-permute-done.1 = bf16[2,24,1792]{2,1,0:T(8,128)(2,1)S(1)} collective-permute-done((bf16[2,24,1792]{2,1,0:T(8,128)(2,1)S(1)}, bf16[2,24,1792]{2,1,0:T(8,128)(2,1)S(1)}, u32[]{:S(2)}, u32[]{:S(2)}) %collective-permute-start.1) | collective-permute-done | bytes 172064 | tf_op jit(solution)/shard_map/ppermute | solution.py:44
  20.0 1.6 %collective-permute-start.2 = (bf16[4,24,1024]{2,1,0:T(8,128)(2,1)S(1)}, bf16[4,24,1024]{2,1,0:T(8,128)(2,1)S(1)}, u32[]{:S(2)}, u32[]{:S(2)}) collective-permute-start(bf16[4,24,1024]{2,1,0:T(8,128)(2,1)S(1)} %slice.80), channel_id=1, source_target_pairs={{0,1},{1,0},{2,3},{3,2},{4,5},{5,4},{6,7},{7,6},{8,9},{9,8},{10,11... | collective-permute-start | bytes 589832 | tf_op jit(solution)/shard_map/ppermute | solution.py:44
  21.6 1.6 %collective-permute-start.6 = (bf16[4,24,768]{2,1,0:T(8,128)(2,1)S(1)}, bf16[4,24,768]{2,1,0:T(8,128)(2,1)S(1)}, u32[]{:S(2)}, u32[]{:S(2)}) collective-permute-start(bf16[4,24,768]{2,1,0:T(8,128)(2,1)S(1)} %slice.81), channel_id=1, source_target_pairs={{0,4},{2,6},{4,0},{6,2},{8,12},{10,14},{12,8},{14,10},{16,20},{18,... | collective-permute-start | bytes 442376 | tf_op jit(solution)/shard_map/ppermute | solution.py:44
  23.7 3.7 %collective-permute-done.2 = bf16[4,24,1024]{2,1,0:T(8,128)(2,1)S(1)} collective-permute-done((bf16[4,24,1024]{2,1,0:T(8,128)(2,1)S(1)}, bf16[4,24,1024]{2,1,0:T(8,128)(2,1)S(1)}, u32[]{:S(2)}, u32[]{:S(2)}) %collective-permute-start.2) | collective-permute-done | bytes 196640 | tf_op jit(solution)/shard_map/ppermute | solution.py:44
  27.5 1.4 collective-permute-start.3
  29.6 2.0 %collective-permute-start.7 = (bf16[8,24,768]{2,1,0:T(8,128)(2,1)}, bf16[8,24,768]{2,1,0:T(8,128)(2,1)}, u32[]{:S(2)}, u32[]{:S(2)}) collective-permute-start(bf16[8,24,768]{2,1,0:T(8,128)(2,1)} %pad_maximum_fusion.1.r0), channel_id=1, source_target_pairs={{0,1},{1,0},{2,3},{3,2},{4,5},{5,4},{6,7},{7,6},{8,9},{9,8},{10,11... | collective-permute-start | bytes 884744 | tf_op jit(solution)/shard_map/ppermute | solution.py:44
  32.7 1.4 %reshape.36 = bf16[8,197,384]{2,1,0:T(8,128)(2,1)} reshape(bf16[1576,384]{1,0:T(8,128)(2,1)S(1)} %copy-done.19) | data formatting | bytes 2420736 | tf_op jit(solution)/shard_map/reshape | solution.py:473
  34.1 1.6 %reshape.37 = bf16[8,197,384]{2,1,0:T(8,128)(2,1)S(1)} reshape(bf16[1576,384]{1,0:T(8,128)(2,1)} %param.15) | data formatting | bytes 2420736 | tf_op jit(solution)/shard_map/reshape | solution.py:473
  35.7 1.4 %pad.7.x_ref.refs_3_ = bf16[8,208,384]{2,1,0:T(8,128)(2,1)S(1)} pad(bf16[8,197,384]{2,1,0:T(8,128)(2,1)} %reshape.36, bf16[]{:T(256)} %constant.2.clone.1), padding=0_0x0_11x0_0 | pad | bytes 2488322 | tf_op jit(solution)/shard_map/jit(_pad)/pad | solution.py:473
  41.8 9.6 %shard_map.144 = (bf16[8,208,1152]{2,1,0:T(8,128)(2,1)S(1)}, bf16[8,3,208,512]{3,2,1,0:T(8,128)(2,1)S(1)}, bf16[8,208,384]{2,1,0:T(8,128)(2,1)S(1)}, bf16[8,208,...) custom-call(bf16[8,24,640]{2,1,0:T(8,128)(2,1)S(1)} %copy-done.9, ...), custom_call_target="tpu_custom_call" | custom-call | flops 8000000000 | bytes 20000000 | tf_op jit(solution)/shard_map/pallas_call | solution.py:456
  53.5 25.5 %shard_map.145 = (bf16[1576,384]{1,0:T(8,128)(2,1)}, f32[8,208,384]{2,1,0:T(8,128)}, bf16[8,208,384]{2,1,0:T(8,128)(2,1)S(1)}, bf16[16,24,1024]{2,1,0:T(8,128)(2...) custom-call(bf16[8,24,1024]{2,1,0:T(8,128)(2,1)S(1)} %pad_maximum_fus, ...), custom_call_target="tpu_custom_call" | custom-call | flops 16000000000 | bytes 30000000 | tf_op jit(solution)/shard_map/pallas_call | solution.py:456
  81.0 1.3 copy-done.4
  82.3 3.6 %shard_map.146.refs_0_ = bf16[4,208,1152]{2,1,0:T(8,128)(2,1)S(1)} custom-call(bf16[8,208,1152]{2,1,0:T(8,128)(2,1)S(1)} %get-tuple-element.37.qkv_ref, bf16[8,3,208,512]{3,2,1,0:T(8,128)(2,1)S(1)} %get-tuple-element.38.probs_ref, bf16[8,208,384]{2,1,0:T(8,128)(2,1)S(1)} %copy-done.4), custom_call_target="tpu_custom_call" | custom-call | flops 3600000000 | bytes 8000000 | tf_op jit(solution)/shard_map/pallas_call | solution.py:456
  85.9 5.9 %shard_map.147 = (bf16[4,208,1152]{2,1,0:T(8,128)(2,1)S(1)}, bf16[16,24,640]{2,1,0:T(8,128)(2,1)S(1)}, bf16[16,24,640]{2,1,0:T(8,128)(2,1)S(1)}) custom-call(bf16[8,208,1152]{2,1,0:T(8,128)(2,1)S(1)} %get-tuple-element.37.qkv_ref, bf16[8,3,208,512]{3,2,1,0:T(8,128)(2,1)S(1)} %get-tuple-element.38.probs_ref, bf16[8,208,384]{2,1,0:T(8,128)(2,1)S(1)} %copy-done.5, ...), custom_call_target="tpu_custom_call" | custom-call | flops 3500000000 | bytes 8000000 | tf_op jit(solution)/shard_map/pallas_call | solution.py:456
  95.1 1.8 %collective-permute-start.25 = (bf16[8,24,768]{2,1,0:T(8,128)(2,1)S(1)}, bf16[8,24,768]{2,1,0:T(8,128)(2,1)S(1)}, u32[]{:S(2)}, u32[]{:S(2)}) collective-permute-start(bf16[8,24,768]{2,1,0:T(8,128)(2,1)S(1)} %slice.94), channel_id=1, source_target_pairs={{0,4},{2,6},{4,0},{6,2},{8,12},{10,14},{12,8},{14,10},{16,20},{18,... | collective-permute-start | bytes 884744 | tf_op jit(solution)/shard_map/ppermute | solution.py:44
  97.0 5.3 %collective-permute-done.17 = bf16[8,24,640]{2,1,0:T(8,128)(2,1)S(1)} collective-permute-done((bf16[8,24,640]{2,1,0:T(8,128)(2,1)S(1)}, bf16[8,24,640]{2,1,0:T(8,128)(2,1)S(1)}, u32[]{:S(2)}, u32[]{:S(2)}) %collective-permute-start.17) | collective-permute-done | bytes 245792 | tf_op jit(solution)/shard_map/ppermute | solution.py:44
  102.4 1.2 collective-permute-start.18
  103.9 1.6 %collective-permute-start.22 = (bf16[8,24,1024]{2,1,0:T(8,128)(2,1)S(1)}, bf16[8,24,1024]{2,1,0:T(8,128)(2,1)S(1)}, u32[]{:S(2)}, u32[]{:S(2)}) collective-permute-start(bf16[8,24,1024]{2,1,0:T(8,128)(2,1)S(1)} %slice.90), channel_id=1, source_target_pairs={{0,1},{1,0},{2,3},{3,2},{4,5},{5,4},{6,7},{7,6},{8,9},{9,8},{10,11... | collective-permute-start | bytes 1179656 | tf_op jit(solution)/shard_map/ppermute | solution.py:44
  105.5 1.8 %collective-permute-done.18 = bf16[4,24,640]{2,1,0:T(8,128)(2,1)S(1)} collective-permute-done((bf16[4,24,640]{2,1,0:T(8,128)(2,1)S(1)}, bf16[4,24,640]{2,1,0:T(8,128)(2,1)S(1)}, u32[]{:S(2)}, u32[]{:S(2)}) %collective-permute-start.18) | collective-permute-done | bytes 122912 | tf_op jit(solution)/shard_map/ppermute | solution.py:44
  108.5 1.4 %collective-permute-start.26 = (bf16[4,24,768]{2,1,0:T(8,128)(2,1)S(1)}, bf16[4,24,768]{2,1,0:T(8,128)(2,1)S(1)}, u32[]{:S(2)}, u32[]{:S(2)}) collective-permute-start(bf16[4,24,768]{2,1,0:T(8,128)(2,1)S(1)} %slice.96), channel_id=1, source_target_pairs={{0,1},{1,0},{2,3},{3,2},{4,5},{5,4},{6,7},{7,6},{8,9},{9,8},{10,11... | collective-permute-start | bytes 442376 | tf_op jit(solution)/shard_map/ppermute | solution.py:44
  109.9 5.9 %collective-permute-done.22 = bf16[8,24,1024]{2,1,0:T(8,128)(2,1)S(1)} collective-permute-done((bf16[8,24,1024]{2,1,0:T(8,128)(2,1)S(1)}, bf16[8,24,1024]{2,1,0:T(8,128)(2,1)S(1)}, u32[]{:S(2)}, u32[]{:S(2)}) %collective-permute-start.22) | collective-permute-done | bytes 393248 | tf_op jit(solution)/shard_map/ppermute | solution.py:44
  117.4 4.3 %collective-permute-done.23 = bf16[4,24,1024]{2,1,0:T(8,128)(2,1)S(1)} collective-permute-done((bf16[4,24,1024]{2,1,0:T(8,128)(2,1)S(1)}, bf16[4,24,1024]{2,1,0:T(8,128)(2,1)S(1)}, u32[]{:S(2)}, u32[]{:S(2)}) %collective-permute-start.23) | collective-permute-done | bytes 196640 | tf_op jit(solution)/shard_map/ppermute | solution.py:44
  121.8 1.2 collective-permute-start.27
  123.0 3.4 %collective-permute-start.20 = (bf16[1,24,640]{2,1,0:T(8,128)(2,1)S(1)}, bf16[1,24,640]{2,1,0:T(8,128)(2,1)S(1)}, u32[]{:S(2)}, u32[]{:S(2)}) collective-permute-start(bf16[1,24,640]{2,1,0:T(8,128)(2,1)S(1)} %slice.88), channel_id=1, source_target_pairs={{0,16},{2,18},{4,20},{6,22},{8,24},{10,26},{12,28},{14,30},{16,0},... | collective-permute-start | bytes 92168 | tf_op jit(solution)/shard_map/ppermute | solution.py:44
  126.4 2.1 %collective-permute-done.27 = bf16[2,24,1792]{2,1,0:T(8,128)(2,1)S(1)} collective-permute-done((bf16[2,24,1792]{2,1,0:T(8,128)(2,1)S(1)}, bf16[2,24,1792]{2,1,0:T(8,128)(2,1)S(1)}, u32[]{:S(2)}, u32[]{:S(2)}) %collective-permute-start.27) | collective-permute-done | bytes 172064 | tf_op jit(solution)/shard_map/ppermute | solution.py:44
  128.6 2.1 %collective-permute-start.28 = (bf16[1,24,1792]{2,1,0:T(8,128)(2,1)S(1)}, bf16[1,24,1792]{2,1,0:T(8,128)(2,1)S(1)}, u32[]{:S(2)}, u32[]{:S(2)}) collective-permute-start(bf16[1,24,1792]{2,1,0:T(8,128)(2,1)S(1)} %slice.99), channel_id=1, source_target_pairs={{0,16},{2,18},{4,20},{6,22},{8,24},{10,26},{12,28},{14,30},{16,0},... | collective-permute-start | bytes 258056 | tf_op jit(solution)/shard_map/ppermute | solution.py:44
  130.7 5.7 %shard_map.148 = f32[1576,384]{1,0:T(8,128)} custom-call(bf16[4,208,1152]{2,1,0:T(8,128)(2,1)S(1)} %shard_map.146.refs_0_, bf16[4,208,1152]{2,1,0:T(8,128)(2,1)S(1)} %get-tuple-element.42.refs_1_, bf16[384,1152]{1,0:T(8,128)(2,1)S(1)} %get-tuple-element.41.w_ref.refs_2_, bf16[8,208,384]{2,1,0:T(8,128)(2,1)S(1)} %pad.7.x_ref.refs_3_, ...), custom_call_target="tpu_custom_call" | custom-call | flops 2000000000 | bytes 10000000 | tf_op jit(solution)/shard_map/pallas_call | solution.py:456
  (112 shorter events, 23.4 us)
Async XLA Ops:
  2.3 6.5 %collective-permute-start.10 = (bf16[1,24,640]{2,1,0:T(8,128)(2,1)}, bf16[1,24,640]{2,1,0:T(8,128)(2,1)S(1)}, u32[]{:S(2)}, u32[]{:S(2)}) collective-permute-start(bf16[1,24,640]{2,1,0:T(8,128)(2,1)} %get-tuple-element.33), channel_id=1, source_target_pairs={{0,16},{2,18},{4,20},{6,22},{8,24},{10,26},{12,28},{14,30},{16,0},... | collective-permute-start | bytes 92168 | tf_op jit(solution)/shard_map/ppermute | solution.py:44
  6.3 7.2 %collective-permute-start = (bf16[1,24,1792]{2,1,0:T(8,128)(2,1)}, bf16[1,24,1792]{2,1,0:T(8,128)(2,1)S(1)}, u32[]{:S(2)}, u32[]{:S(2)}) collective-permute-start(bf16[1,24,1792]{2,1,0:T(8,128)(2,1)} %get-tuple-element.32), channel_id=1, source_target_pairs={{0,16},{2,18},{4,20},{6,22},{8,24},{10,26},{12,28},{14,30},{16,0},... | collective-permute-start | bytes 258056 | tf_op jit(solution)/shard_map/ppermute | solution.py:44
  9.5 5.0 %collective-permute-start.11 = (bf16[2,24,640]{2,1,0:T(8,128)(2,1)S(1)}, bf16[2,24,640]{2,1,0:T(8,128)(2,1)S(1)}, u32[]{:S(2)}, u32[]{:S(2)}) collective-permute-start(bf16[2,24,640]{2,1,0:T(8,128)(2,1)S(1)} %pad_maximum_fusion.5), channel_id=1, source_target_pairs={{0,8},{2,10},{4,12},{6,14},{8,0},{10,2},{12,4},{14,6},{16,24},{18,... | collective-permute-start | bytes 184328 | tf_op jit(solution)/shard_map/ppermute | solution.py:44
  14.4 5.5 %collective-permute-start.1 = (bf16[2,24,1792]{2,1,0:T(8,128)(2,1)S(1)}, bf16[2,24,1792]{2,1,0:T(8,128)(2,1)S(1)}, u32[]{:S(2)}, u32[]{:S(2)}) collective-permute-start(bf16[2,24,1792]{2,1,0:T(8,128)(2,1)S(1)} %pad_maximum_fusion.3), channel_id=1, source_target_pairs={{0,8},{2,10},{4,12},{6,14},{8,0},{10,2},{12,4},{14,6},{16,24},{18,... | collective-permute-start | bytes 516104 | tf_op jit(solution)/shard_map/ppermute | solution.py:44
  15.3 7.8 %collective-permute-start.12 = (bf16[4,24,640]{2,1,0:T(8,128)(2,1)S(1)}, bf16[4,24,640]{2,1,0:T(8,128)(2,1)S(1)}, u32[]{:S(2)}, u32[]{:S(2)}) collective-permute-start(bf16[4,24,640]{2,1,0:T(8,128)(2,1)S(1)} %pad_maximum_fusion.4), channel_id=1, source_target_pairs={{0,4},{2,6},{4,0},{6,2},{8,12},{10,14},{12,8},{14,10},{16,20},{18,... | collective-permute-start | bytes 368648 | tf_op jit(solution)/shard_map/ppermute | solution.py:44
  19.9 12.7 %copy-start.19 = (bf16[1576,384]{1,0:T(8,128)(2,1)S(1)}, bf16[1576,384]{1,0:T(8,128)(2,1)}, u32[]{:S(2)}) copy-start(bf16[1576,384]{1,0:T(8,128)(2,1)} %param.8) | copy-start | bytes 3631108
  20.0 7.5 %collective-permute-start.2 = (bf16[4,24,1024]{2,1,0:T(8,128)(2,1)S(1)}, bf16[4,24,1024]{2,1,0:T(8,128)(2,1)S(1)}, u32[]{:S(2)}, u32[]{:S(2)}) collective-permute-start(bf16[4,24,1024]{2,1,0:T(8,128)(2,1)S(1)} %slice.80), channel_id=1, source_target_pairs={{0,1},{1,0},{2,3},{3,2},{4,5},{5,4},{6,7},{7,6},{8,9},{9,8},{10,11... | collective-permute-start | bytes 589832 | tf_op jit(solution)/shard_map/ppermute | solution.py:44
  21.6 7.3 %collective-permute-start.6 = (bf16[4,24,768]{2,1,0:T(8,128)(2,1)S(1)}, bf16[4,24,768]{2,1,0:T(8,128)(2,1)S(1)}, u32[]{:S(2)}, u32[]{:S(2)}) collective-permute-start(bf16[4,24,768]{2,1,0:T(8,128)(2,1)S(1)} %slice.81), channel_id=1, source_target_pairs={{0,4},{2,6},{4,0},{6,2},{8,12},{10,14},{12,8},{14,10},{16,20},{18,... | collective-permute-start | bytes 442376 | tf_op jit(solution)/shard_map/ppermute | solution.py:44
  23.2 10.9 %copy-start.8 = (bf16[8,24,640]{2,1,0:T(8,128)(2,1)}, bf16[8,24,640]{2,1,0:T(8,128)(2,1)S(1)}, u32[]{:S(2)}) copy-start(bf16[8,24,640]{2,1,0:T(8,128)(2,1)S(1)} %constant_dynamic-update-slice_fusion.3.p0) | copy-start | bytes 737284
  23.2 9.5 %collective-permute-start.13 = (bf16[8,24,640]{2,1,0:T(8,128)(2,1)S(1)}, bf16[8,24,640]{2,1,0:T(8,128)(2,1)S(1)}, u32[]{:S(2)}, u32[]{:S(2)}) collective-permute-start(bf16[8,24,640]{2,1,0:T(8,128)(2,1)S(1)} %constant_dynamic-update-slice_fusion.3.p0), channel_id=1, source_target_pairs={{0,1},{1,0},{2,3},{3,2},{4,5},{5,4},{6,7},{7,6},{8,9},{9,8},{10,11... | collective-permute-start | bytes 737288 | tf_op jit(solution)/shard_map/ppermute | solution.py:44
  27.5 11.6 %collective-permute-start.3 = (bf16[8,24,1024]{2,1,0:T(8,128)(2,1)S(1)}, bf16[8,24,1024]{2,1,0:T(8,128)(2,1)}, u32[]{:S(2)}, u32[]{:S(2)}) collective-permute-start(bf16[8,24,1024]{2,1,0:T(8,128)(2,1)S(1)} %pad_maximum_fusion.p0), channel_id=1, source_target_pairs={{0,4},{2,6},{4,0},{6,2},{8,12},{10,14},{12,8},{14,10},{16,20},{18,... | collective-permute-start | bytes 1179656 | tf_op jit(solution)/shard_map/ppermute | solution.py:44
  29.6 9.0 %collective-permute-start.7 = (bf16[8,24,768]{2,1,0:T(8,128)(2,1)}, bf16[8,24,768]{2,1,0:T(8,128)(2,1)}, u32[]{:S(2)}, u32[]{:S(2)}) collective-permute-start(bf16[8,24,768]{2,1,0:T(8,128)(2,1)} %pad_maximum_fusion.1.r0), channel_id=1, source_target_pairs={{0,1},{1,0},{2,3},{3,2},{4,5},{5,4},{6,7},{7,6},{8,9},{9,8},{10,11... | collective-permute-start | bytes 884744 | tf_op jit(solution)/shard_map/ppermute | solution.py:44
  31.6 6.3 %collective-permute-start.14 = (bf16[8,24,640]{2,1,0:T(8,128)(2,1)S(1)}, bf16[8,24,640]{2,1,0:T(8,128)(2,1)S(1)}, u32[]{:S(2)}, u32[]{:S(2)}) collective-permute-start(bf16[8,24,640]{2,1,0:T(8,128)(2,1)S(1)} %constant_dynamic-update-slice_fusion.3.p0), channel_id=1, source_target_pairs={{0,2},{2,0},{4,6},{6,4},{8,10},{10,8},{12,14},{14,12},{16,18},{18,... | collective-permute-start | bytes 737288 | tf_op jit(solution)/shard_map/ppermute | solution.py:44
  32.7 6.5 %collective-permute-start.15 = (bf16[8,24,640]{2,1,0:T(8,128)(2,1)S(1)}, bf16[8,24,640]{2,1,0:T(8,128)(2,1)S(1)}, u32[]{:S(2)}, u32[]{:S(2)}) collective-permute-start(bf16[8,24,640]{2,1,0:T(8,128)(2,1)S(1)} %collective-permute-done.13.p1), channel_id=1, source_target_pairs={{0,2},{2,0},{4,6},{6,4},{8,10},{10,8},{12,14},{14,12},{16,18},{18,... | collective-permute-start | bytes 737288 | tf_op jit(solution)/shard_map/ppermute | solution.py:44
  37.3 16.2 %collective-permute-start.8 = (bf16[8,24,768]{2,1,0:T(8,128)(2,1)}, bf16[8,24,768]{2,1,0:T(8,128)(2,1)S(1)}, u32[]{:S(2)}, u32[]{:S(2)}) collective-permute-start(bf16[8,24,768]{2,1,0:T(8,128)(2,1)} %pad_maximum_fusion.1.r0), channel_id=1, source_target_pairs={{0,2},{2,0},{4,6},{6,4},{8,10},{10,8},{12,14},{14,12},{16,18},{18,... | collective-permute-start | bytes 884744 | tf_op jit(solution)/shard_map/ppermute | solution.py:44
  38.6 14.9 %collective-permute-start.4 = (bf16[8,24,1024]{2,1,0:T(8,128)(2,1)S(1)}, bf16[8,24,1024]{2,1,0:T(8,128)(2,1)S(1)}, u32[]{:S(2)}, u32[]{:S(2)}) collective-permute-start(bf16[8,24,1024]{2,1,0:T(8,128)(2,1)S(1)} %pad_maximum_fusion.p0), channel_id=1, source_target_pairs={{0,2},{2,0},{4,6},{6,4},{8,10},{10,8},{12,14},{14,12},{16,18},{18,... | collective-permute-start | bytes 1179656 | tf_op jit(solution)/shard_map/ppermute | solution.py:44
  38.6 14.9 %collective-permute-start.9 = (bf16[8,24,768]{2,1,0:T(8,128)(2,1)}, bf16[8,24,768]{2,1,0:T(8,128)(2,1)S(1)}, u32[]{:S(2)}, u32[]{:S(2)}) collective-permute-start(bf16[8,24,768]{2,1,0:T(8,128)(2,1)} %collective-permute-done.7.r1), channel_id=1, source_target_pairs={{0,2},{2,0},{4,6},{6,4},{8,10},{10,8},{12,14},{14,12},{16,18},{18,... | collective-permute-start | bytes 884744 | tf_op jit(solution)/shard_map/ppermute | solution.py:44
  39.1 14.4 %collective-permute-start.5 = (bf16[8,24,1024]{2,1,0:T(8,128)(2,1)}, bf16[8,24,1024]{2,1,0:T(8,128)(2,1)S(1)}, u32[]{:S(2)}, u32[]{:S(2)}) collective-permute-start(bf16[8,24,1024]{2,1,0:T(8,128)(2,1)} %collective-permute-done.3.p1), channel_id=1, source_target_pairs={{0,2},{2,0},{4,6},{6,4},{8,10},{10,8},{12,14},{14,12},{16,18},{18,... | collective-permute-start | bytes 1179656 | tf_op jit(solution)/shard_map/ppermute | solution.py:44
  91.8 2.0 %collective-permute-start.16 = (bf16[16,24,640]{2,1,0:T(8,128)(2,1)S(1)}, bf16[16,24,640]{2,1,0:T(8,128)(2,1)S(1)}, u32[]{:S(2)}, u32[]{:S(2)}) collective-permute-start(bf16[16,24,640]{2,1,0:T(8,128)(2,1)S(1)} %get-tuple-element.45), channel_id=1, source_target_pairs={{0,2},{2,0},{4,6},{6,4},{8,10},{10,8},{12,14},{14,12},{16,18},{18,... | collective-permute-start | bytes 1474568 | tf_op jit(solution)/shard_map/ppermute | solution.py:44
  92.3 2.6 %collective-permute-start.24 = (bf16[16,24,768]{2,1,0:T(8,128)(2,1)S(1)}, bf16[16,24,768]{2,1,0:T(8,128)(2,1)S(1)}, u32[]{:S(2)}, u32[]{:S(2)}) collective-permute-start(bf16[16,24,768]{2,1,0:T(8,128)(2,1)S(1)} %get-tuple-element.49), channel_id=1, source_target_pairs={{0,2},{2,0},{4,6},{6,4},{8,10},{10,8},{12,14},{14,12},{16,18},{18,... | collective-permute-start | bytes 1769480 | tf_op jit(solution)/shard_map/ppermute | solution.py:44
  92.4 11.2 %collective-permute-start.21 = (bf16[16,24,1024]{2,1,0:T(8,128)(2,1)S(1)}, bf16[16,24,1024]{2,1,0:T(8,128)(2,1)S(1)}, u32[]{:S(2)}, u32[]{:S(2)}) collective-permute-start(bf16[16,24,1024]{2,1,0:T(8,128)(2,1)S(1)} %get-tuple-element.47), channel_id=1, source_target_pairs={{0,2},{2,0},{4,6},{6,4},{8,10},{10,8},{12,14},{14,12},{16,18},{18,... | collective-permute-start | bytes 2359304 | tf_op jit(solution)/shard_map/ppermute | solution.py:44
  94.0 8.3 %collective-permute-start.17 = (bf16[8,24,640]{2,1,0:T(8,128)(2,1)S(1)}, bf16[8,24,640]{2,1,0:T(8,128)(2,1)S(1)}, u32[]{:S(2)}, u32[]{:S(2)}) collective-permute-start(bf16[8,24,640]{2,1,0:T(8,128)(2,1)S(1)} %slice.83), channel_id=1, source_target_pairs={{0,1},{1,0},{2,3},{3,2},{4,5},{5,4},{6,7},{7,6},{8,9},{9,8},{10,11... | collective-permute-start | bytes 737288 | tf_op jit(solution)/shard_map/ppermute | solution.py:44
  95.1 13.3 %collective-permute-start.25 = (bf16[8,24,768]{2,1,0:T(8,128)(2,1)S(1)}, bf16[8,24,768]{2,1,0:T(8,128)(2,1)S(1)}, u32[]{:S(2)}, u32[]{:S(2)}) collective-permute-start(bf16[8,24,768]{2,1,0:T(8,128)(2,1)S(1)} %slice.94), channel_id=1, source_target_pairs={{0,4},{2,6},{4,0},{6,2},{8,12},{10,14},{12,8},{14,10},{16,20},{18,... | collective-permute-start | bytes 884744 | tf_op jit(solution)/shard_map/ppermute | solution.py:44
  102.4 4.9 %collective-permute-start.18 = (bf16[4,24,640]{2,1,0:T(8,128)(2,1)S(1)}, bf16[4,24,640]{2,1,0:T(8,128)(2,1)S(1)}, u32[]{:S(2)}, u32[]{:S(2)}) collective-permute-start(bf16[4,24,640]{2,1,0:T(8,128)(2,1)S(1)} %slice.85), channel_id=1, source_target_pairs={{0,4},{2,6},{4,0},{6,2},{8,12},{10,14},{12,8},{14,10},{16,20},{18,... | collective-permute-start | bytes 368648 | tf_op jit(solution)/shard_map/ppermute | solution.py:44
  103.9 11.9 %collective-permute-start.22 = (bf16[8,24,1024]{2,1,0:T(8,128)(2,1)S(1)}, bf16[8,24,1024]{2,1,0:T(8,128)(2,1)S(1)}, u32[]{:S(2)}, u32[]{:S(2)}) collective-permute-start(bf16[8,24,1024]{2,1,0:T(8,128)(2,1)S(1)} %slice.90), channel_id=1, source_target_pairs={{0,1},{1,0},{2,3},{3,2},{4,5},{5,4},{6,7},{7,6},{8,9},{9,8},{10,11... | collective-permute-start | bytes 1179656 | tf_op jit(solution)/shard_map/ppermute | solution.py:44
  107.4 15.7 %collective-permute-start.19 = (bf16[2,24,640]{2,1,0:T(8,128)(2,1)S(1)}, bf16[2,24,640]{2,1,0:T(8,128)(2,1)S(1)}, u32[]{:S(2)}, u32[]{:S(2)}) collective-permute-start(bf16[2,24,640]{2,1,0:T(8,128)(2,1)S(1)} %slice.87), channel_id=1, source_target_pairs={{0,8},{2,10},{4,12},{6,14},{8,0},{10,2},{12,4},{14,6},{16,24},{18,... | collective-permute-start | bytes 184328 | tf_op jit(solution)/shard_map/ppermute | solution.py:44
  108.5 8.9 %collective-permute-start.26 = (bf16[4,24,768]{2,1,0:T(8,128)(2,1)S(1)}, bf16[4,24,768]{2,1,0:T(8,128)(2,1)S(1)}, u32[]{:S(2)}, u32[]{:S(2)}) collective-permute-start(bf16[4,24,768]{2,1,0:T(8,128)(2,1)S(1)} %slice.96), channel_id=1, source_target_pairs={{0,1},{1,0},{2,3},{3,2},{4,5},{5,4},{6,7},{7,6},{8,9},{9,8},{10,11... | collective-permute-start | bytes 442376 | tf_op jit(solution)/shard_map/ppermute | solution.py:44
  116.0 14.7 %copy-start = (f32[8,208,384]{2,1,0:T(8,128)S(1)}, f32[8,208,384]{2,1,0:T(8,128)}, u32[]{:S(2)}) copy-start(f32[8,208,384]{2,1,0:T(8,128)} %get-tuple-element.43.refs_4_) | copy-start | bytes 7667716
  116.0 5.7 %collective-permute-start.23 = (bf16[4,24,1024]{2,1,0:T(8,128)(2,1)S(1)}, bf16[4,24,1024]{2,1,0:T(8,128)(2,1)S(1)}, u32[]{:S(2)}, u32[]{:S(2)}) collective-permute-start(bf16[4,24,1024]{2,1,0:T(8,128)(2,1)S(1)} %slice.92), channel_id=1, source_target_pairs={{0,4},{2,6},{4,0},{6,2},{8,12},{10,14},{12,8},{14,10},{16,20},{18,... | collective-permute-start | bytes 589832 | tf_op jit(solution)/shard_map/ppermute | solution.py:44
  121.8 6.7 %collective-permute-start.27 = (bf16[2,24,1792]{2,1,0:T(8,128)(2,1)S(1)}, bf16[2,24,1792]{2,1,0:T(8,128)(2,1)S(1)}, u32[]{:S(2)}, u32[]{:S(2)}) collective-permute-start(bf16[2,24,1792]{2,1,0:T(8,128)(2,1)S(1)} %pad_maximum_fusion.2), channel_id=1, source_target_pairs={{0,8},{2,10},{4,12},{6,14},{8,0},{10,2},{12,4},{14,6},{16,24},{18,... | collective-permute-start | bytes 516104 | tf_op jit(solution)/shard_map/ppermute | solution.py:44
  123.0 13.3 %collective-permute-start.20 = (bf16[1,24,640]{2,1,0:T(8,128)(2,1)S(1)}, bf16[1,24,640]{2,1,0:T(8,128)(2,1)S(1)}, u32[]{:S(2)}, u32[]{:S(2)}) collective-permute-start(bf16[1,24,640]{2,1,0:T(8,128)(2,1)S(1)} %slice.88), channel_id=1, source_target_pairs={{0,16},{2,18},{4,20},{6,22},{8,24},{10,26},{12,28},{14,30},{16,0},... | collective-permute-start | bytes 92168 | tf_op jit(solution)/shard_map/ppermute | solution.py:44
  128.6 7.8 %collective-permute-start.28 = (bf16[1,24,1792]{2,1,0:T(8,128)(2,1)S(1)}, bf16[1,24,1792]{2,1,0:T(8,128)(2,1)S(1)}, u32[]{:S(2)}, u32[]{:S(2)}) collective-permute-start(bf16[1,24,1792]{2,1,0:T(8,128)(2,1)S(1)} %slice.99), channel_id=1, source_target_pairs={{0,16},{2,18},{4,20},{6,22},{8,24},{10,26},{12,28},{14,30},{16,0},... | collective-permute-start | bytes 258056 | tf_op jit(solution)/shard_map/ppermute | solution.py:44
  (17 other events, 44.4 us)

commit v5 on v4

--- a/solution.py
+++ b/solution.py
@@ -225,7 +225,7 @@
 def mlp_kernel(
     places, places2, rows, blocks, fs, p0, p1, p2, p3, r0, r1, r2, r3, x_ref, og_ref, h_ref, gain_ref,
     y_ref, mg_ref, hg_ref, keep1, send1, keep2, send2,
-    scr, w_out, w_back, w_fc1, w_fc1_turned, fc2_ref, w_fc2_turned, n2_all, pg_all, hid_all, og_all, ml_all, h_all, y_all,
+    scr, w_out, w_back, w_fc1, w_fc1_turned, fc2_ref, w_fc2_turned, n2_all, pg_all, hid_all, og_all, ml_all, h_all,
 ):
     step = pl.program_id(0)
 
@@ -283,10 +283,10 @@
             part = dot(pg, w_fc1_turned[cols, :])
             back = part if back is None else back + part
             middle += dot(hid, w_fc2_turned[cols, :])
-        store_rows(y_all, middle, step, blocks)
+        store_rows(y_ref, middle.astype(BF16), step, blocks)
         mg = og.astype(F32) + norm_back(back, xhat, rstd, gain)
-        mg_ref[...] = mg.reshape(PER, PAD, D)
         ml = mg.astype(BF16)
+        mg_ref[...] = ml.reshape(PER, PAD, D)
         ml_all[at, :] = ml
         hg_ref[...] = dot(ml, w_back[...]).astype(BF16).reshape(PER, PAD, D)
 
@@ -311,7 +311,6 @@
         scr[1, :, 128:256] = jnp.concatenate([grad[:, 256 + HD : 384], gain], axis=1)
         repack(places, rows, scr, (keep1, send1))
         repack(places2, rows, scr, (keep2, send2), 256 + fs)
-        y_ref[...] = y_all[...].astype(BF16)
 
 
 def attend_back(qkv_ref, probs_ref, hg_ref, grad_ref, grad_all, at):
@@ -419,7 +418,7 @@
         at += count
     xhat, rstd = normalize(tall(x_ref).astype(F32))
     back = dot(grad[...], w_turned[...])[:, :D]
-    dx = tall(mg_ref) + norm_back(back, xhat, rstd, gain_ref[0:1, :])
+    dx = tall(mg_ref).astype(F32) + norm_back(back, xhat, rstd, gain_ref[0:1, :])
     store_rows(out_ref, dx, step, sum(cuts))
 
 
@@ -545,7 +544,7 @@
         + [row(PAD, D), row(PAD, D), row(PAD, D), whole(8, D)],
         [
             (once(images * SEQ, D), shape_of(images * SEQ, D)),
-            (row(PAD, D), shape_of(images, PAD, D, dtype=F32)),
+            (row(PAD, D), shape_of(images, PAD, D)),
             (row(PAD, D), shape_of(images, PAD, D)),
         ]
         + [(once(n // 2, rows, w), shape_of(n // 2, rows, w)) for w in (wide1, wide1, wide2, wide2)],
@@ -563,12 +562,11 @@
             pltpu.VMEM((big, D), BF16),
             pltpu.VMEM((big, D), BF16),
             pltpu.VMEM((big, WIDE), BF16),
-            pltpu.VMEM((images * SEQ, D), F32),
         ],
         (*rest1_all, *rest2_all, x, og, heads, gain),
         16000,
         30000,
-        44,
+        34,
     )
     if rows != own_rows:
         keep1, send1 = jnp.split(out_of_order(places, jnp.concatenate([keep1, send1], axis=0), own_rows), 2)

time: 138 us -> 130 us (0.942)
  local copies, waits for them, and re-layouts: 15.1 us -> 9.06 us
  Pallas kernels: 52.7 us -> 51.2 us
    unnamed x45 -> x11, local copies, waits for them, and re-layouts: 10.4 us -> 1.86 us
    reshape x2, local copies, waits for them, and re-layouts: 3.04 us -> 5.38 us  [padded(): return jnp.pad(v.reshape(images, SEQ, D), ((0, 0), (0, PAD - SEQ), (0, 0)))]
    pallas_call x7, Pallas kernels: 52.7 us -> 51.2 us  [call(): pl.pallas_call(kernel, grid=(grid,) if grid else (), in_specs=ins, out_sp...]
  transfers between devices with their start and end apart: 29 -> 29, of which waited for: 12 -> 12; matrix products, arithmetic and copies ran while one was open for 8% -> 10% of each run, Pallas kernels for 11% -> 12%
where the time goes in v5:
time: 130 us; the launch traced here: 129 us
  Pallas kernels  51.2 us (39%)
  starting transfers between devices  32.6 us (25%)
  waiting for transfers between devices  31.9 us (25%)
  local copies, waits for them, and re-layouts  9.06 us (7%)
  other arithmetic  3.55 us (3%)
    pallas_call x7, Pallas kernels, call(): pl.pallas_call(kernel, grid=(grid,) if grid else (), in_specs=ins, out_sp...  51.2 us
    ppermute x29, starting transfers between devices, swap(): return lax.ppermute(value, axis, [(i, i ^ bit) for i in range(sizes[axis])])  32.6 us
    ppermute x29, waiting for transfers between devices, swap(): return lax.ppermute(value, axis, [(i, i ^ bit) for i in range(sizes[axis])])  31.9 us
    reshape x2, local copies, waits for them, and re-layouts, padded(): return jnp.pad(v.reshape(images, SEQ, D), ((0, 0), (0, PAD - SEQ), (0, 0)))  5.38 us
  transfers between devices with their start and end apart: 29, of which 12 were waited for; matrix products, arithmetic and copies ran while one was open for 10% of the time, Pallas kernels for 12%

profile of v5, /device:TPU:0, one launch (start us, length us, event | category | flops | bytes accessed | tf_op | source)
XLA Modules:
  0.0 129.2 jit_solution(16653396527761795487)
XLA Ops:
  0.6 1.6 %shard_map.143 = (bf16[1,24,640]{2,1,0:T(8,128)(2,1)}, bf16[1,24,1792]{2,1,0:T(8,128)(2,1)}) custom-call(bf16[3,24,192]{2,1,0:T(8,128)(2,1)} %bitcast.14, f32[1,24]{1,0:T(1,128)} %bitcast.10, f32[1,24]{1,0:T(1,128)} %bitcast.12, bf16[24,192]{1,0:T(8,128)(2,1)} %bitcast.16, bf16[24,768]{1,0:T(8,128)(2,1)} %fc1.1, bf16[24,768]{1,0:T(8,128)(2,1)} %bitcast.15), custom_call_target="tpu_custom_call" | custom-call | tf_op jit(solution)/shard_map/pallas_call | solution.py:455
  2.3 4.1 %collective-permute-start.10 = (bf16[1,24,640]{2,1,0:T(8,128)(2,1)}, bf16[1,24,640]{2,1,0:T(8,128)(2,1)S(1)}, u32[]{:S(2)}, u32[]{:S(2)}) collective-permute-start(bf16[1,24,640]{2,1,0:T(8,128)(2,1)} %get-tuple-element.33), channel_id=1, source_target_pairs={{0,16},{2,18},{4,20},{6,22},{8,24},{10,26},{12,28},{14,30},{16,0},... | collective-permute-start | bytes 92168 | tf_op jit(solution)/shard_map/ppermute | solution.py:44
  9.5 2.5 %collective-permute-start.11 = (bf16[2,24,640]{2,1,0:T(8,128)(2,1)S(1)}, bf16[2,24,640]{2,1,0:T(8,128)(2,1)S(1)}, u32[]{:S(2)}, u32[]{:S(2)}) collective-permute-start(bf16[2,24,640]{2,1,0:T(8,128)(2,1)S(1)} %pad_maximum_fusion.5), channel_id=1, source_target_pairs={{0,8},{2,10},{4,12},{6,14},{8,0},{10,2},{12,4},{14,6},{16,24},{18,... | collective-permute-start | bytes 184328 | tf_op jit(solution)/shard_map/ppermute | solution.py:44
  12.0 1.6 %collective-permute-done = bf16[1,24,1792]{2,1,0:T(8,128)(2,1)S(1)} collective-permute-done((bf16[1,24,1792]{2,1,0:T(8,128)(2,1)}, bf16[1,24,1792]{2,1,0:T(8,128)(2,1)S(1)}, u32[]{:S(2)}, u32[]{:S(2)}) %collective-permute-start) | collective-permute-done | bytes 86048 | tf_op jit(solution)/shard_map/ppermute | solution.py:44
  15.3 1.6 %collective-permute-start.12 = (bf16[4,24,640]{2,1,0:T(8,128)(2,1)S(1)}, bf16[4,24,640]{2,1,0:T(8,128)(2,1)S(1)}, u32[]{:S(2)}, u32[]{:S(2)}) collective-permute-start(bf16[4,24,640]{2,1,0:T(8,128)(2,1)S(1)} %pad_maximum_fusion.4), channel_id=1, source_target_pairs={{0,4},{2,6},{4,0},{6,2},{8,12},{10,14},{12,8},{14,10},{16,20},{18,... | collective-permute-start | bytes 368648 | tf_op jit(solution)/shard_map/ppermute | solution.py:44
  16.9 3.0 %collective-permute-done.1 = bf16[2,24,1792]{2,1,0:T(8,128)(2,1)S(1)} collective-permute-done((bf16[2,24,1792]{2,1,0:T(8,128)(2,1)S(1)}, bf16[2,24,1792]{2,1,0:T(8,128)(2,1)S(1)}, u32[]{:S(2)}, u32[]{:S(2)}) %collective-permute-start.1) | collective-permute-done | bytes 172064 | tf_op jit(solution)/shard_map/ppermute | solution.py:44
  20.0 1.6 %collective-permute-start.2 = (bf16[4,24,1024]{2,1,0:T(8,128)(2,1)S(1)}, bf16[4,24,1024]{2,1,0:T(8,128)(2,1)S(1)}, u32[]{:S(2)}, u32[]{:S(2)}) collective-permute-start(bf16[4,24,1024]{2,1,0:T(8,128)(2,1)S(1)} %slice.80), channel_id=1, source_target_pairs={{0,1},{1,0},{2,3},{3,2},{4,5},{5,4},{6,7},{7,6},{8,9},{9,8},{10,11... | collective-permute-start | bytes 589832 | tf_op jit(solution)/shard_map/ppermute | solution.py:44
  21.6 1.6 %collective-permute-start.6 = (bf16[4,24,768]{2,1,0:T(8,128)(2,1)S(1)}, bf16[4,24,768]{2,1,0:T(8,128)(2,1)S(1)}, u32[]{:S(2)}, u32[]{:S(2)}) collective-permute-start(bf16[4,24,768]{2,1,0:T(8,128)(2,1)S(1)} %slice.81), channel_id=1, source_target_pairs={{0,4},{2,6},{4,0},{6,2},{8,12},{10,14},{12,8},{14,10},{16,20},{18,... | collective-permute-start | bytes 442376 | tf_op jit(solution)/shard_map/ppermute | solution.py:44
  23.7 4.1 %collective-permute-done.2 = bf16[4,24,1024]{2,1,0:T(8,128)(2,1)S(1)} collective-permute-done((bf16[4,24,1024]{2,1,0:T(8,128)(2,1)S(1)}, bf16[4,24,1024]{2,1,0:T(8,128)(2,1)S(1)}, u32[]{:S(2)}, u32[]{:S(2)}) %collective-permute-start.2) | collective-permute-done | bytes 196640 | tf_op jit(solution)/shard_map/ppermute | solution.py:44
  27.8 1.6 %collective-permute-start.3 = (bf16[8,24,1024]{2,1,0:T(8,128)(2,1)S(1)}, bf16[8,24,1024]{2,1,0:T(8,128)(2,1)S(1)}, u32[]{:S(2)}, u32[]{:S(2)}) collective-permute-start(bf16[8,24,1024]{2,1,0:T(8,128)(2,1)S(1)} %pad_maximum_fusion.p0), channel_id=1, source_target_pairs={{0,4},{2,6},{4,0},{6,2},{8,12},{10,14},{12,8},{14,10},{16,20},{18,... | collective-permute-start | bytes 1179656 | tf_op jit(solution)/shard_map/ppermute | solution.py:44
  29.4 1.6 %collective-permute-start.7 = (bf16[8,24,768]{2,1,0:T(8,128)(2,1)S(1)}, bf16[8,24,768]{2,1,0:T(8,128)(2,1)S(1)}, u32[]{:S(2)}, u32[]{:S(2)}) collective-permute-start(bf16[8,24,768]{2,1,0:T(8,128)(2,1)S(1)} %pad_maximum_fusion.1.r0), channel_id=1, source_target_pairs={{0,1},{1,0},{2,3},{3,2},{4,5},{5,4},{6,7},{7,6},{8,9},{9,8},{10,11... | collective-permute-start | bytes 884744 | tf_op jit(solution)/shard_map/ppermute | solution.py:44
  31.0 1.6 %collective-permute-done.13.p1 = bf16[8,24,640]{2,1,0:T(8,128)(2,1)S(1)} collective-permute-done((bf16[8,24,640]{2,1,0:T(8,128)(2,1)S(1)}, bf16[8,24,640]{2,1,0:T(8,128)(2,1)S(1)}, u32[]{:S(2)}, u32[]{:S(2)}) %collective-permute-start.13) | collective-permute-done | bytes 245792 | tf_op jit(solution)/shard_map/ppermute | solution.py:44
  32.6 2.7 %reshape.36 = bf16[8,197,384]{2,1,0:T(8,128)(2,1)} reshape(bf16[1576,384]{1,0:T(8,128)(2,1)} %param.8) | data formatting | bytes 2420736 | tf_op jit(solution)/shard_map/reshape | solution.py:472
  35.3 2.7 %reshape.37 = bf16[8,197,384]{2,1,0:T(8,128)(2,1)} reshape(bf16[1576,384]{1,0:T(8,128)(2,1)} %param.15) | data formatting | bytes 2420736 | tf_op jit(solution)/shard_map/reshape | solution.py:472
  38.0 1.5 %pad.7.x_ref.refs_3_ = bf16[8,208,384]{2,1,0:T(8,128)(2,1)S(1)} pad(bf16[8,197,384]{2,1,0:T(8,128)(2,1)} %reshape.36, bf16[]{:T(256)} %constant.2.clone.1), padding=0_0x0_11x0_0 | pad | bytes 2488322 | tf_op jit(solution)/shard_map/jit(_pad)/pad | solution.py:472
  41.0 9.8 %shard_map.144 = (bf16[8,208,1152]{2,1,0:T(8,128)(2,1)S(1)}, bf16[8,3,208,512]{3,2,1,0:T(8,128)(2,1)S(1)}, bf16[8,208,384]{2,1,0:T(8,128)(2,1)S(1)}, bf16[8,208,...) custom-call(bf16[8,24,640]{2,1,0:T(8,128)(2,1)S(1)} %constant_dynamic-update-slice_fusion.3.p0, ...), custom_call_target="tpu_custom_call" | custom-call | flops 8000000000 | bytes 20000000 | tf_op jit(solution)/shard_map/pallas_call | solution.py:455
  50.8 24.0 %shard_map.145 = (bf16[1576,384]{1,0:T(8,128)(2,1)}, bf16[8,208,384]{2,1,0:T(8,128)(2,1)S(1)}, bf16[8,208,384]{2,1,0:T(8,128)(2,1)S(1)}, bf16[16,24,1024]{2,1,0:...) custom-call(bf16[8,24,1024]{2,1,0:T(8,128)(2,1)S(1)} %pad_maximum_fu, ...), custom_call_target="tpu_custom_call" | custom-call | flops 16000000000 | bytes 30000000 | tf_op jit(solution)/shard_map/pallas_call | solution.py:455
  74.8 3.5 %shard_map.146.refs_0_ = bf16[4,208,1152]{2,1,0:T(8,128)(2,1)S(1)} custom-call(bf16[8,208,1152]{2,1,0:T(8,128)(2,1)S(1)} %get-tuple-element.37.qkv_ref, bf16[8,3,208,512]{3,2,1,0:T(8,128)(2,1)S(1)} %get-tuple-element.38.probs_ref, bf16[8,208,384]{2,1,0:T(8,128)(2,1)S(1)} %get-tuple-element.39.hg_ref), custom_call_target="tpu_custom_call" | custom-call | flops 3600000000 | bytes 8000000 | tf_op jit(solution)/shard_map/pallas_call | solution.py:455
  78.3 5.8 %shard_map.147 = (bf16[4,208,1152]{2,1,0:T(8,128)(2,1)S(1)}, bf16[16,24,640]{2,1,0:T(8,128)(2,1)S(1)}, bf16[16,24,640]{2,1,0:T(8,128)(2,1)S(1)}) custom-call(bf16[8,208,1152]{2,1,0:T(8,128)(2,1)S(1)} %get-tuple-element.37.qkv_ref, bf16[8,3,208,512]{3,2,1,0:T(8,128)(2,1)S(1)} %get-tuple-element.38.probs_ref, ...), custom_call_target="tpu_custom_call" | custom-call | flops 3500000000 | bytes 8000000 | tf_op jit(solution)/shard_map/pallas_call | solution.py:455
  86.2 1.2 collective-permute-start.17
  87.7 1.6 %collective-permute-start.25 = (bf16[8,24,768]{2,1,0:T(8,128)(2,1)S(1)}, bf16[8,24,768]{2,1,0:T(8,128)(2,1)S(1)}, u32[]{:S(2)}, u32[]{:S(2)}) collective-permute-start(bf16[8,24,768]{2,1,0:T(8,128)(2,1)S(1)} %slice.94), channel_id=1, source_target_pairs={{0,4},{2,6},{4,0},{6,2},{8,12},{10,14},{12,8},{14,10},{16,20},{18,... | collective-permute-start | bytes 884744 | tf_op jit(solution)/shard_map/ppermute | solution.py:44
  89.2 5.2 %collective-permute-done.17 = bf16[8,24,640]{2,1,0:T(8,128)(2,1)S(1)} collective-permute-done((bf16[8,24,640]{2,1,0:T(8,128)(2,1)S(1)}, bf16[8,24,640]{2,1,0:T(8,128)(2,1)S(1)}, u32[]{:S(2)}, u32[]{:S(2)}) %collective-permute-start.17) | collective-permute-done | bytes 245792 | tf_op jit(solution)/shard_map/ppermute | solution.py:44
  94.5 1.2 collective-permute-start.18
  96.1 1.6 %collective-permute-start.22 = (bf16[8,24,1024]{2,1,0:T(8,128)(2,1)S(1)}, bf16[8,24,1024]{2,1,0:T(8,128)(2,1)S(1)}, u32[]{:S(2)}, u32[]{:S(2)}) collective-permute-start(bf16[8,24,1024]{2,1,0:T(8,128)(2,1)S(1)} %slice.90), channel_id=1, source_target_pairs={{0,1},{1,0},{2,3},{3,2},{4,5},{5,4},{6,7},{7,6},{8,9},{9,8},{10,11... | collective-permute-start | bytes 1179656 | tf_op jit(solution)/shard_map/ppermute | solution.py:44
  97.7 1.8 %collective-permute-done.18 = bf16[4,24,640]{2,1,0:T(8,128)(2,1)S(1)} collective-permute-done((bf16[4,24,640]{2,1,0:T(8,128)(2,1)S(1)}, bf16[4,24,640]{2,1,0:T(8,128)(2,1)S(1)}, u32[]{:S(2)}, u32[]{:S(2)}) %collective-permute-start.18) | collective-permute-done | bytes 122912 | tf_op jit(solution)/shard_map/ppermute | solution.py:44
  100.7 1.4 %collective-permute-start.26 = (bf16[4,24,768]{2,1,0:T(8,128)(2,1)S(1)}, bf16[4,24,768]{2,1,0:T(8,128)(2,1)S(1)}, u32[]{:S(2)}, u32[]{:S(2)}) collective-permute-start(bf16[4,24,768]{2,1,0:T(8,128)(2,1)S(1)} %slice.96), channel_id=1, source_target_pairs={{0,1},{1,0},{2,3},{3,2},{4,5},{5,4},{6,7},{7,6},{8,9},{9,8},{10,11... | collective-permute-start | bytes 442376 | tf_op jit(solution)/shard_map/ppermute | solution.py:44
  102.1 5.9 %collective-permute-done.22 = bf16[8,24,1024]{2,1,0:T(8,128)(2,1)S(1)} collective-permute-done((bf16[8,24,1024]{2,1,0:T(8,128)(2,1)S(1)}, bf16[8,24,1024]{2,1,0:T(8,128)(2,1)S(1)}, u32[]{:S(2)}, u32[]{:S(2)}) %collective-permute-start.22) | collective-permute-done | bytes 393248 | tf_op jit(solution)/shard_map/ppermute | solution.py:44
  109.6 4.3 %collective-permute-done.23 = bf16[4,24,1024]{2,1,0:T(8,128)(2,1)S(1)} collective-permute-done((bf16[4,24,1024]{2,1,0:T(8,128)(2,1)S(1)}, bf16[4,24,1024]{2,1,0:T(8,128)(2,1)S(1)}, u32[]{:S(2)}, u32[]{:S(2)}) %collective-permute-start.23) | collective-permute-done | bytes 196640 | tf_op jit(solution)/shard_map/ppermute | solution.py:44
  115.2 3.3 %collective-permute-start.20 = (bf16[1,24,640]{2,1,0:T(8,128)(2,1)S(1)}, bf16[1,24,640]{2,1,0:T(8,128)(2,1)S(1)}, u32[]{:S(2)}, u32[]{:S(2)}) collective-permute-start(bf16[1,24,640]{2,1,0:T(8,128)(2,1)S(1)} %slice.88), channel_id=1, source_target_pairs={{0,16},{2,18},{4,20},{6,22},{8,24},{10,26},{12,28},{14,30},{16,0},... | collective-permute-start | bytes 92168 | tf_op jit(solution)/shard_map/ppermute | solution.py:44
  118.5 2.2 %collective-permute-done.27 = bf16[2,24,1792]{2,1,0:T(8,128)(2,1)S(1)} collective-permute-done((bf16[2,24,1792]{2,1,0:T(8,128)(2,1)S(1)}, bf16[2,24,1792]{2,1,0:T(8,128)(2,1)S(1)}, u32[]{:S(2)}, u32[]{:S(2)}) %collective-permute-start.27) | collective-permute-done | bytes 172064 | tf_op jit(solution)/shard_map/ppermute | solution.py:44
  120.7 2.0 %collective-permute-start.28 = (bf16[1,24,1792]{2,1,0:T(8,128)(2,1)S(1)}, bf16[1,24,1792]{2,1,0:T(8,128)(2,1)S(1)}, u32[]{:S(2)}, u32[]{:S(2)}) collective-permute-start(bf16[1,24,1792]{2,1,0:T(8,128)(2,1)S(1)} %slice.99), channel_id=1, source_target_pairs={{0,16},{2,18},{4,20},{6,22},{8,24},{10,26},{12,28},{14,30},{16,0},... | collective-permute-start | bytes 258056 | tf_op jit(solution)/shard_map/ppermute | solution.py:44
  122.7 5.7 %shard_map.148 = f32[1576,384]{1,0:T(8,128)} custom-call(bf16[4,208,1152]{2,1,0:T(8,128)(2,1)S(1)} %shard_map.146.refs_0_, bf16[4,208,1152]{2,1,0:T(8,128)(2,1)S(1)} %get-tuple-element.42.refs_1_, bf16[384,1152]{1,0:T(8,128)(2,1)S(1)} %get-tuple-element.41.w_ref.refs_2_, bf16[8,208,384]{2,1,0:T(8,128)(2,1)S(1)} %pad.7.x_ref.refs_3_, ...), custom_call_target="tpu_custom_call" | custom-call | flops 2000000000 | bytes 10000000 | tf_op jit(solution)/shard_map/pallas_call | solution.py:455
  (78 shorter events, 14.6 us)
Async XLA Ops:
  2.3 6.5 %collective-permute-start.10 = (bf16[1,24,640]{2,1,0:T(8,128)(2,1)}, bf16[1,24,640]{2,1,0:T(8,128)(2,1)S(1)}, u32[]{:S(2)}, u32[]{:S(2)}) collective-permute-start(bf16[1,24,640]{2,1,0:T(8,128)(2,1)} %get-tuple-element.33), channel_id=1, source_target_pairs={{0,16},{2,18},{4,20},{6,22},{8,24},{10,26},{12,28},{14,30},{16,0},... | collective-permute-start | bytes 92168 | tf_op jit(solution)/shard_map/ppermute | solution.py:44
  6.3 7.2 %collective-permute-start = (bf16[1,24,1792]{2,1,0:T(8,128)(2,1)}, bf16[1,24,1792]{2,1,0:T(8,128)(2,1)S(1)}, u32[]{:S(2)}, u32[]{:S(2)}) collective-permute-start(bf16[1,24,1792]{2,1,0:T(8,128)(2,1)} %get-tuple-element.32), channel_id=1, source_target_pairs={{0,16},{2,18},{4,20},{6,22},{8,24},{10,26},{12,28},{14,30},{16,0},... | collective-permute-start | bytes 258056 | tf_op jit(solution)/shard_map/ppermute | solution.py:44
  9.5 5.0 %collective-permute-start.11 = (bf16[2,24,640]{2,1,0:T(8,128)(2,1)S(1)}, bf16[2,24,640]{2,1,0:T(8,128)(2,1)S(1)}, u32[]{:S(2)}, u32[]{:S(2)}) collective-permute-start(bf16[2,24,640]{2,1,0:T(8,128)(2,1)S(1)} %pad_maximum_fusion.5), channel_id=1, source_target_pairs={{0,8},{2,10},{4,12},{6,14},{8,0},{10,2},{12,4},{14,6},{16,24},{18,... | collective-permute-start | bytes 184328 | tf_op jit(solution)/shard_map/ppermute | solution.py:44
  14.4 5.5 %collective-permute-start.1 = (bf16[2,24,1792]{2,1,0:T(8,128)(2,1)S(1)}, bf16[2,24,1792]{2,1,0:T(8,128)(2,1)S(1)}, u32[]{:S(2)}, u32[]{:S(2)}) collective-permute-start(bf16[2,24,1792]{2,1,0:T(8,128)(2,1)S(1)} %pad_maximum_fusion.3), channel_id=1, source_target_pairs={{0,8},{2,10},{4,12},{6,14},{8,0},{10,2},{12,4},{14,6},{16,24},{18,... | collective-permute-start | bytes 516104 | tf_op jit(solution)/shard_map/ppermute | solution.py:44
  15.3 7.8 %collective-permute-start.12 = (bf16[4,24,640]{2,1,0:T(8,128)(2,1)S(1)}, bf16[4,24,640]{2,1,0:T(8,128)(2,1)S(1)}, u32[]{:S(2)}, u32[]{:S(2)}) collective-permute-start(bf16[4,24,640]{2,1,0:T(8,128)(2,1)S(1)} %pad_maximum_fusion.4), channel_id=1, source_target_pairs={{0,4},{2,6},{4,0},{6,2},{8,12},{10,14},{12,8},{14,10},{16,20},{18,... | collective-permute-start | bytes 368648 | tf_op jit(solution)/shard_map/ppermute | solution.py:44
  20.0 7.8 %collective-permute-start.2 = (bf16[4,24,1024]{2,1,0:T(8,128)(2,1)S(1)}, bf16[4,24,1024]{2,1,0:T(8,128)(2,1)S(1)}, u32[]{:S(2)}, u32[]{:S(2)}) collective-permute-start(bf16[4,24,1024]{2,1,0:T(8,128)(2,1)S(1)} %slice.80), channel_id=1, source_target_pairs={{0,1},{1,0},{2,3},{3,2},{4,5},{5,4},{6,7},{7,6},{8,9},{9,8},{10,11... | collective-permute-start | bytes 589832 | tf_op jit(solution)/shard_map/ppermute | solution.py:44
  21.6 7.8 %collective-permute-start.6 = (bf16[4,24,768]{2,1,0:T(8,128)(2,1)S(1)}, bf16[4,24,768]{2,1,0:T(8,128)(2,1)S(1)}, u32[]{:S(2)}, u32[]{:S(2)}) collective-permute-start(bf16[4,24,768]{2,1,0:T(8,128)(2,1)S(1)} %slice.81), channel_id=1, source_target_pairs={{0,4},{2,6},{4,0},{6,2},{8,12},{10,14},{12,8},{14,10},{16,20},{18,... | collective-permute-start | bytes 442376 | tf_op jit(solution)/shard_map/ppermute | solution.py:44
  23.1 9.5 %collective-permute-start.13 = (bf16[8,24,640]{2,1,0:T(8,128)(2,1)S(1)}, bf16[8,24,640]{2,1,0:T(8,128)(2,1)S(1)}, u32[]{:S(2)}, u32[]{:S(2)}) collective-permute-start(bf16[8,24,640]{2,1,0:T(8,128)(2,1)S(1)} %constant_dynamic-update-slice_fusion.3.p0), channel_id=1, source_target_pairs={{0,1},{1,0},{2,3},{3,2},{4,5},{5,4},{6,7},{7,6},{8,9},{9,8},{10,11... | collective-permute-start | bytes 737288 | tf_op jit(solution)/shard_map/ppermute | solution.py:44
  27.8 13.1 %collective-permute-start.3 = (bf16[8,24,1024]{2,1,0:T(8,128)(2,1)S(1)}, bf16[8,24,1024]{2,1,0:T(8,128)(2,1)S(1)}, u32[]{:S(2)}, u32[]{:S(2)}) collective-permute-start(bf16[8,24,1024]{2,1,0:T(8,128)(2,1)S(1)} %pad_maximum_fusion.p0), channel_id=1, source_target_pairs={{0,4},{2,6},{4,0},{6,2},{8,12},{10,14},{12,8},{14,10},{16,20},{18,... | collective-permute-start | bytes 1179656 | tf_op jit(solution)/shard_map/ppermute | solution.py:44
  29.4 11.1 %collective-permute-start.7 = (bf16[8,24,768]{2,1,0:T(8,128)(2,1)S(1)}, bf16[8,24,768]{2,1,0:T(8,128)(2,1)S(1)}, u32[]{:S(2)}, u32[]{:S(2)}) collective-permute-start(bf16[8,24,768]{2,1,0:T(8,128)(2,1)S(1)} %pad_maximum_fusion.1.r0), channel_id=1, source_target_pairs={{0,1},{1,0},{2,3},{3,2},{4,5},{5,4},{6,7},{7,6},{8,9},{9,8},{10,11... | collective-permute-start | bytes 884744 | tf_op jit(solution)/shard_map/ppermute | solution.py:44
  31.0 9.4 %collective-permute-start.14 = (bf16[8,24,640]{2,1,0:T(8,128)(2,1)S(1)}, bf16[8,24,640]{2,1,0:T(8,128)(2,1)S(1)}, u32[]{:S(2)}, u32[]{:S(2)}) collective-permute-start(bf16[8,24,640]{2,1,0:T(8,128)(2,1)S(1)} %constant_dynamic-update-slice_fusion.3.p0), channel_id=1, source_target_pairs={{0,2},{2,0},{4,6},{6,4},{8,10},{10,8},{12,14},{14,12},{16,18},{18,... | collective-permute-start | bytes 737288 | tf_op jit(solution)/shard_map/ppermute | solution.py:44
  32.6 8.3 %collective-permute-start.15 = (bf16[8,24,640]{2,1,0:T(8,128)(2,1)S(1)}, bf16[8,24,640]{2,1,0:T(8,128)(2,1)S(1)}, u32[]{:S(2)}, u32[]{:S(2)}) collective-permute-start(bf16[8,24,640]{2,1,0:T(8,128)(2,1)S(1)} %collective-permute-done.13.p1), channel_id=1, source_target_pairs={{0,2},{2,0},{4,6},{6,4},{8,10},{10,8},{12,14},{14,12},{16,18},{18,... | collective-permute-start | bytes 737288 | tf_op jit(solution)/shard_map/ppermute | solution.py:44
  38.0 1.7 %copy-start.2 = (bf16[8,197,384]{2,1,0:T(8,128)(2,1)S(1)}, bf16[8,197,384]{2,1,0:T(8,128)(2,1)}, u32[]{:S(2)}) copy-start(bf16[8,197,384]{2,1,0:T(8,128)(2,1)} %reshape.37) | copy-start | bytes 3631108
  39.8 10.9 %collective-permute-start.8 = (bf16[8,24,768]{2,1,0:T(8,128)(2,1)S(1)}, bf16[8,24,768]{2,1,0:T(8,128)(2,1)S(1)}, u32[]{:S(2)}, u32[]{:S(2)}) collective-permute-start(bf16[8,24,768]{2,1,0:T(8,128)(2,1)S(1)} %pad_maximum_fusion.1.r0), channel_id=1, source_target_pairs={{0,2},{2,0},{4,6},{6,4},{8,10},{10,8},{12,14},{14,12},{16,18},{18,... | collective-permute-start | bytes 884744 | tf_op jit(solution)/shard_map/ppermute | solution.py:44
  40.4 10.4 %collective-permute-start.4 = (bf16[8,24,1024]{2,1,0:T(8,128)(2,1)S(1)}, bf16[8,24,1024]{2,1,0:T(8,128)(2,1)S(1)}, u32[]{:S(2)}, u32[]{:S(2)}) collective-permute-start(bf16[8,24,1024]{2,1,0:T(8,128)(2,1)S(1)} %pad_maximum_fusion.p0), channel_id=1, source_target_pairs={{0,2},{2,0},{4,6},{6,4},{8,10},{10,8},{12,14},{14,12},{16,18},{18,... | collective-permute-start | bytes 1179656 | tf_op jit(solution)/shard_map/ppermute | solution.py:44
  40.5 10.3 %collective-permute-start.9 = (bf16[8,24,768]{2,1,0:T(8,128)(2,1)S(1)}, bf16[8,24,768]{2,1,0:T(8,128)(2,1)S(1)}, u32[]{:S(2)}, u32[]{:S(2)}) collective-permute-start(bf16[8,24,768]{2,1,0:T(8,128)(2,1)S(1)} %collective-permute-done.7.r1), channel_id=1, source_target_pairs={{0,2},{2,0},{4,6},{6,4},{8,10},{10,8},{12,14},{14,12},{16,18},{18,... | collective-permute-start | bytes 884744 | tf_op jit(solution)/shard_map/ppermute | solution.py:44
  40.9 9.9 %collective-permute-start.5 = (bf16[8,24,1024]{2,1,0:T(8,128)(2,1)S(1)}, bf16[8,24,1024]{2,1,0:T(8,128)(2,1)S(1)}, u32[]{:S(2)}, u32[]{:S(2)}) collective-permute-start(bf16[8,24,1024]{2,1,0:T(8,128)(2,1)S(1)} %collective-permute-done.3.p1), channel_id=1, source_target_pairs={{0,2},{2,0},{4,6},{6,4},{8,10},{10,8},{12,14},{14,12},{16,18},{18,... | collective-permute-start | bytes 1179656 | tf_op jit(solution)/shard_map/ppermute | solution.py:44
  84.2 1.9 %collective-permute-start.16 = (bf16[16,24,640]{2,1,0:T(8,128)(2,1)S(1)}, bf16[16,24,640]{2,1,0:T(8,128)(2,1)S(1)}, u32[]{:S(2)}, u32[]{:S(2)}) collective-permute-start(bf16[16,24,640]{2,1,0:T(8,128)(2,1)S(1)} %get-tuple-element.45), channel_id=1, source_target_pairs={{0,2},{2,0},{4,6},{6,4},{8,10},{10,8},{12,14},{14,12},{16,18},{18,... | collective-permute-start | bytes 1474568 | tf_op jit(solution)/shard_map/ppermute | solution.py:44
  84.5 3.0 %collective-permute-start.24 = (bf16[16,24,768]{2,1,0:T(8,128)(2,1)S(1)}, bf16[16,24,768]{2,1,0:T(8,128)(2,1)S(1)}, u32[]{:S(2)}, u32[]{:S(2)}) collective-permute-start(bf16[16,24,768]{2,1,0:T(8,128)(2,1)S(1)} %get-tuple-element.49), channel_id=1, source_target_pairs={{0,2},{2,0},{4,6},{6,4},{8,10},{10,8},{12,14},{14,12},{16,18},{18,... | collective-permute-start | bytes 1769480 | tf_op jit(solution)/shard_map/ppermute | solution.py:44
  84.7 11.0 %collective-permute-start.21 = (bf16[16,24,1024]{2,1,0:T(8,128)(2,1)S(1)}, bf16[16,24,1024]{2,1,0:T(8,128)(2,1)S(1)}, u32[]{:S(2)}, u32[]{:S(2)}) collective-permute-start(bf16[16,24,1024]{2,1,0:T(8,128)(2,1)S(1)} %get-tuple-element.47), channel_id=1, source_target_pairs={{0,2},{2,0},{4,6},{6,4},{8,10},{10,8},{12,14},{14,12},{16,18},{18,... | collective-permute-start | bytes 2359304 | tf_op jit(solution)/shard_map/ppermute | solution.py:44
  86.2 8.2 %collective-permute-start.17 = (bf16[8,24,640]{2,1,0:T(8,128)(2,1)S(1)}, bf16[8,24,640]{2,1,0:T(8,128)(2,1)S(1)}, u32[]{:S(2)}, u32[]{:S(2)}) collective-permute-start(bf16[8,24,640]{2,1,0:T(8,128)(2,1)S(1)} %slice.83), channel_id=1, source_target_pairs={{0,1},{1,0},{2,3},{3,2},{4,5},{5,4},{6,7},{7,6},{8,9},{9,8},{10,11... | collective-permute-start | bytes 737288 | tf_op jit(solution)/shard_map/ppermute | solution.py:44
  87.7 12.9 %collective-permute-start.25 = (bf16[8,24,768]{2,1,0:T(8,128)(2,1)S(1)}, bf16[8,24,768]{2,1,0:T(8,128)(2,1)S(1)}, u32[]{:S(2)}, u32[]{:S(2)}) collective-permute-start(bf16[8,24,768]{2,1,0:T(8,128)(2,1)S(1)} %slice.94), channel_id=1, source_target_pairs={{0,4},{2,6},{4,0},{6,2},{8,12},{10,14},{12,8},{14,10},{16,20},{18,... | collective-permute-start | bytes 884744 | tf_op jit(solution)/shard_map/ppermute | solution.py:44
  94.5 4.9 %collective-permute-start.18 = (bf16[4,24,640]{2,1,0:T(8,128)(2,1)S(1)}, bf16[4,24,640]{2,1,0:T(8,128)(2,1)S(1)}, u32[]{:S(2)}, u32[]{:S(2)}) collective-permute-start(bf16[4,24,640]{2,1,0:T(8,128)(2,1)S(1)} %slice.85), channel_id=1, source_target_pairs={{0,4},{2,6},{4,0},{6,2},{8,12},{10,14},{12,8},{14,10},{16,20},{18,... | collective-permute-start | bytes 368648 | tf_op jit(solution)/shard_map/ppermute | solution.py:44
  96.1 11.8 %collective-permute-start.22 = (bf16[8,24,1024]{2,1,0:T(8,128)(2,1)S(1)}, bf16[8,24,1024]{2,1,0:T(8,128)(2,1)S(1)}, u32[]{:S(2)}, u32[]{:S(2)}) collective-permute-start(bf16[8,24,1024]{2,1,0:T(8,128)(2,1)S(1)} %slice.90), channel_id=1, source_target_pairs={{0,1},{1,0},{2,3},{3,2},{4,5},{5,4},{6,7},{7,6},{8,9},{9,8},{10,11... | collective-permute-start | bytes 1179656 | tf_op jit(solution)/shard_map/ppermute | solution.py:44
  99.5 15.6 %collective-permute-start.19 = (bf16[2,24,640]{2,1,0:T(8,128)(2,1)S(1)}, bf16[2,24,640]{2,1,0:T(8,128)(2,1)S(1)}, u32[]{:S(2)}, u32[]{:S(2)}) collective-permute-start(bf16[2,24,640]{2,1,0:T(8,128)(2,1)S(1)} %slice.87), channel_id=1, source_target_pairs={{0,8},{2,10},{4,12},{6,14},{8,0},{10,2},{12,4},{14,6},{16,24},{18,... | collective-permute-start | bytes 184328 | tf_op jit(solution)/shard_map/ppermute | solution.py:44
  100.7 8.9 %collective-permute-start.26 = (bf16[4,24,768]{2,1,0:T(8,128)(2,1)S(1)}, bf16[4,24,768]{2,1,0:T(8,128)(2,1)S(1)}, u32[]{:S(2)}, u32[]{:S(2)}) collective-permute-start(bf16[4,24,768]{2,1,0:T(8,128)(2,1)S(1)} %slice.96), channel_id=1, source_target_pairs={{0,1},{1,0},{2,3},{3,2},{4,5},{5,4},{6,7},{7,6},{8,9},{9,8},{10,11... | collective-permute-start | bytes 442376 | tf_op jit(solution)/shard_map/ppermute | solution.py:44
  108.1 5.7 %collective-permute-start.23 = (bf16[4,24,1024]{2,1,0:T(8,128)(2,1)S(1)}, bf16[4,24,1024]{2,1,0:T(8,128)(2,1)S(1)}, u32[]{:S(2)}, u32[]{:S(2)}) collective-permute-start(bf16[4,24,1024]{2,1,0:T(8,128)(2,1)S(1)} %slice.92), channel_id=1, source_target_pairs={{0,4},{2,6},{4,0},{6,2},{8,12},{10,14},{12,8},{14,10},{16,20},{18,... | collective-permute-start | bytes 589832 | tf_op jit(solution)/shard_map/ppermute | solution.py:44
  113.9 6.7 %collective-permute-start.27 = (bf16[2,24,1792]{2,1,0:T(8,128)(2,1)S(1)}, bf16[2,24,1792]{2,1,0:T(8,128)(2,1)S(1)}, u32[]{:S(2)}, u32[]{:S(2)}) collective-permute-start(bf16[2,24,1792]{2,1,0:T(8,128)(2,1)S(1)} %pad_maximum_fusion.2), channel_id=1, source_target_pairs={{0,8},{2,10},{4,12},{6,14},{8,0},{10,2},{12,4},{14,6},{16,24},{18,... | collective-permute-start | bytes 516104 | tf_op jit(solution)/shard_map/ppermute | solution.py:44
  115.2 13.3 %collective-permute-start.20 = (bf16[1,24,640]{2,1,0:T(8,128)(2,1)S(1)}, bf16[1,24,640]{2,1,0:T(8,128)(2,1)S(1)}, u32[]{:S(2)}, u32[]{:S(2)}) collective-permute-start(bf16[1,24,640]{2,1,0:T(8,128)(2,1)S(1)} %slice.88), channel_id=1, source_target_pairs={{0,16},{2,18},{4,20},{6,22},{8,24},{10,26},{12,28},{14,30},{16,0},... | collective-permute-start | bytes 92168 | tf_op jit(solution)/shard_map/ppermute | solution.py:44
  120.7 7.7 %collective-permute-start.28 = (bf16[1,24,1792]{2,1,0:T(8,128)(2,1)S(1)}, bf16[1,24,1792]{2,1,0:T(8,128)(2,1)S(1)}, u32[]{:S(2)}, u32[]{:S(2)}) collective-permute-start(bf16[1,24,1792]{2,1,0:T(8,128)(2,1)S(1)} %slice.99), channel_id=1, source_target_pairs={{0,16},{2,18},{4,20},{6,22},{8,24},{10,26},{12,28},{14,30},{16,0},... | collective-permute-start | bytes 258056 | tf_op jit(solution)/shard_map/ppermute | solution.py:44
  122.7 5.7 %copy-start = (f32[24]{0:T(128)S(1)}, f32[24]{0:T(128)}, u32[]{:S(2)}) copy-start(f32[24]{0:T(128)} %param.9) | copy-start | bytes 292
  122.7 5.7 %copy-start.1 = (f32[24]{0:T(128)S(1)}, f32[24]{0:T(128)}, u32[]{:S(2)}) copy-start(f32[24]{0:T(128)} %param.12) | copy-start | bytes 292

commit v6 on v5

--- a/solution.py
+++ b/solution.py
@@ -156,7 +156,7 @@
     return jnp.sum(jnp.where(own, jnp.broadcast_to(col, (n, n)), 0.0), axis=0, keepdims=True)
 
 
-def pack_kernel(qkv, gain1, gain2, out, fc1, fc2, first, rest):
+def pack_kernel(qkv, gain1, gain2, out, fc1, fc2, first, rest, rest2):
     rows = out.shape[0]
     fs = fc1.shape[1]
     lane = lax.broadcasted_iota(jnp.int32, (rows, HD), 1)
@@ -170,7 +170,15 @@
     pad = jnp.zeros((rows, HD), F32)
     rest[0, :, 128:256] = jnp.concatenate([out[:, 128:192].astype(F32), pad], axis=1).astype(BF16)
     rest[0, :, 256 : 256 + fs] = fc1[...]
-    rest[0, :, 256 + fs :] = fc2[...]
+    rest2[0] = fc2[...]
+
+
+def pad_kernel(tokens, out_grad, x_ref, og_ref):
+    tail = jnp.zeros((PAD - SEQ, D), F32)
+    for source, target in ((tokens, x_ref), (out_grad, og_ref)):
+        for i in range(target.shape[0]):
+            own = source[i * SEQ : i * SEQ + SEQ, :].astype(F32)
+            target[i] = jnp.concatenate([own, tail], axis=0).astype(BF16)
 
 
 def attend_kernel(places, rows, p0, p1, p2, p3, x_ref, qkv_ref, probs_ref, heads_ref, n1_ref, w_ref, gain_ref, scr):
@@ -225,7 +233,7 @@
 def mlp_kernel(
     places, places2, rows, blocks, fs, p0, p1, p2, p3, r0, r1, r2, r3, x_ref, og_ref, h_ref, gain_ref,
     y_ref, mg_ref, hg_ref, keep1, send1, keep2, send2,
-    scr, w_out, w_back, w_fc1, w_fc1_turned, fc2_ref, w_fc2_turned, n2_all, pg_all, hid_all, og_all, ml_all, h_all,
+    scr, w_back, w_fc1, fc2_ref, n2_all, pg_all, hid_all, og_all, ml_all, h_all,
 ):
     step = pl.program_id(0)
 
@@ -238,15 +246,12 @@
         for b, value in enumerate((scr[0, :, 0:128], scr[1, :, 0:128], last)):
             value = value.astype(BF16)
             w_back[:, b * 128 : b * 128 + 128] = value
-            w_out[b * 128 : b * 128 + 128, :] = value.T
         for t in range(2):
             at = slice(t * fs, t * fs + fs)
             value = scr[t, :, 256 : 256 + fs].astype(BF16)
             w_fc1[:, at] = value
-            w_fc1_turned[at, :] = value.T
             value = scr[t, :, 256 + fs :].astype(BF16)
             fc2_ref[:, at] = value
-            w_fc2_turned[at, :] = value.T
 
     @pl.when(step < blocks)
     def _():
@@ -257,7 +262,7 @@
         og = tall(og_ref)
         h_all[at, :D] = h
         og_all[at, :] = og
-        middle = tall(x_ref).astype(F32) + dot(h, w_out[...])
+        middle = tall(x_ref).astype(F32) + dot(h, w_back[...], NT)
         xhat, rstd = normalize(middle)
         n2 = (xhat * gain).astype(BF16)
         n2_all[at, :] = n2
@@ -280,9 +285,9 @@
             slope = plus + full * (1.0 - plus) * ((2.0 * GELU_C) + (GELU_C * 0.26829) * square)
             pg = (dh * slope).astype(BF16)
             pg_all[at, cols] = pg
-            part = dot(pg, w_fc1_turned[cols, :])
+            part = dot(pg, w_fc1[:, cols], NT)
             back = part if back is None else back + part
-            middle += dot(hid, w_fc2_turned[cols, :])
+            middle += dot(hid, fc2_ref[:, cols], NT)
         store_rows(y_ref, middle.astype(BF16), step, blocks)
         mg = og.astype(F32) + norm_back(back, xhat, rstd, gain)
         ml = mg.astype(BF16)
@@ -468,10 +473,6 @@
     return jax.ShapeDtypeStruct(shape, dtype)
 
 
-def padded(v, images):
-    return jnp.pad(v.reshape(images, SEQ, D), ((0, 0), (0, PAD - SEQ), (0, 0)))
-
-
 def local(sizes, tokens, ln1_gain, qkv_weight, out_weight, ln2_gain, fc1_weight, fc2_weight, out_grad):
     return layer(sizes, tokens, ln1_gain, qkv_weight, out_weight, ln2_gain, fc1_weight, fc2_weight, out_grad)
 
@@ -490,20 +491,17 @@
     big = images * PAD
     gain1, gain2 = ln1_gain.reshape(1, rows), ln2_gain.reshape(1, rows)
 
-    first, rest = call(
+    first, rest1, rest2 = call(
         pack_kernel,
         0,
         [whole(3, rows, 192), whole(1, rows), whole(1, rows), whole(rows, 192), whole(rows, fs), whole(rows, fs)],
-        [(whole(1, rows, QC), shape_of(1, rows, QC)), (whole(1, rows, rc), shape_of(1, rows, rc))],
+        [(whole(1, rows, w), shape_of(1, rows, w)) for w in (QC, 256 + fs, fs)],
         [],
-        (qkv_weight.transpose(1, 0, 2), gain1, gain2, out_weight.T, fc1_weight, fc2_weight.T),
-        vmem=60,
+        tuple(pltpu.with_memory_space_constraint(v, pltpu.HBM) for v in (qkv_weight.transpose(1, 0, 2), gain1, gain2, out_weight.T, fc1_weight, fc2_weight.T)),
     )
     first_all = gather(first, stages, sizes)
-    for stage in stages[:-3]:
-        rest = grow(rest, stage, sizes)
-    rest1_all = gather(rest[:, :, : 256 + fs], stages2[-3:], sizes)
-    rest2_all = gather(rest[:, :, 256 + fs :], stages[-3:], sizes)
+    rest1_all = gather(rest1, stages2, sizes)
+    rest2_all = gather(rest2, stages, sizes)
     if rows % 8 != 0:
         n, rows = 16, 48
         first_all, rest1_all, rest2_all = (
@@ -511,8 +509,17 @@
             for order, v in ((places, first_all), (places2, rest1_all), (places, rest2_all))
         )
 
-    x = padded(tokens, images)
-    og = padded(out_grad, images)
+    x, og = call(
+        pad_kernel,
+        0,
+        [whole(images * SEQ, D)] * 2,
+        [(whole(images, PAD, D), shape_of(images, PAD, D))] * 2,
+        [],
+        (tokens, out_grad),
+        2000,
+        10000,
+        12,
+    )
 
     def row(*shape):
         return part(0, blocks, *shape)
@@ -533,7 +540,7 @@
         (*first_all, x),
         8000,
         20000,
-        24,
+        12,
     )
     wide1, wide2 = 256 + fs, fs
     y, mg, hg, keep1, send1, keep2, send2 = call(
@@ -551,11 +558,8 @@
         [
             pltpu.VMEM((2, D, rc), F32),
             pltpu.VMEM((D, D), BF16),
-            pltpu.VMEM((D, D), BF16),
             pltpu.VMEM((D, ff), BF16),
-            pltpu.VMEM((ff, D), BF16),
             pltpu.VMEM((D, ff), BF16),
-            pltpu.VMEM((ff, D), BF16),
             pltpu.VMEM((big, D), BF16),
             pltpu.VMEM((big, ff), BF16),
             pltpu.VMEM((big, ff), BF16),
@@ -595,7 +599,7 @@
             (qkv, probs, hg),
             1800 * count,
             4000 * count,
-            20,
+            8,
         )
         at += count
     left = cuts[-1]
@@ -611,7 +615,7 @@
         (qkv, probs, hg, n1, w_qkv, *pieces),
         3500,
         8000,
-        32,
+        14,
     )
     pieces.append(last)
     starts = [sum(cuts[:c]) for c in range(len(cuts))]
@@ -625,7 +629,7 @@
         (*pieces, w_qkv, x, mg, gain),
         2000,
         10000,
-        24,
+        10,
     )
     if rows != own_rows:
         keep_q, send_q = jnp.split(out_of_order(places, jnp.concatenate([keep_q, send_q], axis=0), own_rows), 2)

time: 130 us -> 122 us (0.938)
  local copies, waits for them, and re-layouts: 9.06 us -> 0.24 us
  starting transfers between devices: 32.6 us -> 37.7 us
  other arithmetic: 3.55 us -> 1.13 us
    reshape x2 -> x0, local copies, waits for them, and re-layouts: 5.38 us -> none  [padded(): return jnp.pad(v.reshape(images, SEQ, D), ((0, 0), (0, PAD - SEQ), (0, 0)))]
    ppermute x29 -> x31, starting transfers between devices: 32.6 us -> 37.7 us  [swap(): return lax.ppermute(value, axis, [(i, i ^ bit) for i in range(sizes[axis])])]
    concatenate x5 -> x6, other arithmetic: 2.51 us -> 0.09 us  [grow(): return jnp.concatenate([held, got], axis=0)]
    unnamed x11 -> x17, local copies, waits for them, and re-layouts: 1.86 us -> 0.07 us
    pad x2 -> x0, local copies, waits for them, and re-layouts: 1.64 us -> none  [padded(): return jnp.pad(v.reshape(images, SEQ, D), ((0, 0), (0, PAD - SEQ), (0, 0)))]
    ppermute x29 -> x31, waiting for transfers between devices: 31.9 us -> 31.1 us  [swap(): return lax.ppermute(value, axis, [(i, i ^ bit) for i in range(sizes[axis])])]
    pallas_call x7 -> x8, Pallas kernels: 51.2 us -> 50.8 us  [call(): pl.pallas_call(kernel, grid=(grid,) if grid else (), in_specs=ins, out_sp...]
  transfers between devices with their start and end apart: 29 -> 31, of which waited for: 12 -> 16; matrix products, arithmetic and copies ran while one was open for 10% -> 1% of each run, Pallas kernels for 12% -> 13%
where the time goes in v6:
time: 122 us
  Pallas kernels  50.8 us (42%)
  starting transfers between devices  37.7 us (31%)
  waiting for transfers between devices  31.1 us (25%)
    pallas_call x8, Pallas kernels, call(): pl.pallas_call(kernel, grid=(grid,) if grid else (), in_specs=ins, out_sp...  50.8 us
    ppermute x31, starting transfers between devices, swap(): return lax.ppermute(value, axis, [(i, i ^ bit) for i in range(sizes[axis])])  37.7 us
    ppermute x31, waiting for transfers between devices, swap(): return lax.ppermute(value, axis, [(i, i ^ bit) for i in range(sizes[axis])])  31.1 us
  transfers between devices with their start and end apart: 31, of which 16 were waited for; matrix products, arithmetic and copies ran while one was open for 1% of the time, Pallas kernels for 13%

profile of v6, /device:TPU:0, one launch (start us, length us, event | category | flops | bytes accessed | tf_op | source)
XLA Modules:
  0.0 122.0 jit_solution(4177575518689789584)
XLA Ops:
  0.6 1.0 shard_map.143
  1.6 4.1 %collective-permute-start.12 = (bf16[1,24,640]{2,1,0:T(8,128)(2,1)S(1)}, bf16[1,24,640]{2,1,0:T(8,128)(2,1)S(1)}, u32[]{:S(2)}, u32[]{:S(2)}) collective-permute-start(bf16[1,24,640]{2,1,0:T(8,128)(2,1)S(1)} %get-tuple-element.39), channel_id=1, source_target_pairs={{0,16},{2,18},{4,20},{6,22},{8,24},{10,26},{12,28},{14,30},{16,0},... | collective-permute-start | bytes 92168 | tf_op jit(solution)/shard_map/ppermute | solution.py:44
  5.8 2.8 %collective-permute-start = (bf16[1,24,1024]{2,1,0:T(8,128)(2,1)S(1)}, bf16[1,24,1024]{2,1,0:T(8,128)(2,1)S(1)}, u32[]{:S(2)}, u32[]{:S(2)}) collective-permute-start(bf16[1,24,1024]{2,1,0:T(8,128)(2,1)S(1)} %get-tuple-element.35), channel_id=1, source_target_pairs={{0,16},{2,18},{4,20},{6,22},{8,24},{10,26},{12,28},{14,30},{16,0},... | collective-permute-start | bytes 147464 | tf_op jit(solution)/shard_map/ppermute | solution.py:44
  8.7 1.6 %collective-permute-start.13 = (bf16[2,24,640]{2,1,0:T(8,128)(2,1)S(1)}, bf16[2,24,640]{2,1,0:T(8,128)(2,1)S(1)}, u32[]{:S(2)}, u32[]{:S(2)}) collective-permute-start(bf16[2,24,640]{2,1,0:T(8,128)(2,1)S(1)} %pad_maximum_fusion.6), channel_id=1, source_target_pairs={{0,8},{2,10},{4,12},{6,14},{8,0},{10,2},{12,4},{14,6},{16,24},{18,... | collective-permute-start | bytes 184328 | tf_op jit(solution)/shard_map/ppermute | solution.py:44
  13.9 1.6 %collective-permute-start.14 = (bf16[4,24,640]{2,1,0:T(8,128)(2,1)S(1)}, bf16[4,24,640]{2,1,0:T(8,128)(2,1)S(1)}, u32[]{:S(2)}, u32[]{:S(2)}) collective-permute-start(bf16[4,24,640]{2,1,0:T(8,128)(2,1)S(1)} %pad_maximum_fusion.3), channel_id=1, source_target_pairs={{0,4},{2,6},{4,0},{6,2},{8,12},{10,14},{12,8},{14,10},{16,20},{18,... | collective-permute-start | bytes 368648 | tf_op jit(solution)/shard_map/ppermute | solution.py:44
  15.7 1.6 %collective-permute-start.8 = (bf16[4,24,768]{2,1,0:T(8,128)(2,1)S(1)}, bf16[4,24,768]{2,1,0:T(8,128)(2,1)S(1)}, u32[]{:S(2)}, u32[]{:S(2)}) collective-permute-start(bf16[4,24,768]{2,1,0:T(8,128)(2,1)S(1)} %pad_maximum_fusion.2), channel_id=1, source_target_pairs={{0,4},{2,6},{4,0},{6,2},{8,12},{10,14},{12,8},{14,10},{16,20},{18,... | collective-permute-start | bytes 442376 | tf_op jit(solution)/shard_map/ppermute | solution.py:44
  17.4 1.6 %collective-permute-start.2 = (bf16[4,24,1024]{2,1,0:T(8,128)(2,1)S(1)}, bf16[4,24,1024]{2,1,0:T(8,128)(2,1)S(1)}, u32[]{:S(2)}, u32[]{:S(2)}) collective-permute-start(bf16[4,24,1024]{2,1,0:T(8,128)(2,1)S(1)} %pad_maximum_fusion), channel_id=1, source_target_pairs={{0,1},{1,0},{2,3},{3,2},{4,5},{5,4},{6,7},{7,6},{8,9},{9,8},{10,11... | collective-permute-start | bytes 589832 | tf_op jit(solution)/shard_map/ppermute | solution.py:44
  19.3 1.6 %collective-permute-start.15 = (bf16[8,24,640]{2,1,0:T(8,128)(2,1)S(1)}, bf16[8,24,640]{2,1,0:T(8,128)(2,1)S(1)}, u32[]{:S(2)}, u32[]{:S(2)}) collective-permute-start(bf16[8,24,640]{2,1,0:T(8,128)(2,1)S(1)} %constant_dynamic-update-slice_fusion.8.p0), channel_id=1, source_target_pairs={{0,1},{1,0},{2,3},{3,2},{4,5},{5,4},{6,7},{7,6},{8,9},{9,8},{10,11... | collective-permute-start | bytes 737288 | tf_op jit(solution)/shard_map/ppermute | solution.py:44
  20.9 4.4 %collective-permute-done.2 = bf16[4,24,1024]{2,1,0:T(8,128)(2,1)S(1)} collective-permute-done((bf16[4,24,1024]{2,1,0:T(8,128)(2,1)S(1)}, bf16[4,24,1024]{2,1,0:T(8,128)(2,1)S(1)}, u32[]{:S(2)}, u32[]{:S(2)}) %collective-permute-start.2) | collective-permute-done | bytes 196640 | tf_op jit(solution)/shard_map/ppermute | solution.py:44
  25.3 1.6 %collective-permute-start.3 = (bf16[8,24,1024]{2,1,0:T(8,128)(2,1)S(1)}, bf16[8,24,1024]{2,1,0:T(8,128)(2,1)S(1)}, u32[]{:S(2)}, u32[]{:S(2)}) collective-permute-start(bf16[8,24,1024]{2,1,0:T(8,128)(2,1)S(1)} %constant_dynamic-update-slice_fusion.p0), channel_id=1, source_target_pairs={{0,4},{2,6},{4,0},{6,2},{8,12},{10,14},{12,8},{14,10},{16,20},{18,... | collective-permute-start | bytes 1179656 | tf_op jit(solution)/shard_map/ppermute | solution.py:44
  26.9 1.6 %collective-permute-start.9 = (bf16[8,24,768]{2,1,0:T(8,128)(2,1)S(1)}, bf16[8,24,768]{2,1,0:T(8,128)(2,1)S(1)}, u32[]{:S(2)}, u32[]{:S(2)}) collective-permute-start(bf16[8,24,768]{2,1,0:T(8,128)(2,1)S(1)} %constant_dynamic-update-slice_fusion.4.r0), channel_id=1, source_target_pairs={{0,1},{1,0},{2,3},{3,2},{4,5},{5,4},{6,7},{7,6},{8,9},{9,8},{10,11... | collective-permute-start | bytes 884744 | tf_op jit(solution)/shard_map/ppermute | solution.py:44
  28.5 1.9 %collective-permute-done.15.p1 = bf16[8,24,640]{2,1,0:T(8,128)(2,1)S(1)} collective-permute-done((bf16[8,24,640]{2,1,0:T(8,128)(2,1)S(1)}, bf16[8,24,640]{2,1,0:T(8,128)(2,1)S(1)}, u32[]{:S(2)}, u32[]{:S(2)}) %collective-permute-start.15) | collective-permute-done | bytes 245792 | tf_op jit(solution)/shard_map/ppermute | solution.py:44
  31.6 2.1 %collective-permute-done.9.r1 = bf16[8,24,768]{2,1,0:T(8,128)(2,1)S(1)} collective-permute-done((bf16[8,24,768]{2,1,0:T(8,128)(2,1)S(1)}, bf16[8,24,768]{2,1,0:T(8,128)(2,1)S(1)}, u32[]{:S(2)}, u32[]{:S(2)}) %collective-permute-start.9) | collective-permute-done | bytes 294944 | tf_op jit(solution)/shard_map/ppermute | solution.py:44
  34.2 9.6 %shard_map.145 = (bf16[8,208,1152]{2,1,0:T(8,128)(2,1)S(1)}, bf16[8,3,208,512]{3,2,1,0:T(8,128)(2,1)S(1)}, bf16[8,208,384]{2,1,0:T(8,128)(2,1)S(1)}, bf16[8,208,...) custom-call(bf16[8,24,640]{2,1,0:T(8,128)(2,1)S(1)} %constant_dynamic-update-slice_fusion.8.p0, ...), custom_call_target="tpu_custom_call" | custom-call | flops 8000000000 | bytes 20000000 | tf_op jit(solution)/shard_map/pallas_call | solution.py:460
  43.9 23.7 %shard_map.146 = (bf16[1576,384]{1,0:T(8,128)(2,1)}, bf16[8,208,384]{2,1,0:T(8,128)(2,1)S(1)}, bf16[8,208,384]{2,1,0:T(8,128)(2,1)S(1)}, bf16[16,24,1024]{2,1,0:...) custom-call(bf16[8,24,1024]{2,1,0:T(8,128)(2,1)S(1)} %constant_dynam, ...), custom_call_target="tpu_custom_call" | custom-call | flops 16000000000 | bytes 30000000 | tf_op jit(solution)/shard_map/pallas_call | solution.py:460
  67.6 3.6 %shard_map.147.refs_0_ = bf16[4,208,1152]{2,1,0:T(8,128)(2,1)S(1)} custom-call(bf16[8,208,1152]{2,1,0:T(8,128)(2,1)S(1)} %get-tuple-element.43.qkv_ref, bf16[8,3,208,512]{3,2,1,0:T(8,128)(2,1)S(1)} %get-tuple-element.44.probs_ref, bf16[8,208,384]{2,1,0:T(8,128)(2,1)S(1)} %get-tuple-element.45.hg_ref), custom_call_target="tpu_custom_call" | custom-call | flops 3600000000 | bytes 8000000 | tf_op jit(solution)/shard_map/pallas_call | solution.py:460
  71.2 5.9 %shard_map.148 = (bf16[4,208,1152]{2,1,0:T(8,128)(2,1)S(1)}, bf16[16,24,640]{2,1,0:T(8,128)(2,1)S(1)}, bf16[16,24,640]{2,1,0:T(8,128)(2,1)S(1)}) custom-call(bf16[8,208,1152]{2,1,0:T(8,128)(2,1)S(1)} %get-tuple-element.43.qkv_ref, bf16[8,3,208,512]{3,2,1,0:T(8,128)(2,1)S(1)} %get-tuple-element.44.probs_ref, ...), custom_call_target="tpu_custom_call" | custom-call | flops 3500000000 | bytes 8000000 | tf_op jit(solution)/shard_map/pallas_call | solution.py:460
  77.9 1.1 collective-permute-done.18
  79.2 1.6 %collective-permute-start.19 = (bf16[8,24,640]{2,1,0:T(8,128)(2,1)S(1)}, bf16[8,24,640]{2,1,0:T(8,128)(2,1)S(1)}, u32[]{:S(2)}, u32[]{:S(2)}) collective-permute-start(bf16[8,24,640]{2,1,0:T(8,128)(2,1)S(1)} %slice.73), channel_id=1, source_target_pairs={{0,1},{1,0},{2,3},{3,2},{4,5},{5,4},{6,7},{7,6},{8,9},{9,8},{10,11... | collective-permute-start | bytes 737288 | tf_op jit(solution)/shard_map/ppermute | solution.py:44
  81.9 5.4 %collective-permute-done.19 = bf16[8,24,640]{2,1,0:T(8,128)(2,1)S(1)} collective-permute-done((bf16[8,24,640]{2,1,0:T(8,128)(2,1)S(1)}, bf16[8,24,640]{2,1,0:T(8,128)(2,1)S(1)}, u32[]{:S(2)}, u32[]{:S(2)}) %collective-permute-start.19) | collective-permute-done | bytes 245792 | tf_op jit(solution)/shard_map/ppermute | solution.py:44
  87.4 1.0 collective-permute-start.20
  88.7 1.6 %collective-permute-start.24 = (bf16[8,24,1024]{2,1,0:T(8,128)(2,1)S(1)}, bf16[8,24,1024]{2,1,0:T(8,128)(2,1)S(1)}, u32[]{:S(2)}, u32[]{:S(2)}) collective-permute-start(bf16[8,24,1024]{2,1,0:T(8,128)(2,1)S(1)} %slice.80), channel_id=1, source_target_pairs={{0,1},{1,0},{2,3},{3,2},{4,5},{5,4},{6,7},{7,6},{8,9},{9,8},{10,11... | collective-permute-start | bytes 1179656 | tf_op jit(solution)/shard_map/ppermute | solution.py:44
  90.3 2.2 %collective-permute-done.20 = bf16[4,24,640]{2,1,0:T(8,128)(2,1)S(1)} collective-permute-done((bf16[4,24,640]{2,1,0:T(8,128)(2,1)S(1)}, bf16[4,24,640]{2,1,0:T(8,128)(2,1)S(1)}, u32[]{:S(2)}, u32[]{:S(2)}) %collective-permute-start.20) | collective-permute-done | bytes 122912 | tf_op jit(solution)/shard_map/ppermute | solution.py:44
  93.5 1.4 %collective-permute-start.28 = (bf16[4,24,768]{2,1,0:T(8,128)(2,1)S(1)}, bf16[4,24,768]{2,1,0:T(8,128)(2,1)S(1)}, u32[]{:S(2)}, u32[]{:S(2)}) collective-permute-start(bf16[4,24,768]{2,1,0:T(8,128)(2,1)S(1)} %slice.86), channel_id=1, source_target_pairs={{0,1},{1,0},{2,3},{3,2},{4,5},{5,4},{6,7},{7,6},{8,9},{9,8},{10,11... | collective-permute-start | bytes 442376 | tf_op jit(solution)/shard_map/ppermute | solution.py:44
  94.9 5.6 %collective-permute-done.24 = bf16[8,24,1024]{2,1,0:T(8,128)(2,1)S(1)} collective-permute-done((bf16[8,24,1024]{2,1,0:T(8,128)(2,1)S(1)}, bf16[8,24,1024]{2,1,0:T(8,128)(2,1)S(1)}, u32[]{:S(2)}, u32[]{:S(2)}) %collective-permute-start.24) | collective-permute-done | bytes 393248 | tf_op jit(solution)/shard_map/ppermute | solution.py:44
  100.6 1.2 collective-permute-start.25
  102.1 4.3 %collective-permute-done.25 = bf16[4,24,1024]{2,1,0:T(8,128)(2,1)S(1)} collective-permute-done((bf16[4,24,1024]{2,1,0:T(8,128)(2,1)S(1)}, bf16[4,24,1024]{2,1,0:T(8,128)(2,1)S(1)}, u32[]{:S(2)}, u32[]{:S(2)}) %collective-permute-start.25) | collective-permute-done | bytes 196640 | tf_op jit(solution)/shard_map/ppermute | solution.py:44
  106.4 1.4 %collective-permute-start.29 = (bf16[2,24,1792]{2,1,0:T(8,128)(2,1)S(1)}, bf16[2,24,1792]{2,1,0:T(8,128)(2,1)S(1)}, u32[]{:S(2)}, u32[]{:S(2)}) collective-permute-start(bf16[2,24,1792]{2,1,0:T(8,128)(2,1)S(1)} %pad_maximum_fusion.1), channel_id=1, source_target_pairs={{0,8},{2,10},{4,12},{6,14},{8,0},{10,2},{12,4},{14,6},{16,24},{18,... | collective-permute-start | bytes 516104 | tf_op jit(solution)/shard_map/ppermute | solution.py:44
  107.9 3.4 %collective-permute-start.22 = (bf16[1,24,640]{2,1,0:T(8,128)(2,1)S(1)}, bf16[1,24,640]{2,1,0:T(8,128)(2,1)S(1)}, u32[]{:S(2)}, u32[]{:S(2)}) collective-permute-start(bf16[1,24,640]{2,1,0:T(8,128)(2,1)S(1)} %slice.78), channel_id=1, source_target_pairs={{0,16},{2,18},{4,20},{6,22},{8,24},{10,26},{12,28},{14,30},{16,0},... | collective-permute-start | bytes 92168 | tf_op jit(solution)/shard_map/ppermute | solution.py:44
  111.3 1.5 %collective-permute-done.29 = bf16[2,24,1792]{2,1,0:T(8,128)(2,1)S(1)} collective-permute-done((bf16[2,24,1792]{2,1,0:T(8,128)(2,1)S(1)}, bf16[2,24,1792]{2,1,0:T(8,128)(2,1)S(1)}, u32[]{:S(2)}, u32[]{:S(2)}) %collective-permute-start.29) | collective-permute-done | bytes 172064 | tf_op jit(solution)/shard_map/ppermute | solution.py:44
  112.9 2.6 %collective-permute-start.30 = (bf16[1,24,1792]{2,1,0:T(8,128)(2,1)S(1)}, bf16[1,24,1792]{2,1,0:T(8,128)(2,1)S(1)}, u32[]{:S(2)}, u32[]{:S(2)}) collective-permute-start(bf16[1,24,1792]{2,1,0:T(8,128)(2,1)S(1)} %slice.89), channel_id=1, source_target_pairs={{0,16},{2,18},{4,20},{6,22},{8,24},{10,26},{12,28},{14,30},{16,0},... | collective-permute-start | bytes 258056 | tf_op jit(solution)/shard_map/ppermute | solution.py:44
  115.5 5.7 %shard_map.149 = f32[1576,384]{1,0:T(8,128)} custom-call(bf16[4,208,1152]{2,1,0:T(8,128)(2,1)S(1)} %shard_map.147.refs_0_, bf16[4,208,1152]{2,1,0:T(8,128)(2,1)S(1)} %get-tuple-element.48.refs_1_, bf16[384,1152]{1,0:T(8,128)(2,1)S(1)} %get-tuple-element.47.w_ref.refs_2_, bf16[8,208,384]{2,1,0:T(8,128)(2,1)S(1)} %get-tuple-element.37.x_ref.refs_3_, ...), custom_call_target="tpu_custom_call" | custom-call | flops 2000000000 | bytes 10000000 | tf_op jit(solution)/shard_map/pallas_call | solution.py:460
  (85 shorter events, 10.9 us)
Async XLA Ops:
  1.6 7.0 %collective-permute-start.12 = (bf16[1,24,640]{2,1,0:T(8,128)(2,1)S(1)}, bf16[1,24,640]{2,1,0:T(8,128)(2,1)S(1)}, u32[]{:S(2)}, u32[]{:S(2)}) collective-permute-start(bf16[1,24,640]{2,1,0:T(8,128)(2,1)S(1)} %get-tuple-element.39), channel_id=1, source_target_pairs={{0,16},{2,18},{4,20},{6,22},{8,24},{10,26},{12,28},{14,30},{16,0},... | collective-permute-start | bytes 92168 | tf_op jit(solution)/shard_map/ppermute | solution.py:44
  5.7 5.6 %collective-permute-start.6 = (bf16[1,24,768]{2,1,0:T(8,128)(2,1)S(1)}, bf16[1,24,768]{2,1,0:T(8,128)(2,1)S(1)}, u32[]{:S(2)}, u32[]{:S(2)}) collective-permute-start(bf16[1,24,768]{2,1,0:T(8,128)(2,1)S(1)} %get-tuple-element.36), channel_id=1, source_target_pairs={{0,16},{2,18},{4,20},{6,22},{8,24},{10,26},{12,28},{14,30},{16,0},... | collective-permute-start | bytes 110600 | tf_op jit(solution)/shard_map/ppermute | solution.py:44
  5.8 6.9 %collective-permute-start = (bf16[1,24,1024]{2,1,0:T(8,128)(2,1)S(1)}, bf16[1,24,1024]{2,1,0:T(8,128)(2,1)S(1)}, u32[]{:S(2)}, u32[]{:S(2)}) collective-permute-start(bf16[1,24,1024]{2,1,0:T(8,128)(2,1)S(1)} %get-tuple-element.35), channel_id=1, source_target_pairs={{0,16},{2,18},{4,20},{6,22},{8,24},{10,26},{12,28},{14,30},{16,0},... | collective-permute-start | bytes 147464 | tf_op jit(solution)/shard_map/ppermute | solution.py:44
  8.7 5.2 %collective-permute-start.13 = (bf16[2,24,640]{2,1,0:T(8,128)(2,1)S(1)}, bf16[2,24,640]{2,1,0:T(8,128)(2,1)S(1)}, u32[]{:S(2)}, u32[]{:S(2)}) collective-permute-start(bf16[2,24,640]{2,1,0:T(8,128)(2,1)S(1)} %pad_maximum_fusion.6), channel_id=1, source_target_pairs={{0,8},{2,10},{4,12},{6,14},{8,0},{10,2},{12,4},{14,6},{16,24},{18,... | collective-permute-start | bytes 184328 | tf_op jit(solution)/shard_map/ppermute | solution.py:44
  11.3 4.4 %collective-permute-start.7 = (bf16[2,24,768]{2,1,0:T(8,128)(2,1)S(1)}, bf16[2,24,768]{2,1,0:T(8,128)(2,1)S(1)}, u32[]{:S(2)}, u32[]{:S(2)}) collective-permute-start(bf16[2,24,768]{2,1,0:T(8,128)(2,1)S(1)} %pad_maximum_fusion.5), channel_id=1, source_target_pairs={{0,8},{2,10},{4,12},{6,14},{8,0},{10,2},{12,4},{14,6},{16,24},{18,... | collective-permute-start | bytes 221192 | tf_op jit(solution)/shard_map/ppermute | solution.py:44
  12.2 18.1 %copy-start.3 = (bf16[1576,384]{1,0:T(8,128)(2,1)S(1)}, bf16[1576,384]{1,0:T(8,128)(2,1)}, u32[]{:S(2)}) copy-start(bf16[1576,384]{1,0:T(8,128)(2,1)} %out_grad.1) | copy-start | bytes 3631108
  12.7 4.7 %collective-permute-start.1 = (bf16[2,24,1024]{2,1,0:T(8,128)(2,1)S(1)}, bf16[2,24,1024]{2,1,0:T(8,128)(2,1)S(1)}, u32[]{:S(2)}, u32[]{:S(2)}) collective-permute-start(bf16[2,24,1024]{2,1,0:T(8,128)(2,1)S(1)} %pad_maximum_fusion.4), channel_id=1, source_target_pairs={{0,8},{2,10},{4,12},{6,14},{8,0},{10,2},{12,4},{14,6},{16,24},{18,... | collective-permute-start | bytes 294920 | tf_op jit(solution)/shard_map/ppermute | solution.py:44
  13.9 5.4 %collective-permute-start.14 = (bf16[4,24,640]{2,1,0:T(8,128)(2,1)S(1)}, bf16[4,24,640]{2,1,0:T(8,128)(2,1)S(1)}, u32[]{:S(2)}, u32[]{:S(2)}) collective-permute-start(bf16[4,24,640]{2,1,0:T(8,128)(2,1)S(1)} %pad_maximum_fusion.3), channel_id=1, source_target_pairs={{0,4},{2,6},{4,0},{6,2},{8,12},{10,14},{12,8},{14,10},{16,20},{18,... | collective-permute-start | bytes 368648 | tf_op jit(solution)/shard_map/ppermute | solution.py:44
  15.7 11.1 %collective-permute-start.8 = (bf16[4,24,768]{2,1,0:T(8,128)(2,1)S(1)}, bf16[4,24,768]{2,1,0:T(8,128)(2,1)S(1)}, u32[]{:S(2)}, u32[]{:S(2)}) collective-permute-start(bf16[4,24,768]{2,1,0:T(8,128)(2,1)S(1)} %pad_maximum_fusion.2), channel_id=1, source_target_pairs={{0,4},{2,6},{4,0},{6,2},{8,12},{10,14},{12,8},{14,10},{16,20},{18,... | collective-permute-start | bytes 442376 | tf_op jit(solution)/shard_map/ppermute | solution.py:44
  17.4 7.8 %collective-permute-start.2 = (bf16[4,24,1024]{2,1,0:T(8,128)(2,1)S(1)}, bf16[4,24,1024]{2,1,0:T(8,128)(2,1)S(1)}, u32[]{:S(2)}, u32[]{:S(2)}) collective-permute-start(bf16[4,24,1024]{2,1,0:T(8,128)(2,1)S(1)} %pad_maximum_fusion), channel_id=1, source_target_pairs={{0,1},{1,0},{2,3},{3,2},{4,5},{5,4},{6,7},{7,6},{8,9},{9,8},{10,11... | collective-permute-start | bytes 589832 | tf_op jit(solution)/shard_map/ppermute | solution.py:44
  19.3 11.0 %collective-permute-start.15 = (bf16[8,24,640]{2,1,0:T(8,128)(2,1)S(1)}, bf16[8,24,640]{2,1,0:T(8,128)(2,1)S(1)}, u32[]{:S(2)}, u32[]{:S(2)}) collective-permute-start(bf16[8,24,640]{2,1,0:T(8,128)(2,1)S(1)} %constant_dynamic-update-slice_fusion.8.p0), channel_id=1, source_target_pairs={{0,1},{1,0},{2,3},{3,2},{4,5},{5,4},{6,7},{7,6},{8,9},{9,8},{10,11... | collective-permute-start | bytes 737288 | tf_op jit(solution)/shard_map/ppermute | solution.py:44
  25.3 8.4 %collective-permute-start.3 = (bf16[8,24,1024]{2,1,0:T(8,128)(2,1)S(1)}, bf16[8,24,1024]{2,1,0:T(8,128)(2,1)S(1)}, u32[]{:S(2)}, u32[]{:S(2)}) collective-permute-start(bf16[8,24,1024]{2,1,0:T(8,128)(2,1)S(1)} %constant_dynamic-update-slice_fusion.p0), channel_id=1, source_target_pairs={{0,4},{2,6},{4,0},{6,2},{8,12},{10,14},{12,8},{14,10},{16,20},{18,... | collective-permute-start | bytes 1179656 | tf_op jit(solution)/shard_map/ppermute | solution.py:44
  26.9 6.8 %collective-permute-start.9 = (bf16[8,24,768]{2,1,0:T(8,128)(2,1)S(1)}, bf16[8,24,768]{2,1,0:T(8,128)(2,1)S(1)}, u32[]{:S(2)}, u32[]{:S(2)}) collective-permute-start(bf16[8,24,768]{2,1,0:T(8,128)(2,1)S(1)} %constant_dynamic-update-slice_fusion.4.r0), channel_id=1, source_target_pairs={{0,1},{1,0},{2,3},{3,2},{4,5},{5,4},{6,7},{7,6},{8,9},{9,8},{10,11... | collective-permute-start | bytes 884744 | tf_op jit(solution)/shard_map/ppermute | solution.py:44
  28.5 3.0 %collective-permute-start.16 = (bf16[8,24,640]{2,1,0:T(8,128)(2,1)S(1)}, bf16[8,24,640]{2,1,0:T(8,128)(2,1)S(1)}, u32[]{:S(2)}, u32[]{:S(2)}) collective-permute-start(bf16[8,24,640]{2,1,0:T(8,128)(2,1)S(1)} %constant_dynamic-update-slice_fusion.8.p0), channel_id=1, source_target_pairs={{0,2},{2,0},{4,6},{6,4},{8,10},{10,8},{12,14},{14,12},{16,18},{18,... | collective-permute-start | bytes 737288 | tf_op jit(solution)/shard_map/ppermute | solution.py:44
  30.4 3.8 %collective-permute-start.17 = (bf16[8,24,640]{2,1,0:T(8,128)(2,1)S(1)}, bf16[8,24,640]{2,1,0:T(8,128)(2,1)S(1)}, u32[]{:S(2)}, u32[]{:S(2)}) collective-permute-start(bf16[8,24,640]{2,1,0:T(8,128)(2,1)S(1)} %collective-permute-done.15.p1), channel_id=1, source_target_pairs={{0,2},{2,0},{4,6},{6,4},{8,10},{10,8},{12,14},{14,12},{16,18},{18,... | collective-permute-start | bytes 737288 | tf_op jit(solution)/shard_map/ppermute | solution.py:44
  30.9 12.9 %collective-permute-start.10 = (bf16[8,24,768]{2,1,0:T(8,128)(2,1)S(1)}, bf16[8,24,768]{2,1,0:T(8,128)(2,1)S(1)}, u32[]{:S(2)}, u32[]{:S(2)}) collective-permute-start(bf16[8,24,768]{2,1,0:T(8,128)(2,1)S(1)} %constant_dynamic-update-slice_fusion.4.r0), channel_id=1, source_target_pairs={{0,2},{2,0},{4,6},{6,4},{8,10},{10,8},{12,14},{14,12},{16,18},{18,... | collective-permute-start | bytes 884744 | tf_op jit(solution)/shard_map/ppermute | solution.py:44
  31.5 12.3 %collective-permute-start.4 = (bf16[8,24,1024]{2,1,0:T(8,128)(2,1)S(1)}, bf16[8,24,1024]{2,1,0:T(8,128)(2,1)S(1)}, u32[]{:S(2)}, u32[]{:S(2)}) collective-permute-start(bf16[8,24,1024]{2,1,0:T(8,128)(2,1)S(1)} %constant_dynamic-update-slice_fusion.p0), channel_id=1, source_target_pairs={{0,2},{2,0},{4,6},{6,4},{8,10},{10,8},{12,14},{14,12},{16,18},{18,... | collective-permute-start | bytes 1179656 | tf_op jit(solution)/shard_map/ppermute | solution.py:44
  33.7 10.2 %collective-permute-start.11 = (bf16[8,24,768]{2,1,0:T(8,128)(2,1)S(1)}, bf16[8,24,768]{2,1,0:T(8,128)(2,1)S(1)}, u32[]{:S(2)}, u32[]{:S(2)}) collective-permute-start(bf16[8,24,768]{2,1,0:T(8,128)(2,1)S(1)} %collective-permute-done.9.r1), channel_id=1, source_target_pairs={{0,2},{2,0},{4,6},{6,4},{8,10},{10,8},{12,14},{14,12},{16,18},{18,... | collective-permute-start | bytes 884744 | tf_op jit(solution)/shard_map/ppermute | solution.py:44
  33.7 10.2 %collective-permute-start.5 = (bf16[8,24,1024]{2,1,0:T(8,128)(2,1)S(1)}, bf16[8,24,1024]{2,1,0:T(8,128)(2,1)S(1)}, u32[]{:S(2)}, u32[]{:S(2)}) collective-permute-start(bf16[8,24,1024]{2,1,0:T(8,128)(2,1)S(1)} %collective-permute-done.3.p1), channel_id=1, source_target_pairs={{0,2},{2,0},{4,6},{6,4},{8,10},{10,8},{12,14},{14,12},{16,18},{18,... | collective-permute-start | bytes 1179656 | tf_op jit(solution)/shard_map/ppermute | solution.py:44
  77.1 1.9 %collective-permute-start.18 = (bf16[16,24,640]{2,1,0:T(8,128)(2,1)S(1)}, bf16[16,24,640]{2,1,0:T(8,128)(2,1)S(1)}, u32[]{:S(2)}, u32[]{:S(2)}) collective-permute-start(bf16[16,24,640]{2,1,0:T(8,128)(2,1)S(1)} %get-tuple-element.51), channel_id=1, source_target_pairs={{0,2},{2,0},{4,6},{6,4},{8,10},{10,8},{12,14},{14,12},{16,18},{18,... | collective-permute-start | bytes 1474568 | tf_op jit(solution)/shard_map/ppermute | solution.py:44
  77.4 3.4 %collective-permute-start.26 = (bf16[16,24,768]{2,1,0:T(8,128)(2,1)S(1)}, bf16[16,24,768]{2,1,0:T(8,128)(2,1)S(1)}, u32[]{:S(2)}, u32[]{:S(2)}) collective-permute-start(bf16[16,24,768]{2,1,0:T(8,128)(2,1)S(1)} %get-tuple-element.55), channel_id=1, source_target_pairs={{0,2},{2,0},{4,6},{6,4},{8,10},{10,8},{12,14},{14,12},{16,18},{18,... | collective-permute-start | bytes 1769480 | tf_op jit(solution)/shard_map/ppermute | solution.py:44
  77.7 10.7 %collective-permute-start.23 = (bf16[16,24,1024]{2,1,0:T(8,128)(2,1)S(1)}, bf16[16,24,1024]{2,1,0:T(8,128)(2,1)S(1)}, u32[]{:S(2)}, u32[]{:S(2)}) collective-permute-start(bf16[16,24,1024]{2,1,0:T(8,128)(2,1)S(1)} %get-tuple-element.53), channel_id=1, source_target_pairs={{0,2},{2,0},{4,6},{6,4},{8,10},{10,8},{12,14},{14,12},{16,18},{18,... | collective-permute-start | bytes 2359304 | tf_op jit(solution)/shard_map/ppermute | solution.py:44
  79.2 8.1 %collective-permute-start.19 = (bf16[8,24,640]{2,1,0:T(8,128)(2,1)S(1)}, bf16[8,24,640]{2,1,0:T(8,128)(2,1)S(1)}, u32[]{:S(2)}, u32[]{:S(2)}) collective-permute-start(bf16[8,24,640]{2,1,0:T(8,128)(2,1)S(1)} %slice.73), channel_id=1, source_target_pairs={{0,1},{1,0},{2,3},{3,2},{4,5},{5,4},{6,7},{7,6},{8,9},{9,8},{10,11... | collective-permute-start | bytes 737288 | tf_op jit(solution)/shard_map/ppermute | solution.py:44
  81.0 12.4 %collective-permute-start.27 = (bf16[8,24,768]{2,1,0:T(8,128)(2,1)S(1)}, bf16[8,24,768]{2,1,0:T(8,128)(2,1)S(1)}, u32[]{:S(2)}, u32[]{:S(2)}) collective-permute-start(bf16[8,24,768]{2,1,0:T(8,128)(2,1)S(1)} %slice.84), channel_id=1, source_target_pairs={{0,4},{2,6},{4,0},{6,2},{8,12},{10,14},{12,8},{14,10},{16,20},{18,... | collective-permute-start | bytes 884744 | tf_op jit(solution)/shard_map/ppermute | solution.py:44
  87.4 5.1 %collective-permute-start.20 = (bf16[4,24,640]{2,1,0:T(8,128)(2,1)S(1)}, bf16[4,24,640]{2,1,0:T(8,128)(2,1)S(1)}, u32[]{:S(2)}, u32[]{:S(2)}) collective-permute-start(bf16[4,24,640]{2,1,0:T(8,128)(2,1)S(1)} %slice.75), channel_id=1, source_target_pairs={{0,4},{2,6},{4,0},{6,2},{8,12},{10,14},{12,8},{14,10},{16,20},{18,... | collective-permute-start | bytes 368648 | tf_op jit(solution)/shard_map/ppermute | solution.py:44
  88.7 11.7 %collective-permute-start.24 = (bf16[8,24,1024]{2,1,0:T(8,128)(2,1)S(1)}, bf16[8,24,1024]{2,1,0:T(8,128)(2,1)S(1)}, u32[]{:S(2)}, u32[]{:S(2)}) collective-permute-start(bf16[8,24,1024]{2,1,0:T(8,128)(2,1)S(1)} %slice.80), channel_id=1, source_target_pairs={{0,1},{1,0},{2,3},{3,2},{4,5},{5,4},{6,7},{7,6},{8,9},{9,8},{10,11... | collective-permute-start | bytes 1179656 | tf_op jit(solution)/shard_map/ppermute | solution.py:44
  92.5 15.3 %collective-permute-start.21 = (bf16[2,24,640]{2,1,0:T(8,128)(2,1)S(1)}, bf16[2,24,640]{2,1,0:T(8,128)(2,1)S(1)}, u32[]{:S(2)}, u32[]{:S(2)}) collective-permute-start(bf16[2,24,640]{2,1,0:T(8,128)(2,1)S(1)} %slice.77), channel_id=1, source_target_pairs={{0,8},{2,10},{4,12},{6,14},{8,0},{10,2},{12,4},{14,6},{16,24},{18,... | collective-permute-start | bytes 184328 | tf_op jit(solution)/shard_map/ppermute | solution.py:44
  93.5 8.6 %collective-permute-start.28 = (bf16[4,24,768]{2,1,0:T(8,128)(2,1)S(1)}, bf16[4,24,768]{2,1,0:T(8,128)(2,1)S(1)}, u32[]{:S(2)}, u32[]{:S(2)}) collective-permute-start(bf16[4,24,768]{2,1,0:T(8,128)(2,1)S(1)} %slice.86), channel_id=1, source_target_pairs={{0,1},{1,0},{2,3},{3,2},{4,5},{5,4},{6,7},{7,6},{8,9},{9,8},{10,11... | collective-permute-start | bytes 442376 | tf_op jit(solution)/shard_map/ppermute | solution.py:44
  100.6 5.7 %collective-permute-start.25 = (bf16[4,24,1024]{2,1,0:T(8,128)(2,1)S(1)}, bf16[4,24,1024]{2,1,0:T(8,128)(2,1)S(1)}, u32[]{:S(2)}, u32[]{:S(2)}) collective-permute-start(bf16[4,24,1024]{2,1,0:T(8,128)(2,1)S(1)} %slice.82), channel_id=1, source_target_pairs={{0,4},{2,6},{4,0},{6,2},{8,12},{10,14},{12,8},{14,10},{16,20},{18,... | collective-permute-start | bytes 589832 | tf_op jit(solution)/shard_map/ppermute | solution.py:44
  106.4 6.4 %collective-permute-start.29 = (bf16[2,24,1792]{2,1,0:T(8,128)(2,1)S(1)}, bf16[2,24,1792]{2,1,0:T(8,128)(2,1)S(1)}, u32[]{:S(2)}, u32[]{:S(2)}) collective-permute-start(bf16[2,24,1792]{2,1,0:T(8,128)(2,1)S(1)} %pad_maximum_fusion.1), channel_id=1, source_target_pairs={{0,8},{2,10},{4,12},{6,14},{8,0},{10,2},{12,4},{14,6},{16,24},{18,... | collective-permute-start | bytes 516104 | tf_op jit(solution)/shard_map/ppermute | solution.py:44
  107.9 13.4 %collective-permute-start.22 = (bf16[1,24,640]{2,1,0:T(8,128)(2,1)S(1)}, bf16[1,24,640]{2,1,0:T(8,128)(2,1)S(1)}, u32[]{:S(2)}, u32[]{:S(2)}) collective-permute-start(bf16[1,24,640]{2,1,0:T(8,128)(2,1)S(1)} %slice.78), channel_id=1, source_target_pairs={{0,16},{2,18},{4,20},{6,22},{8,24},{10,26},{12,28},{14,30},{16,0},... | collective-permute-start | bytes 92168 | tf_op jit(solution)/shard_map/ppermute | solution.py:44
  112.9 8.3 %collective-permute-start.30 = (bf16[1,24,1792]{2,1,0:T(8,128)(2,1)S(1)}, bf16[1,24,1792]{2,1,0:T(8,128)(2,1)S(1)}, u32[]{:S(2)}, u32[]{:S(2)}) collective-permute-start(bf16[1,24,1792]{2,1,0:T(8,128)(2,1)S(1)} %slice.89), channel_id=1, source_target_pairs={{0,16},{2,18},{4,20},{6,22},{8,24},{10,26},{12,28},{14,30},{16,0},... | collective-permute-start | bytes 258056 | tf_op jit(solution)/shard_map/ppermute | solution.py:44
  (3 other events, 29.6 us)
